TPU v7x, 256 devices: a whole 4x4x8 slice. The times are simulated.
256 devices in a mesh: tm: 64 (over y, z, core), col: 4 (over x).
Axes of the slice: x: 4, y: 4, z: 8, core: 2. Of those that a mesh axis runs over, the one named last changes fastest.
Arguments:
- transition: bfloat16 [512, 256, 256], P('tm', 'col'), may hold values from -1 to 1, as said below
- drive: float32 [512, 16, 256], P('tm', 'col'), may hold values from -0.3125 to 0.3125
- smoother_gain: bfloat16 [512, 256, 256], P('tm', 'col'), may hold values from -1 to 1, as said below
- dynamics: float32 [256, 256], replicated, may hold values from -0.375 to 0.375
- initial_mean: float32 [16, 256], P('col'), may hold values from -6 to 6
Outputs:
- filtered_mean: float32 [512, 16, 256], P('tm', 'col')
- smoothed_mean: float32 [512, 16, 256], P('tm', 'col')
Inputs may be any that keep to these rules, and one draw needn't show every extreme that they name: `transition`: every step operator is a per-channel diagonal plus a dense full-rank part. `smoother_gain`: every gain is a per-channel diagonal plus a dense full-rank part.
All inputs are finite; a program needn't handle non-finite values.
Results may differ from a plain program's by a relative error of at most 0.0018.
Values may be sent and summed in bfloat16 or wider, within the bound.
No kernel may reach another device: no remote copies, remote signals or barrier semaphores. Data moves between devices by JAX's collectives and lax.ppermute only.
A program may use at most 128 MiB of HBM per device.

v0:
```python
import jax
import jax.numpy as jnp
from jax import lax
from jax.experimental import pallas as pl
from jax.experimental.pallas import tpu as pltpu
from jax.sharding import PartitionSpec as P


SUF_X, SUF_Y, SUF_Q = (0, 0), (1, 0), (2, 0)
PRE_X = (1, 1)
D = 256
SER = 16
GRP = 8
ALL = D + SER
f32, bf16 = jnp.float32, jnp.bfloat16


def split(x):
    hi = x.astype(bf16)
    return hi, (x - hi.astype(f32)).astype(bf16)


def dot(a, b):
    return jnp.dot(a, b, preferred_element_type=f32)


def mul_exact(x, b):
    hi, lo = split(x)
    return dot(hi, b) + dot(lo, b)


def mul(x, b):
    hi, lo = split(x)
    bhi, blo = split(b)
    return dot(hi, bhi) + (dot(lo, bhi) + dot(hi, blo))


def place():
    tm = lax.axis_index("tm")
    return tm, lax.rem(tm, 2), lax.axis_index("col")


def roles(core, col):
    return col == 0, jnp.logical_and(col == 1, core == 0), jnp.logical_and(col == 1, core == 1)


def aligned(index, unit):
    return pl.multiple_of(index * unit, unit)


def assemble(dst, pieces, col):
    rows = pieces[0].shape[1]
    for lag, piece in zip((0, 3, 1, 2), pieces):
        dst[:, pl.ds(aligned(lax.rem(col + lag, 4), rows), rows), :] = piece[...]


def stage_kernel(a, g, dyn, a_out, g_out, dyn_out):
    a_out[...] = a[...]
    g_out[...] = g[...]
    dyn_out[...] = dyn[...]


def forward_kernel(a0, a1, a2, a3, d0, d1, d2, d3, dyn, araw, drive, xs, proj, x_out):
    tm, _, col = place()
    steps = a0.shape[0]
    assemble(araw, (a0, a1, a2, a3), col)
    per = d0.shape[1]
    for c in range(4):

        @pl.when(col == c)
        def _(c=c):
            for lag, piece in zip((0, 3, 1, 2), (d0, d1, d2, d3)):
                first = (c + lag) % 4 * per
                drive[:, first : first + per, :] = piece[...]

    start = jnp.where(tm == 0, 1.0, 0.0).astype(f32)
    dhi, dlo = split(dyn[...])
    for t in range(steps):
        if t == 0:
            xs[0, :D, :] = araw[0].astype(f32)
            xs[0, D:, :] = mul_exact(drive[steps] * start, araw[0]) + drive[0]
        else:
            new = mul_exact(xs[t - 1], araw[t])
            xs[t, :D, :] = new[:D]
            xs[t, D:, :] = new[D:] + drive[t]
        hi, lo = split(xs[t])
        proj[t] = dot(hi, dhi) + (dot(lo, dhi) + dot(hi, dlo))
    x_out[...] = xs[steps - 1]


def backward_kernel(g0, g1, g2, g3, xs, proj, graw, qy_out):
    tm, _, col = place()
    steps = g0.shape[0]
    assemble(graw, (g0, g1, g2, g3), col)

    @pl.when(tm == lax.axis_size("tm") - 1)
    def _():
        graw[steps - 1] = jnp.zeros((D, D), bf16)

    g = graw[steps - 1]
    q = g.astype(f32)
    s = mul_exact(-proj[steps - 1], g) + xs[steps - 1]
    for t in range(steps - 2, -1, -1):
        g = graw[t]
        q = mul_exact(q, g)
        s = mul_exact(s - proj[t], g) + xs[t]
    qy_out[:D, :] = q
    qy_out[D:, :] = s


def chip_kernel(x, x_m, qy, qy_m, own, xrow, qrow):
    _, core, col = place()
    suf_x, suf_y, pre_x = roles(core, col)

    def work(x0_ref, e0, x1, e1):
        x0, q0 = x0_ref[...], e0[:D, :]
        new = mul(x0, x1[:D, :])
        xrow[:D, :] = new[:D]
        xrow[D:, :] = new[D:] + x1[D:, :]
        qrow[:D, :] = mul(e1[:D, :], q0)
        qrow[D:, :] = jnp.zeros((SER, D), f32)
        mid = mul(x0, e1[D : 2 * D, :])
        mid = jnp.concatenate([mid[:D], mid[D:] + e1[2 * D :, :]], 0)
        new_y = e0[D:, :] + mul(mid, q0)
        rest = jnp.where(jnp.logical_or(suf_x, pre_x), xrow[...], qrow[...])
        own[...] = jnp.where(suf_y, new_y, rest)

    @pl.when(core == 0)
    def _():
        work(x, qy, x_m, qy_m)

    @pl.when(core == 1)
    def _():
        work(x_m, qy_m, x, qy)


def round_kernel(dist, own, got, xrow, qrow, kept_a, kept_d, out, vec):
    tm, core, col = place()
    suf_x, suf_y, pre_x = roles(core, col)
    chip = lax.div(tm, 2)
    later = chip + dist < lax.axis_size("tm") // 2

    @pl.when(jnp.logical_not(jnp.logical_or(suf_x, suf_y)))
    def _():
        valid = jnp.where(pre_x, chip >= dist, later)
        new = mul(got[...], own[:D, :])
        out[:D, :] = jnp.where(valid, new[:D], own[:D, :])
        out[D:, :] = new[D:] + own[D:, :]

    @pl.when(suf_x)
    def _():
        new = mul(own[...], got[:D, :])
        out[:D, :] = jnp.where(later, new[:D], own[:D, :])
        out[D:, :] = jnp.where(later, new[D:] + got[D:, :], own[D:, :])

    @pl.when(suf_y)
    def _():
        mid = mul(xrow[...], got[:D, :])
        mid = jnp.concatenate([mid[:D], mid[D:] + got[D:, :]], 0)
        out[...] = own[...] + mul(mid, qrow[:D, :])

    vec[...] = out[D:, :]


def mean_kernel(own, got, out):
    out[...] = mul(got[...], own[:D, :]) + own[D:, :]


def near_kernel(own, xrow, begin, near, mid):
    x = begin[...]
    near[...] = mul(x, own[:D, :]) + own[D:, :]
    mid[...] = mul(x, xrow[:D, :]) + xrow[D:, :]


def top_kernel(near, mid, qrow, got, s_out):
    far = mul(mid[...], got[:D, :]) + got[D:, :]
    s_out[...] = near[...] + mul(far, qrow[:D, :])


def group(value, low):
    return jnp.where(low, value[:GRP], value[GRP:])


def mean_sweep_kernel(araw, drive, dyn, x_b, x_bm, x_r, x0, x2, x3, xs, proj, mid, filt):
    tm, core, col = place()
    steps = araw.shape[0]
    low = col < 2
    begin = group(jnp.where(col == 1, x_r[...], x0[...] + x2[...] + x3[...]), low)

    @pl.when(core == 0)
    def _():
        mid[...] = mul(begin, x_b[:D, :]) + group(x_b[D:, :], low)

    @pl.when(core == 1)
    def _():
        mid[...] = mul(begin, x_bm[:D, :]) + group(x_bm[D:, :], low)

    first = begin + jnp.where(tm == 0, 1.0, 0.0).astype(f32) * group(drive[steps], low)
    x = jnp.where(core == 0, first, mid[...])
    per = GRP // 2
    upper = lax.rem(col, 2) == 1
    for t in range(steps):
        x = mul_exact(x, araw[t]) + group(drive[t], low)
        xs[t] = x
        filt[t] = jnp.where(upper, x[per:], x[:per])
    proj[...] = mul(xs[...].reshape(steps * GRP, D), dyn[...]).reshape(steps, GRP, D)


def smooth_sweep_kernel(graw, xs, proj, mid, qy_m, s0, s1, s2, s3, smooth):
    _, core, col = place()
    steps = graw.shape[0]
    low = col < 2
    got = group(s0[...] + s1[...] + (s2[...] + s3[...]), low)
    inner = mul(got, qy_m[:D, :]) + (
        mul(mid[...], qy_m[D : 2 * D, :]) + group(qy_m[2 * D :, :], low)
    )
    s = jnp.where(core == 0, inner, got)
    per = GRP // 2
    upper = lax.rem(col, 2) == 1
    for t in range(steps - 1, -1, -1):
        s = mul_exact(s - proj[t], graw[t]) + xs[t]
        smooth[t] = jnp.where(upper, s[per:], s[:per])


VM = pl.BlockSpec(memory_space=pltpu.VMEM)


def call(kernel, outs, *args, grant=8):
    return pl.pallas_call(
        kernel,
        out_shape=tuple(jax.ShapeDtypeStruct(s, d) for s, d in outs),
        in_specs=[VM] * len(args),
        out_specs=tuple(VM for _ in outs),
        compiler_params=pltpu.CompilerParams(vmem_limit_bytes=grant << 20),
    )(*args)


def scan(transition, drive, smoother_gain, dynamics, initial_mean):
    tms, cols = lax.axis_size("tm"), lax.axis_size("col")
    steps = transition.shape[0]
    chips = tms // 2
    whole, vector = ((ALL, D), f32), ((SER, D), f32)

    def send(x, pairs):
        return lax.ppermute(
            x, ("tm", "col"), [(a * cols + b, c * cols + d) for (a, b), (c, d) in pairs]
        )

    def swap(x):
        return lax.ppermute(x, "tm", [(i, i ^ 1) for i in range(tms)])

    def turn(x, by):
        return lax.ppermute(x, "col", [(c, (c + by) % 4) for c in range(4)])

    def hop(x, moves, by=0):
        return send(
            x,
            [
                ((2 * k + h, c), (2 * (k + by) + g, d))
                for k in range(chips)
                for (c, h), (d, g) in moves
                if 0 <= k + by < chips
            ],
        )

    def shift(x, dist, lanes):
        pairs = []
        for c, h in lanes:
            by = dist if (c, h) == PRE_X else -dist
            for k in range(chips):
                if 0 <= k + by < chips:
                    pairs.append(((2 * k + h, c), (2 * (k + by) + h, c)))
        return send(x, pairs)

    def across(c):
        return [((1, h), (c, h)) for h in range(2)]

    extra = jnp.concatenate([drive, initial_mean[None]], 0)
    a_left, a_right = turn(transition, 1), turn(transition, -1)
    a_far = turn(a_left, 1)
    g_right, g_left = turn(smoother_gain, -1), turn(smoother_gain, 1)
    g_far = turn(g_right, -1)
    e_left, e_right, e_far = turn(extra, 1), turn(extra, -1), turn(extra, 2)

    quarter = (transition.shape, bf16)
    a_own, g_own, dyn = call(
        stage_kernel, [quarter, quarter, ((D, D), f32)], transition, smoother_gain, dynamics
    )
    araw, drive16, xs, proj, x_b = call(
        forward_kernel,
        [
            ((steps, D, D), bf16),
            ((steps + 1, SER, D), f32),
            ((steps, ALL, D), f32),
            ((steps, ALL, D), f32),
            whole,
        ],
        a_own, a_left, a_right, a_far,
        extra, e_left, e_right, e_far, dyn,
        grant=16,
    )
    x_bm = swap(x_b)
    graw, qy_b = call(
        backward_kernel,
        [((steps, D, D), bf16), ((ALL + D, D), f32)],
        g_own, g_left, g_right, g_far, xs, proj,
        grant=16,
    )
    qy_bm = swap(qy_b)
    own, xrow, qrow = call(chip_kernel, [whole] * 3, x_b, x_bm, qy_b, qy_bm)

    dist = 1
    while 2 * dist < chips:
        if dist > 1:
            xrow = hop(own, [(SUF_X, SUF_Y)])
            qrow = hop(own, [(SUF_Q, SUF_Y)])
        got = shift(own, dist, (SUF_X, SUF_Y, SUF_Q, PRE_X))
        own, vec = call(
            lambda *r, dist=dist: round_kernel(dist, *r),
            [whole, vector],
            own, got, xrow, qrow, araw, drive16,
        )
        dist *= 2

    got_v = shift(vec, dist, (PRE_X,))
    got = shift(own, dist, (SUF_Y,))
    xrow = hop(own, [(SUF_X, SUF_Y)])
    qrow = hop(own, [(SUF_Q, SUF_Y)])
    (leaving,) = call(mean_kernel, [vector], own, got_v)
    x_one = hop(leaving, [(PRE_X, PRE_X)], 1)
    first = lax.rem(lax.axis_index("tm"), 2) == 0
    x_two = jnp.where(first, hop(x_one, [(PRE_X, SUF_Y)]), x_one)
    means = [hop(x_two, across(c)) for c in (3, 0, 2)]
    near, mid = call(near_kernel, [vector, vector], own, xrow, x_two)
    (s_one,) = call(top_kernel, [vector], near, mid, qrow, got)
    s_two = jnp.where(first, s_one, hop(s_one, [(SUF_Y, PRE_X)]))
    s_in = [hop(s_two, across(c), -1) for c in (3, 0, 2, 1)]
    part = ((steps, GRP, D), f32)
    result = ((steps, drive.shape[1], D), f32)
    xs8, proj8, mid8, filtered = call(
        mean_sweep_kernel,
        [part, part, ((GRP, D), f32), result],
        araw, drive16, dyn, x_b, x_bm, x_two, *means,
    )
    (smoothed,) = call(smooth_sweep_kernel, [result], graw, xs8, proj8, mid8, qy_bm, *s_in)
    return filtered, smoothed


def solution(mesh):
    placed = (P("tm", "col", None), P("tm", "col", None), P("tm", "col", None), P(), P("col", None))
    return jax.shard_map(
        scan,
        mesh=mesh,
        in_specs=placed,
        out_specs=(P("tm", "col", None), P("tm", "col", None)),
        check_vma=False,
    )
```

profile of v0, /device:TPU:18, one launch (start us, length us, event | category | flops | bytes accessed | tf_op | source)
XLA Modules:
  0.0 131.7 jit_solution(13260739143617893178)
XLA Ops:
  0.6 1.6 %collective-permute-start = (bf16[8,64,256]{2,1,0:T(8,128)(2,1)}, bf16[8,64,256]{2,1,0:T(8,128)(2,1)S(1)}, u32[]{:S(2)}, u32[]{:S(2)}) collective-permute-start(bf16[8,64,256]{2,1,0:T(8,128)(2,1)} %a.1), channel_id=1, source_target_pairs={{0,1},{1,2},{2,3},{3,0},{4,5},{5,6},{6,7},{7,4},{8,9},{9,10},{10,1... | collective-permute-start | bytes 786440 | tf_op jit(solution)/shard_map/ppermute | solution.py:253
  2.2 0.5 collective-permute-start.8
  2.7 1.7 %collective-permute-start.1 = (bf16[8,64,256]{2,1,0:T(8,128)(2,1)}, bf16[8,64,256]{2,1,0:T(8,128)(2,1)S(1)}, u32[]{:S(2)}, u32[]{:S(2)}) collective-permute-start(bf16[8,64,256]{2,1,0:T(8,128)(2,1)} %a.1), channel_id=1, source_target_pairs={{0,3},{1,0},{2,1},{3,2},{4,7},{5,4},{6,5},{7,6},{8,11},{9,8},{10,9... | collective-permute-start | bytes 786440 | tf_op jit(solution)/shard_map/ppermute | solution.py:253
  4.5 4.5 %collective-permute-done.a1 = bf16[8,64,256]{2,1,0:T(8,128)(2,1)S(1)} collective-permute-done((bf16[8,64,256]{2,1,0:T(8,128)(2,1)}, bf16[8,64,256]{2,1,0:T(8,128)(2,1)S(1)}, u32[]{:S(2)}, u32[]{:S(2)}) %collective-permute-start) | collective-permute-done | bytes 262176 | tf_op jit(solution)/shard_map/ppermute | solution.py:253
  9.0 1.5 %collective-permute-start.2 = (bf16[8,64,256]{2,1,0:T(8,128)(2,1)S(1)}, bf16[8,64,256]{2,1,0:T(8,128)(2,1)S(1)}, u32[]{:S(2)}, u32[]{:S(2)}) collective-permute-start(bf16[8,64,256]{2,1,0:T(8,128)(2,1)S(1)} %collective-permute-done.a1), channel_id=1, source_target_pairs={{0,1},{1,2},{2,3},{3,0},{4,5},{5,6},{6,7},{7,4},{8,9},{9,10},{10,1... | collective-permute-start | bytes 786440 | tf_op jit(solution)/shard_map/ppermute | solution.py:253
  10.5 1.2 collective-permute-start.7
  11.7 0.8 collective-permute-start.9
  12.5 0.8 pad_maximum_fusion.d0
  13.3 1.3 collective-permute-start.3
  14.5 8.0 %collective-permute-done.3.d1 = f32[9,4,256]{2,1,0:T(4,128)S(1)} collective-permute-done((f32[9,4,256]{2,1,0:T(4,128)S(1)}, f32[9,4,256]{2,1,0:T(4,128)S(1)}, u32[]{:S(2)}, u32[]{:S(2)}) %collective-permute-start.3) | collective-permute-done | bytes 36896 | tf_op jit(solution)/shard_map/ppermute | solution.py:253
  22.6 3.0 %collective-permute-start.4 = (f32[9,4,256]{2,1,0:T(4,128)S(1)}, f32[9,4,256]{2,1,0:T(4,128)S(1)}, u32[]{:S(2)}, u32[]{:S(2)}) collective-permute-start(f32[9,4,256]{2,1,0:T(4,128)S(1)} %pad_maximum_fusion.d0), channel_id=1, source_target_pairs={{0,3},{1,0},{2,1},{3,2},{4,7},{5,4},{6,5},{7,6},{8,11},{9,8},{10,9... | collective-permute-start | bytes 110600 | tf_op jit(solution)/shard_map/ppermute | solution.py:253
  25.5 1.6 %collective-permute-done.4.d2 = f32[9,4,256]{2,1,0:T(4,128)S(1)} collective-permute-done((f32[9,4,256]{2,1,0:T(4,128)S(1)}, f32[9,4,256]{2,1,0:T(4,128)S(1)}, u32[]{:S(2)}, u32[]{:S(2)}) %collective-permute-start.4) | collective-permute-done | bytes 36896 | tf_op jit(solution)/shard_map/ppermute | solution.py:253
  27.2 2.7 %collective-permute-start.5 = (f32[9,4,256]{2,1,0:T(4,128)S(1)}, f32[9,4,256]{2,1,0:T(4,128)S(1)}, u32[]{:S(2)}, u32[]{:S(2)}) collective-permute-start(f32[9,4,256]{2,1,0:T(4,128)S(1)} %pad_maximum_fusion.d0), channel_id=1, source_target_pairs={{0,2},{1,3},{2,0},{3,1},{4,6},{5,7},{6,4},{7,5},{8,10},{9,11},{10,... | collective-permute-start | bytes 110600 | tf_op jit(solution)/shard_map/ppermute | solution.py:253
  29.9 0.9 copy-done.2
  30.8 0.9 copy-done.3
  31.8 0.9 copy-done.4
  32.8 2.1 %shard_map.69 = (bf16[8,256,256]{2,1,0:T(8,128)(2,1)S(1)}, f32[9,16,256]{2,1,0:T(8,128)S(1)}, f32[8,272,256]{2,1,0:T(8,128)S(1)}, f32[8,272,256]{2,1,0:T(8,128)S(1)}, f32[272,256]{1,0:T(8,128)S(1)}) custom-call(bf16[8,64,256]{2,1,0:T(8,128)(2,1)S(1)} %get-tuple-element.26.a0, bf16[8,64,256]{2,1,0:T(8,128)(2,1)S(1)} %collective-permute-done.a1, ...), custom_call_target="tpu_custom_call" | custom-call | tf_op jit(solution)/shard_map/pallas_call | solution.py:229
  35.0 1.8 %shard_map.70 = (bf16[8,256,256]{2,1,0:T(8,128)(2,1)S(1)}, f32[528,256]{1,0:T(8,128)S(1)}) custom-call(bf16[8,64,256]{2,1,0:T(8,128)(2,1)S(1)} %get-tuple-element.31.g0, bf16[8,64,256]{2,1,0:T(8,128)(2,1)S(1)} %collective-permute-done.7.g1, bf16[8,64,256]{2,1,0:T(8,128)(2,1)S(1)} %collective-permute-done.8.g2, ...), custom_call_target="tpu_custom_call" | custom-call | tf_op jit(solution)/shard_map/pallas_call | solution.py:229
  36.9 0.5 collective-permute-start.6
  37.4 1.8 %collective-permute-done.6.x_m.x_bm = f32[272,256]{1,0:T(8,128)S(1)} collective-permute-done((f32[272,256]{1,0:T(8,128)S(1)}, f32[272,256]{1,0:T(8,128)S(1)}, u32[]{:S(2)}, u32[]{:S(2)}) %collective-permute-start.6) | collective-permute-done | bytes 278560 | tf_op jit(solution)/shard_map/ppermute | solution.py:250
  39.2 1.1 shard_map.71
  40.3 7.7 %collective-permute-start.11 = (f32[272,256]{1,0:T(8,128)S(1)}, f32[272,256]{1,0:T(8,128)S(1)}, u32[]{:S(2)}, u32[]{:S(2)}) collective-permute-start(f32[272,256]{1,0:T(8,128)S(1)} %get-tuple-element.35.r_0_), channel_id=1, source_target_pairs={{8,0},{16,8},{24,16},{32,24},{40,32},{48,40},{56,48},{64,56},{72,6... | collective-permute-start | bytes 835592 | tf_op jit(solution)/shard_map/ppermute | solution.py:245
  48.0 4.0 %collective-permute-done.11.r_1_ = f32[272,256]{1,0:T(8,128)S(1)} collective-permute-done((f32[272,256]{1,0:T(8,128)S(1)}, f32[272,256]{1,0:T(8,128)S(1)}, u32[]{:S(2)}, u32[]{:S(2)}) %collective-permute-start.11) | collective-permute-done | bytes 278560 | tf_op jit(solution)/shard_map/ppermute | solution.py:245
  52.0 1.2 shard_map.72
  53.2 4.8 %collective-permute-start.12 = (f32[272,256]{1,0:T(8,128)S(1)}, f32[272,256]{1,0:T(8,128)S(1)}, u32[]{:S(2)}, u32[]{:S(2)}) collective-permute-start(f32[272,256]{1,0:T(8,128)S(1)} %get-tuple-element.38.r_0_), channel_id=1, source_target_pairs={{16,0},{24,8},{32,16},{40,24},{48,32},{56,40},{64,48},{72,56},{80,... | collective-permute-start | bytes 835592 | tf_op jit(solution)/shard_map/ppermute | solution.py:245
  58.1 1.3 collective-permute-start.13
  59.4 1.3 collective-permute-start.14
  60.7 3.2 %collective-permute-done.12.r_1_ = f32[272,256]{1,0:T(8,128)S(1)} collective-permute-done((f32[272,256]{1,0:T(8,128)S(1)}, f32[272,256]{1,0:T(8,128)S(1)}, u32[]{:S(2)}, u32[]{:S(2)}) %collective-permute-start.12) | collective-permute-done | bytes 278560 | tf_op jit(solution)/shard_map/ppermute | solution.py:245
  63.9 2.7 %collective-permute-done.13.r_2_ = f32[272,256]{1,0:T(8,128)S(1)} collective-permute-done((f32[272,256]{1,0:T(8,128)S(1)}, f32[272,256]{1,0:T(8,128)S(1)}, u32[]{:S(2)}, u32[]{:S(2)}) %collective-permute-start.13) | collective-permute-done | bytes 278560 | tf_op jit(solution)/shard_map/ppermute | solution.py:245
  66.5 1.3 collective-permute-done.14.r_3_
  67.8 1.2 shard_map.73
  69.1 2.8 %collective-permute-start.15 = (f32[272,256]{1,0:T(8,128)S(1)}, f32[272,256]{1,0:T(8,128)S(1)}, u32[]{:S(2)}, u32[]{:S(2)}) collective-permute-start(f32[272,256]{1,0:T(8,128)S(1)} %get-tuple-element.39.r_0_), channel_id=1, source_target_pairs={{32,0},{40,8},{48,16},{56,24},{64,32},{72,40},{80,48},{88,56},{96,... | collective-permute-start | bytes 835592 | tf_op jit(solution)/shard_map/ppermute | solution.py:245
  71.9 1.3 collective-permute-start.16
  73.2 1.3 collective-permute-start.17
  74.5 12.7 %collective-permute-done.15.r_1_ = f32[272,256]{1,0:T(8,128)S(1)} collective-permute-done((f32[272,256]{1,0:T(8,128)S(1)}, f32[272,256]{1,0:T(8,128)S(1)}, u32[]{:S(2)}, u32[]{:S(2)}) %collective-permute-start.15) | collective-permute-done | bytes 278560 | tf_op jit(solution)/shard_map/ppermute | solution.py:245
  87.1 1.2 shard_map.74
  88.4 2.3 %collective-permute-start.18 = (f32[272,256]{1,0:T(8,128)S(1)}, f32[272,256]{1,0:T(8,128)S(1)}, u32[]{:S(2)}, u32[]{:S(2)}) collective-permute-start(f32[272,256]{1,0:T(8,128)S(1)} %get-tuple-element.40.r_0_), channel_id=1, source_target_pairs={{64,0},{72,8},{80,16},{88,24},{96,32},{104,40},{112,48},{120,56},{... | collective-permute-start | bytes 835592 | tf_op jit(solution)/shard_map/ppermute | solution.py:245
  90.7 1.3 collective-permute-start.19
  92.0 1.3 collective-permute-start.20
  93.3 3.5 %collective-permute-done.18.r_1_ = f32[272,256]{1,0:T(8,128)S(1)} collective-permute-done((f32[272,256]{1,0:T(8,128)S(1)}, f32[272,256]{1,0:T(8,128)S(1)}, u32[]{:S(2)}, u32[]{:S(2)}) %collective-permute-start.18) | collective-permute-done | bytes 278560 | tf_op jit(solution)/shard_map/ppermute | solution.py:245
  96.8 2.3 %collective-permute-done.19.r_2_ = f32[272,256]{1,0:T(8,128)S(1)} collective-permute-done((f32[272,256]{1,0:T(8,128)S(1)}, f32[272,256]{1,0:T(8,128)S(1)}, u32[]{:S(2)}, u32[]{:S(2)}) %collective-permute-start.19) | collective-permute-done | bytes 278560 | tf_op jit(solution)/shard_map/ppermute | solution.py:245
  99.2 1.3 collective-permute-done.20.r_3_
  100.5 0.6 shard_map.75
  101.1 1.3 collective-permute-start.27
  102.4 1.3 collective-permute-start.28
  103.7 1.3 collective-permute-start.29
  105.0 0.7 collective-permute-start.21
  105.7 0.1 shard_map.76
  105.8 0.7 collective-permute-start.22
  106.5 1.3 collective-permute-start.23
  107.9 4.7 %collective-permute-done.23 = f32[16,256]{1,0:T(8,128)S(1)} collective-permute-done((f32[16,256]{1,0:T(8,128)S(1)}, f32[16,256]{1,0:T(8,128)S(1)}, u32[]{:S(2)}, u32[]{:S(2)}) %collective-permute-start.23) | collective-permute-done | bytes 16416 | tf_op jit(solution)/shard_map/ppermute | solution.py:245
  112.6 1.2 shard_map.78
  113.8 0.4 shard_map.79
  114.2 2.1 %collective-permute-start.30 = (f32[16,256]{1,0:T(8,128)S(1)}, f32[16,256]{1,0:T(8,128)S(1)}, u32[]{:S(2)}, u32[]{:S(2)}) collective-permute-start(f32[16,256]{1,0:T(8,128)S(1)} %shard_map.79), channel_id=1, source_target_pairs={{1,5},{9,13},{17,21},{25,29},{33,37},{41,45},{49,53},{57,61},{65,6... | collective-permute-start | bytes 49160 | tf_op jit(solution)/shard_map/ppermute | solution.py:245
  116.2 1.3 collective-permute-start.24
  117.5 1.3 collective-permute-start.25
  118.8 1.3 collective-permute-start.26
  120.2 1.3 collective-permute-start.31
  121.4 1.3 collective-permute-start.32
  122.8 1.3 collective-permute-start.33
  124.1 1.9 %collective-permute-start.34 = (f32[16,256]{1,0:T(8,128)S(1)}, f32[16,256]{1,0:T(8,128)S(1)}, u32[]{:S(2)}, u32[]{:S(2)}) collective-permute-start(f32[16,256]{1,0:T(8,128)S(1)} %broadcast_select_fusion), channel_id=1, source_target_pairs={{9,1},{13,5},{17,9},{21,13},{25,17},{29,21},{33,25},{37,29},{41,33... | collective-permute-start | bytes 49160 | tf_op jit(solution)/shard_map/ppermute | solution.py:245
  126.0 1.9 %shard_map.77 = (f32[8,8,256]{2,1,0:T(8,128)S(1)}, f32[8,8,256]{2,1,0:T(8,128)S(1)}, f32[8,256]{1,0:T(8,128)S(1)}, f32[8,4,256]{2,1,0:T(4,128)}) custom-call(bf16[8,256,256]{2,1,0:T(8,128)(2,1)S(1)} %get-tuple-element.28.r_4_.araw, f32[9,16,256]{2,1,0:T(8,128)S(1)} %get-tuple-element.29.r_5_.drive, f32[256,256]{1,0:T(8,128)S(1)} %get-tuple-element.27.dyn, ...), custom_call_target="tpu_custom_call" | custom-call | tf_op jit(solution)/shard_map/pallas_call | solution.py:229
  127.9 1.8 %collective-permute-done.34.s3 = f32[16,256]{1,0:T(8,128)S(1)} collective-permute-done((f32[16,256]{1,0:T(8,128)S(1)}, f32[16,256]{1,0:T(8,128)S(1)}, u32[]{:S(2)}, u32[]{:S(2)}) %collective-permute-start.34) | collective-permute-done | bytes 16416 | tf_op jit(solution)/shard_map/ppermute | solution.py:245
  129.7 2.0 %shard_map.80 = f32[8,4,256]{2,1,0:T(4,128)} custom-call(bf16[8,256,256]{2,1,0:T(8,128)(2,1)S(1)} %copy-done.1, f32[8,8,256]{2,1,0:T(8,128)S(1)} %get-tuple-element.45.xs, f32[8,8,256]{2,1,0:T(8,128)S(1)} %get-tuple-element.46.proj, f32[8,256]{1,0:T(8,128)S(1)} %get-tuple-element.47.mid, f32[528,256]{1,0:T(8,128)S(1)} %collective-permute-done.10.qy_m, ...), custom_call_target="tpu_custom_call" | custom-call | tf_op jit(solution)/shard_map/pallas_call | solution.py:229
  (32 shorter events, 0.2 us)
Async XLA Ops:
  0.6 8.3 %collective-permute-start = (bf16[8,64,256]{2,1,0:T(8,128)(2,1)}, bf16[8,64,256]{2,1,0:T(8,128)(2,1)S(1)}, u32[]{:S(2)}, u32[]{:S(2)}) collective-permute-start(bf16[8,64,256]{2,1,0:T(8,128)(2,1)} %a.1), channel_id=1, source_target_pairs={{0,1},{1,2},{2,3},{3,0},{4,5},{5,6},{6,7},{7,4},{8,9},{9,10},{10,1... | collective-permute-start | bytes 786440 | tf_op jit(solution)/shard_map/ppermute | solution.py:253
  2.2 9.5 %collective-permute-start.8 = (bf16[8,64,256]{2,1,0:T(8,128)(2,1)}, bf16[8,64,256]{2,1,0:T(8,128)(2,1)S(1)}, u32[]{:S(2)}, u32[]{:S(2)}) collective-permute-start(bf16[8,64,256]{2,1,0:T(8,128)(2,1)} %g.1), channel_id=1, source_target_pairs={{0,3},{1,0},{2,1},{3,2},{4,7},{5,4},{6,5},{7,6},{8,11},{9,8},{10,9... | collective-permute-start | bytes 786440 | tf_op jit(solution)/shard_map/ppermute | solution.py:253
  2.7 30.0 %collective-permute-start.1 = (bf16[8,64,256]{2,1,0:T(8,128)(2,1)}, bf16[8,64,256]{2,1,0:T(8,128)(2,1)S(1)}, u32[]{:S(2)}, u32[]{:S(2)}) collective-permute-start(bf16[8,64,256]{2,1,0:T(8,128)(2,1)} %a.1), channel_id=1, source_target_pairs={{0,3},{1,0},{2,1},{3,2},{4,7},{5,4},{6,5},{7,6},{8,11},{9,8},{10,9... | collective-permute-start | bytes 786440 | tf_op jit(solution)/shard_map/ppermute | solution.py:253
  9.0 23.8 %collective-permute-start.2 = (bf16[8,64,256]{2,1,0:T(8,128)(2,1)S(1)}, bf16[8,64,256]{2,1,0:T(8,128)(2,1)S(1)}, u32[]{:S(2)}, u32[]{:S(2)}) collective-permute-start(bf16[8,64,256]{2,1,0:T(8,128)(2,1)S(1)} %collective-permute-done.a1), channel_id=1, source_target_pairs={{0,1},{1,2},{2,3},{3,0},{4,5},{5,6},{6,7},{7,4},{8,9},{9,10},{10,1... | collective-permute-start | bytes 786440 | tf_op jit(solution)/shard_map/ppermute | solution.py:253
  10.5 24.5 %collective-permute-start.7 = (bf16[8,64,256]{2,1,0:T(8,128)(2,1)}, bf16[8,64,256]{2,1,0:T(8,128)(2,1)S(1)}, u32[]{:S(2)}, u32[]{:S(2)}) collective-permute-start(bf16[8,64,256]{2,1,0:T(8,128)(2,1)} %g.1), channel_id=1, source_target_pairs={{0,1},{1,2},{2,3},{3,0},{4,5},{5,6},{6,7},{7,4},{8,9},{9,10},{10,1... | collective-permute-start | bytes 786440 | tf_op jit(solution)/shard_map/ppermute | solution.py:253
  11.7 23.3 %collective-permute-start.9 = (bf16[8,64,256]{2,1,0:T(8,128)(2,1)S(1)}, bf16[8,64,256]{2,1,0:T(8,128)(2,1)S(1)}, u32[]{:S(2)}, u32[]{:S(2)}) collective-permute-start(bf16[8,64,256]{2,1,0:T(8,128)(2,1)S(1)} %collective-permute-done.8.g2), channel_id=1, source_target_pairs={{0,3},{1,0},{2,1},{3,2},{4,7},{5,4},{6,5},{7,6},{8,11},{9,8},{10,9... | collective-permute-start | bytes 786440 | tf_op jit(solution)/shard_map/ppermute | solution.py:253
  13.3 9.3 %collective-permute-start.3 = (f32[9,4,256]{2,1,0:T(4,128)S(1)}, f32[9,4,256]{2,1,0:T(4,128)S(1)}, u32[]{:S(2)}, u32[]{:S(2)}) collective-permute-start(f32[9,4,256]{2,1,0:T(4,128)S(1)} %pad_maximum_fusion.d0), channel_id=1, source_target_pairs={{0,1},{1,2},{2,3},{3,0},{4,5},{5,6},{6,7},{7,4},{8,9},{9,10},{10,1... | collective-permute-start | bytes 110600 | tf_op jit(solution)/shard_map/ppermute | solution.py:253
  22.6 4.6 %collective-permute-start.4 = (f32[9,4,256]{2,1,0:T(4,128)S(1)}, f32[9,4,256]{2,1,0:T(4,128)S(1)}, u32[]{:S(2)}, u32[]{:S(2)}) collective-permute-start(f32[9,4,256]{2,1,0:T(4,128)S(1)} %pad_maximum_fusion.d0), channel_id=1, source_target_pairs={{0,3},{1,0},{2,1},{3,2},{4,7},{5,4},{6,5},{7,6},{8,11},{9,8},{10,9... | collective-permute-start | bytes 110600 | tf_op jit(solution)/shard_map/ppermute | solution.py:253
  27.2 5.6 %collective-permute-start.5 = (f32[9,4,256]{2,1,0:T(4,128)S(1)}, f32[9,4,256]{2,1,0:T(4,128)S(1)}, u32[]{:S(2)}, u32[]{:S(2)}) collective-permute-start(f32[9,4,256]{2,1,0:T(4,128)S(1)} %pad_maximum_fusion.d0), channel_id=1, source_target_pairs={{0,2},{1,3},{2,0},{3,1},{4,6},{5,7},{6,4},{7,5},{8,10},{9,11},{10,... | collective-permute-start | bytes 110600 | tf_op jit(solution)/shard_map/ppermute | solution.py:253
  29.9 0.9 copy-start.2
  30.8 0.9 copy-start.3
  31.8 0.9 copy-start.4
  36.8 32.3 %copy-start = (bf16[8,256,256]{2,1,0:T(8,128)(2,1)}, bf16[8,256,256]{2,1,0:T(8,128)(2,1)S(1)}, u32[]{:S(2)}) copy-start(bf16[8,256,256]{2,1,0:T(8,128)(2,1)S(1)} %get-tuple-element.44.graw) | copy-start | bytes 3145732
  36.8 2.4 %collective-permute-start.10 = (f32[528,256]{1,0:T(8,128)S(1)}, f32[528,256]{1,0:T(8,128)S(1)}, u32[]{:S(2)}, u32[]{:S(2)}) collective-permute-start(f32[528,256]{1,0:T(8,128)S(1)} %get-tuple-element.34.qy), channel_id=1, source_target_pairs={{0,4},{4,0},{8,12},{12,8},{16,20},{20,16},{24,28},{28,24},{32,36},... | collective-permute-start | bytes 1622024 | tf_op jit(solution)/shard_map/ppermute | solution.py:250
  36.9 2.3 %collective-permute-start.6 = (f32[272,256]{1,0:T(8,128)S(1)}, f32[272,256]{1,0:T(8,128)S(1)}, u32[]{:S(2)}, u32[]{:S(2)}) collective-permute-start(f32[272,256]{1,0:T(8,128)S(1)} %get-tuple-element.30.x.x_b), channel_id=1, source_target_pairs={{0,4},{4,0},{8,12},{12,8},{16,20},{20,16},{24,28},{28,24},{32,36},... | collective-permute-start | bytes 835592 | tf_op jit(solution)/shard_map/ppermute | solution.py:250
  40.3 11.7 %collective-permute-start.11 = (f32[272,256]{1,0:T(8,128)S(1)}, f32[272,256]{1,0:T(8,128)S(1)}, u32[]{:S(2)}, u32[]{:S(2)}) collective-permute-start(f32[272,256]{1,0:T(8,128)S(1)} %get-tuple-element.35.r_0_), channel_id=1, source_target_pairs={{8,0},{16,8},{24,16},{32,24},{40,32},{48,40},{56,48},{64,56},{72,6... | collective-permute-start | bytes 835592 | tf_op jit(solution)/shard_map/ppermute | solution.py:245
  53.2 10.6 %collective-permute-start.12 = (f32[272,256]{1,0:T(8,128)S(1)}, f32[272,256]{1,0:T(8,128)S(1)}, u32[]{:S(2)}, u32[]{:S(2)}) collective-permute-start(f32[272,256]{1,0:T(8,128)S(1)} %get-tuple-element.38.r_0_), channel_id=1, source_target_pairs={{16,0},{24,8},{32,16},{40,24},{48,32},{56,40},{64,48},{72,56},{80,... | collective-permute-start | bytes 835592 | tf_op jit(solution)/shard_map/ppermute | solution.py:245
  58.1 8.4 %collective-permute-start.13 = (f32[272,256]{1,0:T(8,128)S(1)}, f32[272,256]{1,0:T(8,128)S(1)}, u32[]{:S(2)}, u32[]{:S(2)}) collective-permute-start(f32[272,256]{1,0:T(8,128)S(1)} %get-tuple-element.38.r_0_), channel_id=1, source_target_pairs={{0,1},{8,9},{16,17},{24,25},{32,33},{40,41},{48,49},{56,57},{64,65... | collective-permute-start | bytes 835592 | tf_op jit(solution)/shard_map/ppermute | solution.py:245
  59.4 8.4 %collective-permute-start.14 = (f32[272,256]{1,0:T(8,128)S(1)}, f32[272,256]{1,0:T(8,128)S(1)}, u32[]{:S(2)}, u32[]{:S(2)}) collective-permute-start(f32[272,256]{1,0:T(8,128)S(1)} %get-tuple-element.38.r_0_), channel_id=1, source_target_pairs={{2,1},{10,9},{18,17},{26,25},{34,33},{42,41},{50,49},{58,57},{66,6... | collective-permute-start | bytes 835592 | tf_op jit(solution)/shard_map/ppermute | solution.py:245
  69.1 18.1 %collective-permute-start.15 = (f32[272,256]{1,0:T(8,128)S(1)}, f32[272,256]{1,0:T(8,128)S(1)}, u32[]{:S(2)}, u32[]{:S(2)}) collective-permute-start(f32[272,256]{1,0:T(8,128)S(1)} %get-tuple-element.39.r_0_), channel_id=1, source_target_pairs={{32,0},{40,8},{48,16},{56,24},{64,32},{72,40},{80,48},{88,56},{96,... | collective-permute-start | bytes 835592 | tf_op jit(solution)/shard_map/ppermute | solution.py:245
  71.9 15.3 %collective-permute-start.16 = (f32[272,256]{1,0:T(8,128)S(1)}, f32[272,256]{1,0:T(8,128)S(1)}, u32[]{:S(2)}, u32[]{:S(2)}) collective-permute-start(f32[272,256]{1,0:T(8,128)S(1)} %get-tuple-element.39.r_0_), channel_id=1, source_target_pairs={{0,1},{8,9},{16,17},{24,25},{32,33},{40,41},{48,49},{56,57},{64,65... | collective-permute-start | bytes 835592 | tf_op jit(solution)/shard_map/ppermute | solution.py:245
  73.2 14.0 %collective-permute-start.17 = (f32[272,256]{1,0:T(8,128)S(1)}, f32[272,256]{1,0:T(8,128)S(1)}, u32[]{:S(2)}, u32[]{:S(2)}) collective-permute-start(f32[272,256]{1,0:T(8,128)S(1)} %get-tuple-element.39.r_0_), channel_id=1, source_target_pairs={{2,1},{10,9},{18,17},{26,25},{34,33},{42,41},{50,49},{58,57},{66,6... | collective-permute-start | bytes 835592 | tf_op jit(solution)/shard_map/ppermute | solution.py:245
  88.4 8.4 %collective-permute-start.18 = (f32[272,256]{1,0:T(8,128)S(1)}, f32[272,256]{1,0:T(8,128)S(1)}, u32[]{:S(2)}, u32[]{:S(2)}) collective-permute-start(f32[272,256]{1,0:T(8,128)S(1)} %get-tuple-element.40.r_0_), channel_id=1, source_target_pairs={{64,0},{72,8},{80,16},{88,24},{96,32},{104,40},{112,48},{120,56},{... | collective-permute-start | bytes 835592 | tf_op jit(solution)/shard_map/ppermute | solution.py:245
  90.7 8.4 %collective-permute-start.19 = (f32[272,256]{1,0:T(8,128)S(1)}, f32[272,256]{1,0:T(8,128)S(1)}, u32[]{:S(2)}, u32[]{:S(2)}) collective-permute-start(f32[272,256]{1,0:T(8,128)S(1)} %get-tuple-element.40.r_0_), channel_id=1, source_target_pairs={{0,1},{8,9},{16,17},{24,25},{32,33},{40,41},{48,49},{56,57},{64,65... | collective-permute-start | bytes 835592 | tf_op jit(solution)/shard_map/ppermute | solution.py:245
  92.0 8.4 %collective-permute-start.20 = (f32[272,256]{1,0:T(8,128)S(1)}, f32[272,256]{1,0:T(8,128)S(1)}, u32[]{:S(2)}, u32[]{:S(2)}) collective-permute-start(f32[272,256]{1,0:T(8,128)S(1)} %get-tuple-element.40.r_0_), channel_id=1, source_target_pairs={{2,1},{10,9},{18,17},{26,25},{34,33},{42,41},{50,49},{58,57},{66,6... | collective-permute-start | bytes 835592 | tf_op jit(solution)/shard_map/ppermute | solution.py:245
  101.1 11.5 %collective-permute-start.27 = (f32[272,256]{1,0:T(8,128)S(1)}, f32[272,256]{1,0:T(8,128)}, u32[]{:S(2)}, u32[]{:S(2)}) collective-permute-start(f32[272,256]{1,0:T(8,128)S(1)} %get-tuple-element.41.own), channel_id=1, source_target_pairs={{0,1},{8,9},{16,17},{24,25},{32,33},{40,41},{48,49},{56,57},{64,65... | collective-permute-start | bytes 835592 | tf_op jit(solution)/shard_map/ppermute | solution.py:245
  102.4 11.3 %collective-permute-start.28 = (f32[272,256]{1,0:T(8,128)S(1)}, f32[272,256]{1,0:T(8,128)S(1)}, u32[]{:S(2)}, u32[]{:S(2)}) collective-permute-start(f32[272,256]{1,0:T(8,128)S(1)} %get-tuple-element.41.own), channel_id=1, source_target_pairs={{2,1},{10,9},{18,17},{26,25},{34,33},{42,41},{50,49},{58,57},{66,6... | collective-permute-start | bytes 835592 | tf_op jit(solution)/shard_map/ppermute | solution.py:245
  103.7 10.1 %collective-permute-start.29 = (f32[272,256]{1,0:T(8,128)S(1)}, f32[272,256]{1,0:T(8,128)S(1)}, u32[]{:S(2)}, u32[]{:S(2)}) collective-permute-start(f32[272,256]{1,0:T(8,128)S(1)} %get-tuple-element.41.own), channel_id=1, source_target_pairs={{129,1},{137,9},{145,17},{153,25},{161,33},{169,41},{177,49},{185,... | collective-permute-start | bytes 835592 | tf_op jit(solution)/shard_map/ppermute | solution.py:245
  105.0 0.7 collective-permute-start.21
  105.8 0.7 collective-permute-start.22
  106.5 6.0 %collective-permute-start.23 = (f32[16,256]{1,0:T(8,128)S(1)}, f32[16,256]{1,0:T(8,128)S(1)}, u32[]{:S(2)}, u32[]{:S(2)}) collective-permute-start(f32[16,256]{1,0:T(8,128)S(1)} %collective-permute-done.22), channel_id=1, source_target_pairs={{5,1},{13,9},{21,17},{29,25},{37,33},{45,41},{53,49},{61,57},{69,6... | collective-permute-start | bytes 49160 | tf_op jit(solution)/shard_map/ppermute | solution.py:245
  107.9 21.8 %copy-start.1 = (bf16[8,256,256]{2,1,0:T(8,128)(2,1)S(1)}, bf16[8,256,256]{2,1,0:T(8,128)(2,1)}, u32[]{:S(2)}) copy-start(bf16[8,256,256]{2,1,0:T(8,128)(2,1)} %copy-done) | copy-start | bytes 3145732
  114.2 6.0 %collective-permute-start.30 = (f32[16,256]{1,0:T(8,128)S(1)}, f32[16,256]{1,0:T(8,128)S(1)}, u32[]{:S(2)}, u32[]{:S(2)}) collective-permute-start(f32[16,256]{1,0:T(8,128)S(1)} %shard_map.79), channel_id=1, source_target_pairs={{1,5},{9,13},{17,21},{25,29},{33,37},{41,45},{49,53},{57,61},{65,6... | collective-permute-start | bytes 49160 | tf_op jit(solution)/shard_map/ppermute | solution.py:245
  116.2 6.5 %collective-permute-start.24 = (f32[16,256]{1,0:T(8,128)S(1)}, f32[16,256]{1,0:T(8,128)S(1)}, u32[]{:S(2)}, u32[]{:S(2)}) collective-permute-start(f32[16,256]{1,0:T(8,128)S(1)} %broadcast_select_fusion.1.x_r.begin), channel_id=1, source_target_pairs={{1,3},{5,7},{9,11},{13,15},{17,19},{21,23},{25,27},{29,31},{33,35}... | collective-permute-start | bytes 49160 | tf_op jit(solution)/shard_map/ppermute | solution.py:245
  117.5 6.5 %collective-permute-start.25 = (f32[16,256]{1,0:T(8,128)S(1)}, f32[16,256]{1,0:T(8,128)S(1)}, u32[]{:S(2)}, u32[]{:S(2)}) collective-permute-start(f32[16,256]{1,0:T(8,128)S(1)} %broadcast_select_fusion.1.x_r.begin), channel_id=1, source_target_pairs={{1,0},{5,4},{9,8},{13,12},{17,16},{21,20},{25,24},{29,28},{33,32},... | collective-permute-start | bytes 49160 | tf_op jit(solution)/shard_map/ppermute | solution.py:245
  118.8 7.2 %collective-permute-start.26 = (f32[16,256]{1,0:T(8,128)S(1)}, f32[16,256]{1,0:T(8,128)S(1)}, u32[]{:S(2)}, u32[]{:S(2)}) collective-permute-start(f32[16,256]{1,0:T(8,128)S(1)} %broadcast_select_fusion.1.x_r.begin), channel_id=1, source_target_pairs={{1,2},{5,6},{9,10},{13,14},{17,18},{21,22},{25,26},{29,30},{33,34}... | collective-permute-start | bytes 49160 | tf_op jit(solution)/shard_map/ppermute | solution.py:245
  120.2 7.8 %collective-permute-start.31 = (f32[16,256]{1,0:T(8,128)S(1)}, f32[16,256]{1,0:T(8,128)S(1)}, u32[]{:S(2)}, u32[]{:S(2)}) collective-permute-start(f32[16,256]{1,0:T(8,128)S(1)} %broadcast_select_fusion), channel_id=1, source_target_pairs={{9,3},{13,7},{17,11},{21,15},{25,19},{29,23},{33,27},{37,31},{41,3... | collective-permute-start | bytes 49160 | tf_op jit(solution)/shard_map/ppermute | solution.py:245
  121.4 6.5 %collective-permute-start.32 = (f32[16,256]{1,0:T(8,128)S(1)}, f32[16,256]{1,0:T(8,128)S(1)}, u32[]{:S(2)}, u32[]{:S(2)}) collective-permute-start(f32[16,256]{1,0:T(8,128)S(1)} %broadcast_select_fusion), channel_id=1, source_target_pairs={{9,0},{13,4},{17,8},{21,12},{25,16},{29,20},{33,24},{37,28},{41,32... | collective-permute-start | bytes 49160 | tf_op jit(solution)/shard_map/ppermute | solution.py:245
  122.8 5.2 %collective-permute-start.33 = (f32[16,256]{1,0:T(8,128)S(1)}, f32[16,256]{1,0:T(8,128)S(1)}, u32[]{:S(2)}, u32[]{:S(2)}) collective-permute-start(f32[16,256]{1,0:T(8,128)S(1)} %broadcast_select_fusion), channel_id=1, source_target_pairs={{9,2},{13,6},{17,10},{21,14},{25,18},{29,22},{33,26},{37,30},{41,3... | collective-permute-start | bytes 49160 | tf_op jit(solution)/shard_map/ppermute | solution.py:245
  124.1 5.6 %collective-permute-start.34 = (f32[16,256]{1,0:T(8,128)S(1)}, f32[16,256]{1,0:T(8,128)S(1)}, u32[]{:S(2)}, u32[]{:S(2)}) collective-permute-start(f32[16,256]{1,0:T(8,128)S(1)} %broadcast_select_fusion), channel_id=1, source_target_pairs={{9,1},{13,5},{17,9},{21,13},{25,17},{29,21},{33,25},{37,29},{41,33... | collective-permute-start | bytes 49160 | tf_op jit(solution)/shard_map/ppermute | solution.py:245
where the time goes:
time: 132 us
  starting transfers between devices  58.5 us (44%)
  waiting for transfers between devices  53.5 us (41%)
  Pallas kernels  15.1 us (11%)
  local copies, waits for them, and re-layouts  2.86 us (2%)
    ppermute x24, starting transfers between devices, send(): lax.ppermute(x, ('tm', 'col'), [(a * cols + b, c * cols + d) for (a, b),...  43.6 us
    ppermute x24, waiting for transfers between devices, send(): lax.ppermute(x, ('tm', 'col'), [(a * cols + b, c * cols + d) for (a, b),...  37.5 us
    pallas_call x13, Pallas kernels, call(): pl.pallas_call(kernel, out_shape=tuple((jax.ShapeDtypeStruct(s, d) for s,...  15.1 us
    ppermute x9, starting transfers between devices, turn(): return lax.ppermute(x, 'col', [(c, (c + by) % 4) for c in range(4)])  14.3 us
    ppermute x9, waiting for transfers between devices, turn(): return lax.ppermute(x, 'col', [(c, (c + by) % 4) for c in range(4)])  14.2 us
    unnamed x10, local copies, waits for them, and re-layouts  2.86 us
  transfers between devices with their start and end apart: 35, of which 14 were waited for; matrix products, arithmetic and copies ran while one was open for 1% of the time, Pallas kernels for 4%

commit v1 on v0

--- a/solution.py
+++ b/solution.py
@@ -7,7 +7,7 @@
 
 
 SUF_X, SUF_Y, SUF_Q = (0, 0), (1, 0), (2, 0)
-PRE_X = (1, 1)
+PRE_X = (3, 0)
 D = 256
 SER = 16
 GRP = 8
@@ -40,8 +40,8 @@
     return tm, lax.rem(tm, 2), lax.axis_index("col")
 
 
-def roles(core, col):
-    return col == 0, jnp.logical_and(col == 1, core == 0), jnp.logical_and(col == 1, core == 1)
+def roles(col):
+    return col == 0, col == 1, col == 3
 
 
 def aligned(index, unit):
@@ -110,7 +110,7 @@
 
 def chip_kernel(x, x_m, qy, qy_m, own, xrow, qrow):
     _, core, col = place()
-    suf_x, suf_y, pre_x = roles(core, col)
+    suf_x, suf_y, pre_x = roles(col)
 
     def work(x0_ref, e0, x1, e1):
         x0, q0 = x0_ref[...], e0[:D, :]
@@ -135,8 +135,8 @@
 
 
 def round_kernel(dist, own, got, xrow, qrow, kept_a, kept_d, out, vec):
-    tm, core, col = place()
-    suf_x, suf_y, pre_x = roles(core, col)
+    tm, _, col = place()
+    suf_x, suf_y, pre_x = roles(col)
     chip = lax.div(tm, 2)
     later = chip + dist < lax.axis_size("tm") // 2
 
@@ -181,11 +181,11 @@
     return jnp.where(low, value[:GRP], value[GRP:])
 
 
-def mean_sweep_kernel(araw, drive, dyn, x_b, x_bm, x_r, x0, x2, x3, xs, proj, mid, filt):
+def mean_sweep_kernel(araw, drive, dyn, x_b, x_bm, m0, m1, m2, m3, m4, xs, proj, mid, filt):
     tm, core, col = place()
     steps = araw.shape[0]
     low = col < 2
-    begin = group(jnp.where(col == 1, x_r[...], x0[...] + x2[...] + x3[...]), low)
+    begin = group((m0[...] + m1[...]) + (m2[...] + m3[...]) + m4[...], low)
 
     @pl.when(core == 0)
     def _():
@@ -327,20 +327,20 @@
     xrow = hop(own, [(SUF_X, SUF_Y)])
     qrow = hop(own, [(SUF_Q, SUF_Y)])
     (leaving,) = call(mean_kernel, [vector], own, got_v)
-    x_one = hop(leaving, [(PRE_X, PRE_X)], 1)
+    means = [hop(leaving, [(PRE_X, (c, 0))], 1) for c in range(4)]
+    begin = means[1]
+    means.append(hop(sum(means), [((c, 0), (c, 1)) for c in range(4)]))
     first = lax.rem(lax.axis_index("tm"), 2) == 0
-    x_two = jnp.where(first, hop(x_one, [(PRE_X, SUF_Y)]), x_one)
-    means = [hop(x_two, across(c)) for c in (3, 0, 2)]
-    near, mid = call(near_kernel, [vector, vector], own, xrow, x_two)
+    near, mid = call(near_kernel, [vector, vector], own, xrow, begin)
     (s_one,) = call(top_kernel, [vector], near, mid, qrow, got)
-    s_two = jnp.where(first, s_one, hop(s_one, [(SUF_Y, PRE_X)]))
+    s_two = jnp.where(first, s_one, hop(s_one, [(SUF_Y, (1, 1))]))
     s_in = [hop(s_two, across(c), -1) for c in (3, 0, 2, 1)]
     part = ((steps, GRP, D), f32)
     result = ((steps, drive.shape[1], D), f32)
     xs8, proj8, mid8, filtered = call(
         mean_sweep_kernel,
         [part, part, ((GRP, D), f32), result],
-        araw, drive16, dyn, x_b, x_bm, x_two, *means,
+        araw, drive16, dyn, x_b, x_bm, *means,
     )
     (smoothed,) = call(smooth_sweep_kernel, [result], graw, xs8, proj8, mid8, qy_bm, *s_in)
     return filtered, smoothed

time: 132 us -> 136 us (1.030)
  the two profiles are of different devices: /device:TPU:18 before, /device:TPU:26 now
where the time goes in v1:
time: 136 us
  starting transfers between devices  61.7 us (45%)
  waiting for transfers between devices  53.5 us (39%)
  Pallas kernels  14.1 us (10%)
  local copies, waits for them, and re-layouts  4.5 us (3%)
    ppermute x24, starting transfers between devices, send(): lax.ppermute(x, ('tm', 'col'), [(a * cols + b, c * cols + d) for (a, b),...  46.8 us
    ppermute x24, waiting for transfers between devices, send(): lax.ppermute(x, ('tm', 'col'), [(a * cols + b, c * cols + d) for (a, b),...  37.6 us
    ppermute x9, starting transfers between devices, turn(): return lax.ppermute(x, 'col', [(c, (c + by) % 4) for c in range(4)])  14.3 us
    ppermute x9, waiting for transfers between devices, turn(): return lax.ppermute(x, 'col', [(c, (c + by) % 4) for c in range(4)])  14.2 us
    pallas_call x13, Pallas kernels, call(): pl.pallas_call(kernel, out_shape=tuple((jax.ShapeDtypeStruct(s, d) for s,...  14.1 us
    unnamed x14, local copies, waits for them, and re-layouts  4.5 us
  transfers between devices with their start and end apart: 35, of which 14 were waited for; matrix products, arithmetic and copies ran while one was open for 1% of the time, Pallas kernels for 4%

profile of v1, /device:TPU:26, one launch (start us, length us, event | category | flops | bytes accessed | tf_op | source)
XLA Modules:
  0.0 135.7 jit_solution(11030388313352481833)
XLA Ops:
  0.6 1.6 %collective-permute-start = (bf16[8,64,256]{2,1,0:T(8,128)(2,1)}, bf16[8,64,256]{2,1,0:T(8,128)(2,1)S(1)}, u32[]{:S(2)}, u32[]{:S(2)}) collective-permute-start(bf16[8,64,256]{2,1,0:T(8,128)(2,1)} %a.1), channel_id=1, source_target_pairs={{0,1},{1,2},{2,3},{3,0},{4,5},{5,6},{6,7},{7,4},{8,9},{9,10},{10,1... | collective-permute-start | bytes 786440 | tf_op jit(solution)/shard_map/ppermute | solution.py:253
  2.2 0.5 collective-permute-start.8
  2.7 1.7 %collective-permute-start.1 = (bf16[8,64,256]{2,1,0:T(8,128)(2,1)}, bf16[8,64,256]{2,1,0:T(8,128)(2,1)S(1)}, u32[]{:S(2)}, u32[]{:S(2)}) collective-permute-start(bf16[8,64,256]{2,1,0:T(8,128)(2,1)} %a.1), channel_id=1, source_target_pairs={{0,3},{1,0},{2,1},{3,2},{4,7},{5,4},{6,5},{7,6},{8,11},{9,8},{10,9... | collective-permute-start | bytes 786440 | tf_op jit(solution)/shard_map/ppermute | solution.py:253
  4.5 4.5 %collective-permute-done.a1 = bf16[8,64,256]{2,1,0:T(8,128)(2,1)S(1)} collective-permute-done((bf16[8,64,256]{2,1,0:T(8,128)(2,1)}, bf16[8,64,256]{2,1,0:T(8,128)(2,1)S(1)}, u32[]{:S(2)}, u32[]{:S(2)}) %collective-permute-start) | collective-permute-done | bytes 262176 | tf_op jit(solution)/shard_map/ppermute | solution.py:253
  9.0 1.5 %collective-permute-start.2 = (bf16[8,64,256]{2,1,0:T(8,128)(2,1)S(1)}, bf16[8,64,256]{2,1,0:T(8,128)(2,1)S(1)}, u32[]{:S(2)}, u32[]{:S(2)}) collective-permute-start(bf16[8,64,256]{2,1,0:T(8,128)(2,1)S(1)} %collective-permute-done.a1), channel_id=1, source_target_pairs={{0,1},{1,2},{2,3},{3,0},{4,5},{5,6},{6,7},{7,4},{8,9},{9,10},{10,1... | collective-permute-start | bytes 786440 | tf_op jit(solution)/shard_map/ppermute | solution.py:253
  10.5 1.2 collective-permute-start.7
  11.7 0.8 collective-permute-start.9
  12.5 0.8 pad_maximum_fusion.d0
  13.3 1.3 collective-permute-start.3
  14.5 8.0 %collective-permute-done.3.d1 = f32[9,4,256]{2,1,0:T(4,128)S(1)} collective-permute-done((f32[9,4,256]{2,1,0:T(4,128)S(1)}, f32[9,4,256]{2,1,0:T(4,128)S(1)}, u32[]{:S(2)}, u32[]{:S(2)}) %collective-permute-start.3) | collective-permute-done | bytes 36896 | tf_op jit(solution)/shard_map/ppermute | solution.py:253
  22.6 3.0 %collective-permute-start.4 = (f32[9,4,256]{2,1,0:T(4,128)S(1)}, f32[9,4,256]{2,1,0:T(4,128)S(1)}, u32[]{:S(2)}, u32[]{:S(2)}) collective-permute-start(f32[9,4,256]{2,1,0:T(4,128)S(1)} %pad_maximum_fusion.d0), channel_id=1, source_target_pairs={{0,3},{1,0},{2,1},{3,2},{4,7},{5,4},{6,5},{7,6},{8,11},{9,8},{10,9... | collective-permute-start | bytes 110600 | tf_op jit(solution)/shard_map/ppermute | solution.py:253
  25.5 1.6 %collective-permute-done.4.d2 = f32[9,4,256]{2,1,0:T(4,128)S(1)} collective-permute-done((f32[9,4,256]{2,1,0:T(4,128)S(1)}, f32[9,4,256]{2,1,0:T(4,128)S(1)}, u32[]{:S(2)}, u32[]{:S(2)}) %collective-permute-start.4) | collective-permute-done | bytes 36896 | tf_op jit(solution)/shard_map/ppermute | solution.py:253
  27.2 2.7 %collective-permute-start.5 = (f32[9,4,256]{2,1,0:T(4,128)S(1)}, f32[9,4,256]{2,1,0:T(4,128)S(1)}, u32[]{:S(2)}, u32[]{:S(2)}) collective-permute-start(f32[9,4,256]{2,1,0:T(4,128)S(1)} %pad_maximum_fusion.d0), channel_id=1, source_target_pairs={{0,2},{1,3},{2,0},{3,1},{4,6},{5,7},{6,4},{7,5},{8,10},{9,11},{10,... | collective-permute-start | bytes 110600 | tf_op jit(solution)/shard_map/ppermute | solution.py:253
  29.9 0.9 copy-done.4
  30.8 0.9 copy-done.5
  31.8 0.9 copy-done.6
  32.8 2.1 %shard_map.69 = (bf16[8,256,256]{2,1,0:T(8,128)(2,1)S(1)}, f32[9,16,256]{2,1,0:T(8,128)S(1)}, f32[8,272,256]{2,1,0:T(8,128)S(1)}, f32[8,272,256]{2,1,0:T(8,128)S(1)}, f32[272,256]{1,0:T(8,128)S(1)}) custom-call(bf16[8,64,256]{2,1,0:T(8,128)(2,1)S(1)} %get-tuple-element.26.a0, bf16[8,64,256]{2,1,0:T(8,128)(2,1)S(1)} %collective-permute-done.a1, ...), custom_call_target="tpu_custom_call" | custom-call | tf_op jit(solution)/shard_map/pallas_call | solution.py:229
  35.0 1.8 %shard_map.70 = (bf16[8,256,256]{2,1,0:T(8,128)(2,1)S(1)}, f32[528,256]{1,0:T(8,128)S(1)}) custom-call(bf16[8,64,256]{2,1,0:T(8,128)(2,1)S(1)} %get-tuple-element.31.g0, bf16[8,64,256]{2,1,0:T(8,128)(2,1)S(1)} %collective-permute-done.7.g1, bf16[8,64,256]{2,1,0:T(8,128)(2,1)S(1)} %collective-permute-done.8.g2, ...), custom_call_target="tpu_custom_call" | custom-call | tf_op jit(solution)/shard_map/pallas_call | solution.py:229
  36.9 0.5 collective-permute-start.6
  37.4 1.8 %collective-permute-done.6.x_m.x_bm = f32[272,256]{1,0:T(8,128)S(1)} collective-permute-done((f32[272,256]{1,0:T(8,128)S(1)}, f32[272,256]{1,0:T(8,128)S(1)}, u32[]{:S(2)}, u32[]{:S(2)}) %collective-permute-start.6) | collective-permute-done | bytes 278560 | tf_op jit(solution)/shard_map/ppermute | solution.py:250
  39.2 1.1 shard_map.71
  40.3 7.9 %collective-permute-start.11 = (f32[272,256]{1,0:T(8,128)S(1)}, f32[272,256]{1,0:T(8,128)S(1)}, u32[]{:S(2)}, u32[]{:S(2)}) collective-permute-start(f32[272,256]{1,0:T(8,128)S(1)} %get-tuple-element.35.r_0_), channel_id=1, source_target_pairs={{8,0},{16,8},{24,16},{32,24},{40,32},{48,40},{56,48},{64,56},{72,6... | collective-permute-start | bytes 835592 | tf_op jit(solution)/shard_map/ppermute | solution.py:245
  48.2 4.0 %collective-permute-done.11.r_1_ = f32[272,256]{1,0:T(8,128)S(1)} collective-permute-done((f32[272,256]{1,0:T(8,128)S(1)}, f32[272,256]{1,0:T(8,128)S(1)}, u32[]{:S(2)}, u32[]{:S(2)}) %collective-permute-start.11) | collective-permute-done | bytes 278560 | tf_op jit(solution)/shard_map/ppermute | solution.py:245
  52.3 1.2 shard_map.72
  53.5 4.8 %collective-permute-start.12 = (f32[272,256]{1,0:T(8,128)S(1)}, f32[272,256]{1,0:T(8,128)S(1)}, u32[]{:S(2)}, u32[]{:S(2)}) collective-permute-start(f32[272,256]{1,0:T(8,128)S(1)} %get-tuple-element.38.r_0_), channel_id=1, source_target_pairs={{16,0},{24,8},{32,16},{40,24},{48,32},{56,40},{64,48},{72,56},{80,... | collective-permute-start | bytes 835592 | tf_op jit(solution)/shard_map/ppermute | solution.py:245
  58.4 1.3 collective-permute-start.13
  59.7 1.3 collective-permute-start.14
  61.0 4.4 %collective-permute-done.12.r_1_ = f32[272,256]{1,0:T(8,128)S(1)} collective-permute-done((f32[272,256]{1,0:T(8,128)S(1)}, f32[272,256]{1,0:T(8,128)S(1)}, u32[]{:S(2)}, u32[]{:S(2)}) %collective-permute-start.12) | collective-permute-done | bytes 278560 | tf_op jit(solution)/shard_map/ppermute | solution.py:245
  65.3 1.5 %collective-permute-done.13.r_2_ = f32[272,256]{1,0:T(8,128)S(1)} collective-permute-done((f32[272,256]{1,0:T(8,128)S(1)}, f32[272,256]{1,0:T(8,128)S(1)}, u32[]{:S(2)}, u32[]{:S(2)}) %collective-permute-start.13) | collective-permute-done | bytes 278560 | tf_op jit(solution)/shard_map/ppermute | solution.py:245
  66.8 1.3 collective-permute-done.14.r_3_
  68.1 1.2 shard_map.73
  69.4 2.8 %collective-permute-start.15 = (f32[272,256]{1,0:T(8,128)S(1)}, f32[272,256]{1,0:T(8,128)S(1)}, u32[]{:S(2)}, u32[]{:S(2)}) collective-permute-start(f32[272,256]{1,0:T(8,128)S(1)} %get-tuple-element.39.r_0_), channel_id=1, source_target_pairs={{32,0},{40,8},{48,16},{56,24},{64,32},{72,40},{80,48},{88,56},{96,... | collective-permute-start | bytes 835592 | tf_op jit(solution)/shard_map/ppermute | solution.py:245
  72.2 1.3 collective-permute-start.16
  73.5 1.3 collective-permute-start.17
  74.8 9.5 %collective-permute-done.15.r_1_ = f32[272,256]{1,0:T(8,128)S(1)} collective-permute-done((f32[272,256]{1,0:T(8,128)S(1)}, f32[272,256]{1,0:T(8,128)S(1)}, u32[]{:S(2)}, u32[]{:S(2)}) %collective-permute-start.15) | collective-permute-done | bytes 278560 | tf_op jit(solution)/shard_map/ppermute | solution.py:245
  84.3 1.2 shard_map.74
  85.6 2.4 %collective-permute-start.18 = (f32[272,256]{1,0:T(8,128)S(1)}, f32[272,256]{1,0:T(8,128)S(1)}, u32[]{:S(2)}, u32[]{:S(2)}) collective-permute-start(f32[272,256]{1,0:T(8,128)S(1)} %get-tuple-element.40.r_0_), channel_id=1, source_target_pairs={{64,0},{72,8},{80,16},{88,24},{96,32},{104,40},{112,48},{120,56},{... | collective-permute-start | bytes 835592 | tf_op jit(solution)/shard_map/ppermute | solution.py:245
  87.9 1.3 collective-permute-start.19
  89.2 1.3 collective-permute-start.20
  90.5 1.4 %collective-permute-done.18.r_1_ = f32[272,256]{1,0:T(8,128)S(1)} collective-permute-done((f32[272,256]{1,0:T(8,128)S(1)}, f32[272,256]{1,0:T(8,128)S(1)}, u32[]{:S(2)}, u32[]{:S(2)}) %collective-permute-start.18) | collective-permute-done | bytes 278560 | tf_op jit(solution)/shard_map/ppermute | solution.py:245
  92.0 4.4 %collective-permute-done.19.r_2_ = f32[272,256]{1,0:T(8,128)S(1)} collective-permute-done((f32[272,256]{1,0:T(8,128)S(1)}, f32[272,256]{1,0:T(8,128)S(1)}, u32[]{:S(2)}, u32[]{:S(2)}) %collective-permute-start.19) | collective-permute-done | bytes 278560 | tf_op jit(solution)/shard_map/ppermute | solution.py:245
  96.4 1.3 collective-permute-done.20.r_3_
  97.7 0.6 shard_map.75
  98.3 1.3 collective-permute-start.27
  99.6 1.3 collective-permute-start.28
  100.9 2.6 %collective-permute-start.29 = (f32[272,256]{1,0:T(8,128)S(1)}, f32[272,256]{1,0:T(8,128)S(1)}, u32[]{:S(2)}, u32[]{:S(2)}) collective-permute-start(f32[272,256]{1,0:T(8,128)S(1)} %get-tuple-element.41.own), channel_id=1, source_target_pairs={{129,1},{137,9},{145,17},{153,25},{161,33},{169,41},{177,49},{185,... | collective-permute-start | bytes 835592 | tf_op jit(solution)/shard_map/ppermute | solution.py:245
  103.5 0.7 collective-permute-start.21
  104.4 1.3 collective-permute-start.23
  105.7 0.7 collective-permute-start.22
  106.4 8.2 %collective-permute-done.23.m1.begin = f32[16,256]{1,0:T(8,128)S(1)} collective-permute-done((f32[16,256]{1,0:T(8,128)S(1)}, f32[16,256]{1,0:T(8,128)S(1)}, u32[]{:S(2)}, u32[]{:S(2)}) %collective-permute-start.23) | collective-permute-done | bytes 16416 | tf_op jit(solution)/shard_map/ppermute | solution.py:245
  114.5 0.7 collective-permute-start.24
  115.2 0.7 copy-done.2
  115.9 0.7 collective-permute-start.25
  116.6 0.9 copy-done.3
  117.8 0.4 shard_map.79
  118.2 1.3 collective-permute-start.30
  119.5 1.3 collective-permute-start.26
  120.8 4.6 %collective-permute-start.31 = (f32[16,256]{1,0:T(8,128)S(1)}, f32[16,256]{1,0:T(8,128)S(1)}, u32[]{:S(2)}, u32[]{:S(2)}) collective-permute-start(f32[16,256]{1,0:T(8,128)S(1)} %broadcast_select_fusion), channel_id=1, source_target_pairs={{9,3},{13,7},{17,11},{21,15},{25,19},{29,23},{33,27},{37,31},{41,3... | collective-permute-start | bytes 49160 | tf_op jit(solution)/shard_map/ppermute | solution.py:245
  125.4 1.3 collective-permute-start.32
  126.7 1.3 collective-permute-start.33
  128.0 2.2 %collective-permute-start.34 = (f32[16,256]{1,0:T(8,128)S(1)}, f32[16,256]{1,0:T(8,128)S(1)}, u32[]{:S(2)}, u32[]{:S(2)}) collective-permute-start(f32[16,256]{1,0:T(8,128)S(1)} %broadcast_select_fusion), channel_id=1, source_target_pairs={{9,1},{13,5},{17,9},{21,13},{25,17},{29,21},{33,25},{37,29},{41,33... | collective-permute-start | bytes 49160 | tf_op jit(solution)/shard_map/ppermute | solution.py:245
  130.3 1.9 %shard_map.77 = (f32[8,8,256]{2,1,0:T(8,128)S(1)}, f32[8,8,256]{2,1,0:T(8,128)S(1)}, f32[8,256]{1,0:T(8,128)S(1)}, f32[8,4,256]{2,1,0:T(4,128)}) custom-call(bf16[8,256,256]{2,1,0:T(8,128)(2,1)S(1)} %get-tuple-element.28.r_4_.araw, f32[9,16,256]{2,1,0:T(8,128)S(1)} %get-tuple-element.29.r_5_.drive, f32[256,256]{1,0:T(8,128)S(1)} %get-tuple-element.27.dyn, ...), custom_call_target="tpu_custom_call" | custom-call | tf_op jit(solution)/shard_map/pallas_call | solution.py:229
  132.2 1.5 %collective-permute-done.34.s3 = f32[16,256]{1,0:T(8,128)S(1)} collective-permute-done((f32[16,256]{1,0:T(8,128)S(1)}, f32[16,256]{1,0:T(8,128)S(1)}, u32[]{:S(2)}, u32[]{:S(2)}) %collective-permute-start.34) | collective-permute-done | bytes 16416 | tf_op jit(solution)/shard_map/ppermute | solution.py:245
  133.7 2.0 %shard_map.80 = f32[8,4,256]{2,1,0:T(4,128)} custom-call(bf16[8,256,256]{2,1,0:T(8,128)(2,1)S(1)} %copy-done.1, f32[8,8,256]{2,1,0:T(8,128)S(1)} %get-tuple-element.45.xs, f32[8,8,256]{2,1,0:T(8,128)S(1)} %get-tuple-element.46.proj, f32[8,256]{1,0:T(8,128)S(1)} %get-tuple-element.47.mid, f32[528,256]{1,0:T(8,128)S(1)} %collective-permute-done.10.qy_m, ...), custom_call_target="tpu_custom_call" | custom-call | tf_op jit(solution)/shard_map/pallas_call | solution.py:229
  (36 shorter events, 0.6 us)
Async XLA Ops:
  0.6 8.3 %collective-permute-start = (bf16[8,64,256]{2,1,0:T(8,128)(2,1)}, bf16[8,64,256]{2,1,0:T(8,128)(2,1)S(1)}, u32[]{:S(2)}, u32[]{:S(2)}) collective-permute-start(bf16[8,64,256]{2,1,0:T(8,128)(2,1)} %a.1), channel_id=1, source_target_pairs={{0,1},{1,2},{2,3},{3,0},{4,5},{5,6},{6,7},{7,4},{8,9},{9,10},{10,1... | collective-permute-start | bytes 786440 | tf_op jit(solution)/shard_map/ppermute | solution.py:253
  2.2 9.5 %collective-permute-start.8 = (bf16[8,64,256]{2,1,0:T(8,128)(2,1)}, bf16[8,64,256]{2,1,0:T(8,128)(2,1)S(1)}, u32[]{:S(2)}, u32[]{:S(2)}) collective-permute-start(bf16[8,64,256]{2,1,0:T(8,128)(2,1)} %g.1), channel_id=1, source_target_pairs={{0,3},{1,0},{2,1},{3,2},{4,7},{5,4},{6,5},{7,6},{8,11},{9,8},{10,9... | collective-permute-start | bytes 786440 | tf_op jit(solution)/shard_map/ppermute | solution.py:253
  2.7 30.0 %collective-permute-start.1 = (bf16[8,64,256]{2,1,0:T(8,128)(2,1)}, bf16[8,64,256]{2,1,0:T(8,128)(2,1)S(1)}, u32[]{:S(2)}, u32[]{:S(2)}) collective-permute-start(bf16[8,64,256]{2,1,0:T(8,128)(2,1)} %a.1), channel_id=1, source_target_pairs={{0,3},{1,0},{2,1},{3,2},{4,7},{5,4},{6,5},{7,6},{8,11},{9,8},{10,9... | collective-permute-start | bytes 786440 | tf_op jit(solution)/shard_map/ppermute | solution.py:253
  9.0 23.8 %collective-permute-start.2 = (bf16[8,64,256]{2,1,0:T(8,128)(2,1)S(1)}, bf16[8,64,256]{2,1,0:T(8,128)(2,1)S(1)}, u32[]{:S(2)}, u32[]{:S(2)}) collective-permute-start(bf16[8,64,256]{2,1,0:T(8,128)(2,1)S(1)} %collective-permute-done.a1), channel_id=1, source_target_pairs={{0,1},{1,2},{2,3},{3,0},{4,5},{5,6},{6,7},{7,4},{8,9},{9,10},{10,1... | collective-permute-start | bytes 786440 | tf_op jit(solution)/shard_map/ppermute | solution.py:253
  10.5 24.5 %collective-permute-start.7 = (bf16[8,64,256]{2,1,0:T(8,128)(2,1)}, bf16[8,64,256]{2,1,0:T(8,128)(2,1)S(1)}, u32[]{:S(2)}, u32[]{:S(2)}) collective-permute-start(bf16[8,64,256]{2,1,0:T(8,128)(2,1)} %g.1), channel_id=1, source_target_pairs={{0,1},{1,2},{2,3},{3,0},{4,5},{5,6},{6,7},{7,4},{8,9},{9,10},{10,1... | collective-permute-start | bytes 786440 | tf_op jit(solution)/shard_map/ppermute | solution.py:253
  11.7 23.3 %collective-permute-start.9 = (bf16[8,64,256]{2,1,0:T(8,128)(2,1)S(1)}, bf16[8,64,256]{2,1,0:T(8,128)(2,1)S(1)}, u32[]{:S(2)}, u32[]{:S(2)}) collective-permute-start(bf16[8,64,256]{2,1,0:T(8,128)(2,1)S(1)} %collective-permute-done.8.g2), channel_id=1, source_target_pairs={{0,3},{1,0},{2,1},{3,2},{4,7},{5,4},{6,5},{7,6},{8,11},{9,8},{10,9... | collective-permute-start | bytes 786440 | tf_op jit(solution)/shard_map/ppermute | solution.py:253
  13.3 9.3 %collective-permute-start.3 = (f32[9,4,256]{2,1,0:T(4,128)S(1)}, f32[9,4,256]{2,1,0:T(4,128)S(1)}, u32[]{:S(2)}, u32[]{:S(2)}) collective-permute-start(f32[9,4,256]{2,1,0:T(4,128)S(1)} %pad_maximum_fusion.d0), channel_id=1, source_target_pairs={{0,1},{1,2},{2,3},{3,0},{4,5},{5,6},{6,7},{7,4},{8,9},{9,10},{10,1... | collective-permute-start | bytes 110600 | tf_op jit(solution)/shard_map/ppermute | solution.py:253
  22.6 4.6 %collective-permute-start.4 = (f32[9,4,256]{2,1,0:T(4,128)S(1)}, f32[9,4,256]{2,1,0:T(4,128)S(1)}, u32[]{:S(2)}, u32[]{:S(2)}) collective-permute-start(f32[9,4,256]{2,1,0:T(4,128)S(1)} %pad_maximum_fusion.d0), channel_id=1, source_target_pairs={{0,3},{1,0},{2,1},{3,2},{4,7},{5,4},{6,5},{7,6},{8,11},{9,8},{10,9... | collective-permute-start | bytes 110600 | tf_op jit(solution)/shard_map/ppermute | solution.py:253
  27.2 5.6 %collective-permute-start.5 = (f32[9,4,256]{2,1,0:T(4,128)S(1)}, f32[9,4,256]{2,1,0:T(4,128)S(1)}, u32[]{:S(2)}, u32[]{:S(2)}) collective-permute-start(f32[9,4,256]{2,1,0:T(4,128)S(1)} %pad_maximum_fusion.d0), channel_id=1, source_target_pairs={{0,2},{1,3},{2,0},{3,1},{4,6},{5,7},{6,4},{7,5},{8,10},{9,11},{10,... | collective-permute-start | bytes 110600 | tf_op jit(solution)/shard_map/ppermute | solution.py:253
  29.9 0.9 copy-start.4
  30.8 0.9 copy-start.5
  31.8 0.9 copy-start.6
  36.8 32.6 %copy-start = (bf16[8,256,256]{2,1,0:T(8,128)(2,1)}, bf16[8,256,256]{2,1,0:T(8,128)(2,1)S(1)}, u32[]{:S(2)}) copy-start(bf16[8,256,256]{2,1,0:T(8,128)(2,1)S(1)} %get-tuple-element.44.graw) | copy-start | bytes 3145732
  36.8 2.4 %collective-permute-start.10 = (f32[528,256]{1,0:T(8,128)S(1)}, f32[528,256]{1,0:T(8,128)S(1)}, u32[]{:S(2)}, u32[]{:S(2)}) collective-permute-start(f32[528,256]{1,0:T(8,128)S(1)} %get-tuple-element.34.qy), channel_id=1, source_target_pairs={{0,4},{4,0},{8,12},{12,8},{16,20},{20,16},{24,28},{28,24},{32,36},... | collective-permute-start | bytes 1622024 | tf_op jit(solution)/shard_map/ppermute | solution.py:250
  36.9 2.3 %collective-permute-start.6 = (f32[272,256]{1,0:T(8,128)S(1)}, f32[272,256]{1,0:T(8,128)S(1)}, u32[]{:S(2)}, u32[]{:S(2)}) collective-permute-start(f32[272,256]{1,0:T(8,128)S(1)} %get-tuple-element.30.x.x_b), channel_id=1, source_target_pairs={{0,4},{4,0},{8,12},{12,8},{16,20},{20,16},{24,28},{28,24},{32,36},... | collective-permute-start | bytes 835592 | tf_op jit(solution)/shard_map/ppermute | solution.py:250
  40.3 12.0 %collective-permute-start.11 = (f32[272,256]{1,0:T(8,128)S(1)}, f32[272,256]{1,0:T(8,128)S(1)}, u32[]{:S(2)}, u32[]{:S(2)}) collective-permute-start(f32[272,256]{1,0:T(8,128)S(1)} %get-tuple-element.35.r_0_), channel_id=1, source_target_pairs={{8,0},{16,8},{24,16},{32,24},{40,32},{48,40},{56,48},{64,56},{72,6... | collective-permute-start | bytes 835592 | tf_op jit(solution)/shard_map/ppermute | solution.py:245
  53.5 11.8 %collective-permute-start.12 = (f32[272,256]{1,0:T(8,128)S(1)}, f32[272,256]{1,0:T(8,128)S(1)}, u32[]{:S(2)}, u32[]{:S(2)}) collective-permute-start(f32[272,256]{1,0:T(8,128)S(1)} %get-tuple-element.38.r_0_), channel_id=1, source_target_pairs={{16,0},{24,8},{32,16},{40,24},{48,32},{56,40},{64,48},{72,56},{80,... | collective-permute-start | bytes 835592 | tf_op jit(solution)/shard_map/ppermute | solution.py:245
  58.4 8.4 %collective-permute-start.13 = (f32[272,256]{1,0:T(8,128)S(1)}, f32[272,256]{1,0:T(8,128)S(1)}, u32[]{:S(2)}, u32[]{:S(2)}) collective-permute-start(f32[272,256]{1,0:T(8,128)S(1)} %get-tuple-element.38.r_0_), channel_id=1, source_target_pairs={{0,1},{8,9},{16,17},{24,25},{32,33},{40,41},{48,49},{56,57},{64,65... | collective-permute-start | bytes 835592 | tf_op jit(solution)/shard_map/ppermute | solution.py:245
  59.7 8.4 %collective-permute-start.14 = (f32[272,256]{1,0:T(8,128)S(1)}, f32[272,256]{1,0:T(8,128)S(1)}, u32[]{:S(2)}, u32[]{:S(2)}) collective-permute-start(f32[272,256]{1,0:T(8,128)S(1)} %get-tuple-element.38.r_0_), channel_id=1, source_target_pairs={{2,1},{10,9},{18,17},{26,25},{34,33},{42,41},{50,49},{58,57},{66,6... | collective-permute-start | bytes 835592 | tf_op jit(solution)/shard_map/ppermute | solution.py:245
  69.4 14.9 %collective-permute-start.15 = (f32[272,256]{1,0:T(8,128)S(1)}, f32[272,256]{1,0:T(8,128)S(1)}, u32[]{:S(2)}, u32[]{:S(2)}) collective-permute-start(f32[272,256]{1,0:T(8,128)S(1)} %get-tuple-element.39.r_0_), channel_id=1, source_target_pairs={{32,0},{40,8},{48,16},{56,24},{64,32},{72,40},{80,48},{88,56},{96,... | collective-permute-start | bytes 835592 | tf_op jit(solution)/shard_map/ppermute | solution.py:245
  72.2 12.1 %collective-permute-start.16 = (f32[272,256]{1,0:T(8,128)S(1)}, f32[272,256]{1,0:T(8,128)S(1)}, u32[]{:S(2)}, u32[]{:S(2)}) collective-permute-start(f32[272,256]{1,0:T(8,128)S(1)} %get-tuple-element.39.r_0_), channel_id=1, source_target_pairs={{0,1},{8,9},{16,17},{24,25},{32,33},{40,41},{48,49},{56,57},{64,65... | collective-permute-start | bytes 835592 | tf_op jit(solution)/shard_map/ppermute | solution.py:245
  73.5 10.9 %collective-permute-start.17 = (f32[272,256]{1,0:T(8,128)S(1)}, f32[272,256]{1,0:T(8,128)S(1)}, u32[]{:S(2)}, u32[]{:S(2)}) collective-permute-start(f32[272,256]{1,0:T(8,128)S(1)} %get-tuple-element.39.r_0_), channel_id=1, source_target_pairs={{2,1},{10,9},{18,17},{26,25},{34,33},{42,41},{50,49},{58,57},{66,6... | collective-permute-start | bytes 835592 | tf_op jit(solution)/shard_map/ppermute | solution.py:245
  85.6 6.4 %collective-permute-start.18 = (f32[272,256]{1,0:T(8,128)S(1)}, f32[272,256]{1,0:T(8,128)S(1)}, u32[]{:S(2)}, u32[]{:S(2)}) collective-permute-start(f32[272,256]{1,0:T(8,128)S(1)} %get-tuple-element.40.r_0_), channel_id=1, source_target_pairs={{64,0},{72,8},{80,16},{88,24},{96,32},{104,40},{112,48},{120,56},{... | collective-permute-start | bytes 835592 | tf_op jit(solution)/shard_map/ppermute | solution.py:245
  87.9 8.4 %collective-permute-start.19 = (f32[272,256]{1,0:T(8,128)S(1)}, f32[272,256]{1,0:T(8,128)S(1)}, u32[]{:S(2)}, u32[]{:S(2)}) collective-permute-start(f32[272,256]{1,0:T(8,128)S(1)} %get-tuple-element.40.r_0_), channel_id=1, source_target_pairs={{0,1},{8,9},{16,17},{24,25},{32,33},{40,41},{48,49},{56,57},{64,65... | collective-permute-start | bytes 835592 | tf_op jit(solution)/shard_map/ppermute | solution.py:245
  89.2 8.4 %collective-permute-start.20 = (f32[272,256]{1,0:T(8,128)S(1)}, f32[272,256]{1,0:T(8,128)S(1)}, u32[]{:S(2)}, u32[]{:S(2)}) collective-permute-start(f32[272,256]{1,0:T(8,128)S(1)} %get-tuple-element.40.r_0_), channel_id=1, source_target_pairs={{2,1},{10,9},{18,17},{26,25},{34,33},{42,41},{50,49},{58,57},{66,6... | collective-permute-start | bytes 835592 | tf_op jit(solution)/shard_map/ppermute | solution.py:245
  98.3 16.9 %collective-permute-start.27 = (f32[272,256]{1,0:T(8,128)S(1)}, f32[272,256]{1,0:T(8,128)S(1)}, u32[]{:S(2)}, u32[]{:S(2)}) collective-permute-start(f32[272,256]{1,0:T(8,128)S(1)} %get-tuple-element.41.own), channel_id=1, source_target_pairs={{0,1},{8,9},{16,17},{24,25},{32,33},{40,41},{48,49},{56,57},{64,65... | collective-permute-start | bytes 835592 | tf_op jit(solution)/shard_map/ppermute | solution.py:245
  99.6 18.2 %collective-permute-start.28 = (f32[272,256]{1,0:T(8,128)S(1)}, f32[272,256]{1,0:T(8,128)S(1)}, u32[]{:S(2)}, u32[]{:S(2)}) collective-permute-start(f32[272,256]{1,0:T(8,128)S(1)} %get-tuple-element.41.own), channel_id=1, source_target_pairs={{2,1},{10,9},{18,17},{26,25},{34,33},{42,41},{50,49},{58,57},{66,6... | collective-permute-start | bytes 835592 | tf_op jit(solution)/shard_map/ppermute | solution.py:245
  100.9 16.9 %collective-permute-start.29 = (f32[272,256]{1,0:T(8,128)S(1)}, f32[272,256]{1,0:T(8,128)S(1)}, u32[]{:S(2)}, u32[]{:S(2)}) collective-permute-start(f32[272,256]{1,0:T(8,128)S(1)} %get-tuple-element.41.own), channel_id=1, source_target_pairs={{129,1},{137,9},{145,17},{153,25},{161,33},{169,41},{177,49},{185,... | collective-permute-start | bytes 835592 | tf_op jit(solution)/shard_map/ppermute | solution.py:245
  103.5 0.7 collective-permute-start.21
  104.4 10.2 %collective-permute-start.23 = (f32[16,256]{1,0:T(8,128)S(1)}, f32[16,256]{1,0:T(8,128)S(1)}, u32[]{:S(2)}, u32[]{:S(2)}) collective-permute-start(f32[16,256]{1,0:T(8,128)S(1)} %shard_map.76), channel_id=1, source_target_pairs={{3,9},{11,17},{19,25},{27,33},{35,41},{43,49},{51,57},{59,65},{67,... | collective-permute-start | bytes 49160 | tf_op jit(solution)/shard_map/ppermute | solution.py:245
  105.7 13.8 %collective-permute-start.22 = (f32[16,256]{1,0:T(8,128)S(1)}, f32[16,256]{1,0:T(8,128)S(1)}, u32[]{:S(2)}, u32[]{:S(2)}) collective-permute-start(f32[16,256]{1,0:T(8,128)S(1)} %shard_map.76), channel_id=1, source_target_pairs={{3,8},{11,16},{19,24},{27,32},{35,40},{43,48},{51,56},{59,64},{67,... | collective-permute-start | bytes 49160 | tf_op jit(solution)/shard_map/ppermute | solution.py:245
  114.5 5.0 %collective-permute-start.24 = (f32[16,256]{1,0:T(8,128)S(1)}, f32[16,256]{1,0:T(8,128)S(1)}, u32[]{:S(2)}, u32[]{:S(2)}) collective-permute-start(f32[16,256]{1,0:T(8,128)S(1)} %shard_map.76), channel_id=1, source_target_pairs={{3,10},{11,18},{19,26},{27,34},{35,42},{43,50},{51,58},{59,66},{67... | collective-permute-start | bytes 49160 | tf_op jit(solution)/shard_map/ppermute | solution.py:245
  115.2 0.7 copy-start.2
  115.9 3.6 %collective-permute-start.25 = (f32[16,256]{1,0:T(8,128)S(1)}, f32[16,256]{1,0:T(8,128)S(1)}, u32[]{:S(2)}, u32[]{:S(2)}) collective-permute-start(f32[16,256]{1,0:T(8,128)S(1)} %shard_map.76), channel_id=1, source_target_pairs={{3,11},{11,19},{19,27},{27,35},{35,43},{43,51},{51,59},{59,67},{67... | collective-permute-start | bytes 49160 | tf_op jit(solution)/shard_map/ppermute | solution.py:245
  116.6 1.0 copy-start.3
  117.5 16.1 %copy-start.1 = (bf16[8,256,256]{2,1,0:T(8,128)(2,1)S(1)}, bf16[8,256,256]{2,1,0:T(8,128)(2,1)}, u32[]{:S(2)}) copy-start(bf16[8,256,256]{2,1,0:T(8,128)(2,1)} %copy-done) | copy-start | bytes 3145732
  118.2 2.7 %collective-permute-start.30 = (f32[16,256]{1,0:T(8,128)S(1)}, f32[16,256]{1,0:T(8,128)S(1)}, u32[]{:S(2)}, u32[]{:S(2)}) collective-permute-start(f32[16,256]{1,0:T(8,128)S(1)} %shard_map.79), channel_id=1, source_target_pairs={{1,5},{9,13},{17,21},{25,29},{33,37},{41,45},{49,53},{57,61},{65,6... | collective-permute-start | bytes 49160 | tf_op jit(solution)/shard_map/ppermute | solution.py:245
  119.5 10.8 %collective-permute-start.26 = (f32[16,256]{1,0:T(8,128)S(1)}, f32[16,256]{1,0:T(8,128)S(1)}, u32[]{:S(2)}, u32[]{:S(2)}) collective-permute-start(f32[16,256]{1,0:T(8,128)S(1)} %add_add_fusion), channel_id=1, source_target_pairs={{0,4},{1,5},{2,6},{3,7},{8,12},{9,13},{10,14},{11,15},{16,20},{17,... | collective-permute-start | bytes 49160 | tf_op jit(solution)/shard_map/ppermute | solution.py:245
  120.8 11.3 %collective-permute-start.31 = (f32[16,256]{1,0:T(8,128)S(1)}, f32[16,256]{1,0:T(8,128)S(1)}, u32[]{:S(2)}, u32[]{:S(2)}) collective-permute-start(f32[16,256]{1,0:T(8,128)S(1)} %broadcast_select_fusion), channel_id=1, source_target_pairs={{9,3},{13,7},{17,11},{21,15},{25,19},{29,23},{33,27},{37,31},{41,3... | collective-permute-start | bytes 49160 | tf_op jit(solution)/shard_map/ppermute | solution.py:245
  125.4 6.7 %collective-permute-start.32 = (f32[16,256]{1,0:T(8,128)S(1)}, f32[16,256]{1,0:T(8,128)S(1)}, u32[]{:S(2)}, u32[]{:S(2)}) collective-permute-start(f32[16,256]{1,0:T(8,128)S(1)} %broadcast_select_fusion), channel_id=1, source_target_pairs={{9,0},{13,4},{17,8},{21,12},{25,16},{29,20},{33,24},{37,28},{41,32... | collective-permute-start | bytes 49160 | tf_op jit(solution)/shard_map/ppermute | solution.py:245
  126.7 5.4 %collective-permute-start.33 = (f32[16,256]{1,0:T(8,128)S(1)}, f32[16,256]{1,0:T(8,128)S(1)}, u32[]{:S(2)}, u32[]{:S(2)}) collective-permute-start(f32[16,256]{1,0:T(8,128)S(1)} %broadcast_select_fusion), channel_id=1, source_target_pairs={{9,2},{13,6},{17,10},{21,14},{25,18},{29,22},{33,26},{37,30},{41,3... | collective-permute-start | bytes 49160 | tf_op jit(solution)/shard_map/ppermute | solution.py:245
  128.0 5.6 %collective-permute-start.34 = (f32[16,256]{1,0:T(8,128)S(1)}, f32[16,256]{1,0:T(8,128)S(1)}, u32[]{:S(2)}, u32[]{:S(2)}) collective-permute-start(f32[16,256]{1,0:T(8,128)S(1)} %broadcast_select_fusion), channel_id=1, source_target_pairs={{9,1},{13,5},{17,9},{21,13},{25,17},{29,21},{33,25},{37,29},{41,33... | collective-permute-start | bytes 49160 | tf_op jit(solution)/shard_map/ppermute | solution.py:245

commit v2 on v1

--- a/solution.py
+++ b/solution.py
@@ -134,7 +134,7 @@
         work(x_m, qy_m, x, qy)
 
 
-def round_kernel(dist, own, got, xrow, qrow, kept_a, kept_d, out, vec):
+def round_kernel(dist, own, got, xrow, qrow, kept_a, kept_d, kept_g, out, vec):
     tm, _, col = place()
     suf_x, suf_y, pre_x = roles(col)
     chip = lax.div(tm, 2)
@@ -318,7 +318,7 @@
         own, vec = call(
             lambda *r, dist=dist: round_kernel(dist, *r),
             [whole, vector],
-            own, got, xrow, qrow, araw, drive16,
+            own, got, xrow, qrow, araw, drive16, dyn,
         )
         dist *= 2
 
@@ -329,12 +329,13 @@
     (leaving,) = call(mean_kernel, [vector], own, got_v)
     means = [hop(leaving, [(PRE_X, (c, 0))], 1) for c in range(4)]
     begin = means[1]
-    means.append(hop(sum(means), [((c, 0), (c, 1)) for c in range(4)]))
+    total = (means[0] + means[1]) + (means[2] + means[3])
+    means.append(hop(total, [((c, 0), (c, 1)) for c in range(4)]))
     first = lax.rem(lax.axis_index("tm"), 2) == 0
     near, mid = call(near_kernel, [vector, vector], own, xrow, begin)
     (s_one,) = call(top_kernel, [vector], near, mid, qrow, got)
     s_two = jnp.where(first, s_one, hop(s_one, [(SUF_Y, (1, 1))]))
-    s_in = [hop(s_two, across(c), -1) for c in (3, 0, 2, 1)]
+    s_in = [hop(s_two, across(c), -1) for c in (0, 2, 1, 3)]
     part = ((steps, GRP, D), f32)
     result = ((steps, drive.shape[1], D), f32)
     xs8, proj8, mid8, filtered = call(

time: 136 us -> 134 us (0.985)
  the two profiles are of different devices: /device:TPU:26 before, /device:TPU:30 now
where the time goes in v2:
time: 134 us; the launch traced here: 133 us
  waiting for transfers between devices  68.7 us (51%)
  starting transfers between devices  45.7 us (34%)
  Pallas kernels  12.8 us (10%)
  local copies, waits for them, and re-layouts  4.5 us (3%)
    ppermute x24, waiting for transfers between devices, send(): lax.ppermute(x, ('tm', 'col'), [(a * cols + b, c * cols + d) for (a, b),...  47.8 us
    ppermute x24, starting transfers between devices, send(): lax.ppermute(x, ('tm', 'col'), [(a * cols + b, c * cols + d) for (a, b),...  35.2 us
    ppermute x9, waiting for transfers between devices, turn(): return lax.ppermute(x, 'col', [(c, (c + by) % 4) for c in range(4)])  19 us
    pallas_call x13, Pallas kernels, call(): pl.pallas_call(kernel, out_shape=tuple((jax.ShapeDtypeStruct(s, d) for s,...  12.8 us
    ppermute x9, starting transfers between devices, turn(): return lax.ppermute(x, 'col', [(c, (c + by) % 4) for c in range(4)])  9.87 us
    unnamed x14, local copies, waits for them, and re-layouts  4.5 us
  transfers between devices with their start and end apart: 35, of which 14 were waited for; matrix products, arithmetic and copies ran while one was open for 1% of the time, Pallas kernels for 4%

profile of v2, /device:TPU:30, one launch (start us, length us, event | category | flops | bytes accessed | tf_op | source)
XLA Modules:
  0.0 133.4 jit_solution(20767056222549986)
XLA Ops:
  0.6 0.6 collective-permute-start
  1.2 1.5 %collective-permute-start.8 = (bf16[8,64,256]{2,1,0:T(8,128)(2,1)}, bf16[8,64,256]{2,1,0:T(8,128)(2,1)S(1)}, u32[]{:S(2)}, u32[]{:S(2)}) collective-permute-start(bf16[8,64,256]{2,1,0:T(8,128)(2,1)} %g.1), channel_id=1, source_target_pairs={{0,3},{1,0},{2,1},{3,2},{4,7},{5,4},{6,5},{7,6},{8,11},{9,8},{10,9... | collective-permute-start | bytes 786440 | tf_op jit(solution)/shard_map/ppermute | solution.py:253
  2.7 0.8 collective-permute-start.1
  3.6 5.4 %collective-permute-done.a1 = bf16[8,64,256]{2,1,0:T(8,128)(2,1)S(1)} collective-permute-done((bf16[8,64,256]{2,1,0:T(8,128)(2,1)}, bf16[8,64,256]{2,1,0:T(8,128)(2,1)S(1)}, u32[]{:S(2)}, u32[]{:S(2)}) %collective-permute-start) | collective-permute-done | bytes 262176 | tf_op jit(solution)/shard_map/ppermute | solution.py:253
  9.0 1.7 %collective-permute-start.2 = (bf16[8,64,256]{2,1,0:T(8,128)(2,1)S(1)}, bf16[8,64,256]{2,1,0:T(8,128)(2,1)S(1)}, u32[]{:S(2)}, u32[]{:S(2)}) collective-permute-start(bf16[8,64,256]{2,1,0:T(8,128)(2,1)S(1)} %collective-permute-done.a1), channel_id=1, source_target_pairs={{0,1},{1,2},{2,3},{3,0},{4,5},{5,6},{6,7},{7,4},{8,9},{9,10},{10,1... | collective-permute-start | bytes 786440 | tf_op jit(solution)/shard_map/ppermute | solution.py:253
  10.7 0.3 collective-permute-start.7
  10.9 0.8 collective-permute-done.8.g2
  11.8 0.9 collective-permute-start.9
  12.7 0.8 pad_maximum_fusion.d0
  13.5 2.4 %collective-permute-start.3 = (f32[9,4,256]{2,1,0:T(4,128)S(1)}, f32[9,4,256]{2,1,0:T(4,128)S(1)}, u32[]{:S(2)}, u32[]{:S(2)}) collective-permute-start(f32[9,4,256]{2,1,0:T(4,128)S(1)} %pad_maximum_fusion.d0), channel_id=1, source_target_pairs={{0,1},{1,2},{2,3},{3,0},{4,5},{5,6},{6,7},{7,4},{8,9},{9,10},{10,1... | collective-permute-start | bytes 110600 | tf_op jit(solution)/shard_map/ppermute | solution.py:253
  15.9 6.7 %collective-permute-done.3.d1 = f32[9,4,256]{2,1,0:T(4,128)S(1)} collective-permute-done((f32[9,4,256]{2,1,0:T(4,128)S(1)}, f32[9,4,256]{2,1,0:T(4,128)S(1)}, u32[]{:S(2)}, u32[]{:S(2)}) %collective-permute-start.3) | collective-permute-done | bytes 36896 | tf_op jit(solution)/shard_map/ppermute | solution.py:253
  22.6 0.8 collective-permute-start.4
  23.4 4.3 %collective-permute-done.4.d2 = f32[9,4,256]{2,1,0:T(4,128)S(1)} collective-permute-done((f32[9,4,256]{2,1,0:T(4,128)S(1)}, f32[9,4,256]{2,1,0:T(4,128)S(1)}, u32[]{:S(2)}, u32[]{:S(2)}) %collective-permute-start.4) | collective-permute-done | bytes 36896 | tf_op jit(solution)/shard_map/ppermute | solution.py:253
  27.7 0.8 collective-permute-start.5
  28.6 0.9 copy-done.4
  29.5 0.9 copy-done.5
  30.5 0.9 copy-done.6
  31.5 1.7 %collective-permute-done.5.d3 = f32[9,4,256]{2,1,0:T(4,128)S(1)} collective-permute-done((f32[9,4,256]{2,1,0:T(4,128)S(1)}, f32[9,4,256]{2,1,0:T(4,128)S(1)}, u32[]{:S(2)}, u32[]{:S(2)}) %collective-permute-start.5) | collective-permute-done | bytes 36896 | tf_op jit(solution)/shard_map/ppermute | solution.py:253
  33.2 2.1 %shard_map.69 = (bf16[8,256,256]{2,1,0:T(8,128)(2,1)S(1)}, f32[9,16,256]{2,1,0:T(8,128)S(1)}, f32[8,272,256]{2,1,0:T(8,128)S(1)}, f32[8,272,256]{2,1,0:T(8,128)S(1)}, f32[272,256]{1,0:T(8,128)S(1)}) custom-call(bf16[8,64,256]{2,1,0:T(8,128)(2,1)S(1)} %get-tuple-element.26.a0, bf16[8,64,256]{2,1,0:T(8,128)(2,1)S(1)} %collective-permute-done.a1, ...), custom_call_target="tpu_custom_call" | custom-call | tf_op jit(solution)/shard_map/pallas_call | solution.py:229
  35.4 1.8 %shard_map.70 = (bf16[8,256,256]{2,1,0:T(8,128)(2,1)S(1)}, f32[528,256]{1,0:T(8,128)S(1)}) custom-call(bf16[8,64,256]{2,1,0:T(8,128)(2,1)S(1)} %get-tuple-element.31.g0, bf16[8,64,256]{2,1,0:T(8,128)(2,1)S(1)} %collective-permute-done.7.g1, bf16[8,64,256]{2,1,0:T(8,128)(2,1)S(1)} %collective-permute-done.8.g2, ...), custom_call_target="tpu_custom_call" | custom-call | tf_op jit(solution)/shard_map/pallas_call | solution.py:229
  37.3 0.5 collective-permute-start.6
  37.8 1.8 %collective-permute-done.6.x_m.x_bm = f32[272,256]{1,0:T(8,128)S(1)} collective-permute-done((f32[272,256]{1,0:T(8,128)S(1)}, f32[272,256]{1,0:T(8,128)S(1)}, u32[]{:S(2)}, u32[]{:S(2)}) %collective-permute-start.6) | collective-permute-done | bytes 278560 | tf_op jit(solution)/shard_map/ppermute | solution.py:250
  39.6 1.1 shard_map.71
  40.7 3.8 %collective-permute-start.11 = (f32[272,256]{1,0:T(8,128)S(1)}, f32[272,256]{1,0:T(8,128)S(1)}, u32[]{:S(2)}, u32[]{:S(2)}) collective-permute-start(f32[272,256]{1,0:T(8,128)S(1)} %get-tuple-element.35.r_0_), channel_id=1, source_target_pairs={{8,0},{16,8},{24,16},{32,24},{40,32},{48,40},{56,48},{64,56},{72,6... | collective-permute-start | bytes 835592 | tf_op jit(solution)/shard_map/ppermute | solution.py:245
  44.5 8.6 %collective-permute-done.11.r_1_ = f32[272,256]{1,0:T(8,128)S(1)} collective-permute-done((f32[272,256]{1,0:T(8,128)S(1)}, f32[272,256]{1,0:T(8,128)S(1)}, u32[]{:S(2)}, u32[]{:S(2)}) %collective-permute-start.11) | collective-permute-done | bytes 278560 | tf_op jit(solution)/shard_map/ppermute | solution.py:245
  53.2 0.9 shard_map.72
  54.1 1.9 %collective-permute-start.12 = (f32[272,256]{1,0:T(8,128)S(1)}, f32[272,256]{1,0:T(8,128)S(1)}, u32[]{:S(2)}, u32[]{:S(2)}) collective-permute-start(f32[272,256]{1,0:T(8,128)S(1)} %get-tuple-element.38.r_0_), channel_id=1, source_target_pairs={{16,0},{24,8},{32,16},{40,24},{48,32},{56,40},{64,48},{72,56},{80,... | collective-permute-start | bytes 835592 | tf_op jit(solution)/shard_map/ppermute | solution.py:245
  56.0 0.7 collective-permute-start.13
  56.7 0.7 collective-permute-start.14
  57.4 10.6 %collective-permute-done.12.r_1_ = f32[272,256]{1,0:T(8,128)S(1)} collective-permute-done((f32[272,256]{1,0:T(8,128)S(1)}, f32[272,256]{1,0:T(8,128)S(1)}, u32[]{:S(2)}, u32[]{:S(2)}) %collective-permute-start.12) | collective-permute-done | bytes 278560 | tf_op jit(solution)/shard_map/ppermute | solution.py:245
  68.0 0.9 shard_map.73
  68.9 5.8 %collective-permute-start.15 = (f32[272,256]{1,0:T(8,128)S(1)}, f32[272,256]{1,0:T(8,128)S(1)}, u32[]{:S(2)}, u32[]{:S(2)}) collective-permute-start(f32[272,256]{1,0:T(8,128)S(1)} %get-tuple-element.39.r_0_), channel_id=1, source_target_pairs={{32,0},{40,8},{48,16},{56,24},{64,32},{72,40},{80,48},{88,56},{96,... | collective-permute-start | bytes 835592 | tf_op jit(solution)/shard_map/ppermute | solution.py:245
  74.7 0.7 collective-permute-start.16
  75.4 0.7 collective-permute-start.17
  76.1 8.5 %collective-permute-done.15.r_1_ = f32[272,256]{1,0:T(8,128)S(1)} collective-permute-done((f32[272,256]{1,0:T(8,128)S(1)}, f32[272,256]{1,0:T(8,128)S(1)}, u32[]{:S(2)}, u32[]{:S(2)}) %collective-permute-start.15) | collective-permute-done | bytes 278560 | tf_op jit(solution)/shard_map/ppermute | solution.py:245
  84.6 0.9 shard_map.74
  85.5 1.3 collective-permute-start.18
  86.8 0.7 collective-permute-start.19
  87.4 0.7 collective-permute-start.20
  88.1 5.8 %collective-permute-done.18.r_1_ = f32[272,256]{1,0:T(8,128)S(1)} collective-permute-done((f32[272,256]{1,0:T(8,128)S(1)}, f32[272,256]{1,0:T(8,128)S(1)}, u32[]{:S(2)}, u32[]{:S(2)}) %collective-permute-start.18) | collective-permute-done | bytes 278560 | tf_op jit(solution)/shard_map/ppermute | solution.py:245
  93.9 0.3 shard_map.75
  94.2 0.7 collective-permute-start.27
  94.9 0.7 collective-permute-start.28
  95.6 0.7 collective-permute-start.29
  96.3 1.3 collective-permute-start.21
  97.6 5.8 %collective-permute-done.21.got = f32[16,256]{1,0:T(8,128)S(1)} collective-permute-done((f32[16,256]{1,0:T(8,128)S(1)}, f32[16,256]{1,0:T(8,128)S(1)}, u32[]{:S(2)}, u32[]{:S(2)}) %collective-permute-start.21) | collective-permute-done | bytes 16416 | tf_op jit(solution)/shard_map/ppermute | solution.py:245
  103.5 5.3 %collective-permute-start.23 = (f32[16,256]{1,0:T(8,128)S(1)}, f32[16,256]{1,0:T(8,128)S(1)}, u32[]{:S(2)}, u32[]{:S(2)}) collective-permute-start(f32[16,256]{1,0:T(8,128)S(1)} %shard_map.76), channel_id=1, source_target_pairs={{3,9},{11,17},{19,25},{27,33},{35,41},{43,49},{51,57},{59,65},{67,... | collective-permute-start | bytes 49160 | tf_op jit(solution)/shard_map/ppermute | solution.py:245
  108.8 1.3 collective-permute-start.22
  110.3 1.3 collective-permute-start.24
  111.6 0.7 copy-done.2
  112.3 1.9 %collective-permute-start.25 = (f32[16,256]{1,0:T(8,128)S(1)}, f32[16,256]{1,0:T(8,128)S(1)}, u32[]{:S(2)}, u32[]{:S(2)}) collective-permute-start(f32[16,256]{1,0:T(8,128)S(1)} %shard_map.76), channel_id=1, source_target_pairs={{3,11},{11,19},{19,27},{27,35},{35,43},{43,51},{51,59},{59,67},{67... | collective-permute-start | bytes 49160 | tf_op jit(solution)/shard_map/ppermute | solution.py:245
  114.2 0.9 copy-done.3
  115.2 0.2 shard_map.78
  115.4 0.4 shard_map.79
  115.8 0.7 collective-permute-start.30
  116.5 3.5 %collective-permute-done.25.m3 = f32[16,256]{1,0:T(8,128)S(1)} collective-permute-done((f32[16,256]{1,0:T(8,128)S(1)}, f32[16,256]{1,0:T(8,128)S(1)}, u32[]{:S(2)}, u32[]{:S(2)}) %collective-permute-start.25) | collective-permute-done | bytes 16416 | tf_op jit(solution)/shard_map/ppermute | solution.py:245
  120.0 1.3 collective-permute-start.26
  121.3 0.7 collective-permute-start.31
  122.0 0.7 collective-permute-start.32
  122.7 0.7 collective-permute-start.33
  123.3 1.3 collective-permute-start.34
  124.7 1.9 %shard_map.77 = (f32[8,8,256]{2,1,0:T(8,128)S(1)}, f32[8,8,256]{2,1,0:T(8,128)S(1)}, f32[8,256]{1,0:T(8,128)S(1)}, f32[8,4,256]{2,1,0:T(4,128)}) custom-call(bf16[8,256,256]{2,1,0:T(8,128)(2,1)S(1)} %get-tuple-element.28.r_4_.araw, f32[9,16,256]{2,1,0:T(8,128)S(1)} %get-tuple-element.29.r_5_.drive, f32[256,256]{1,0:T(8,128)S(1)} %get-tuple-element.27.dyn.r_6_, ...), custom_call_target="tpu_custom_call" | custom-call | tf_op jit(solution)/shard_map/pallas_call | solution.py:229
  126.6 4.8 %collective-permute-done.34.s3 = f32[16,256]{1,0:T(8,128)S(1)} collective-permute-done((f32[16,256]{1,0:T(8,128)S(1)}, f32[16,256]{1,0:T(8,128)S(1)}, u32[]{:S(2)}, u32[]{:S(2)}) %collective-permute-start.34) | collective-permute-done | bytes 16416 | tf_op jit(solution)/shard_map/ppermute | solution.py:245
  131.4 2.0 %shard_map.80 = f32[8,4,256]{2,1,0:T(4,128)} custom-call(bf16[8,256,256]{2,1,0:T(8,128)(2,1)S(1)} %copy-done.1, f32[8,8,256]{2,1,0:T(8,128)S(1)} %get-tuple-element.45.xs, f32[8,8,256]{2,1,0:T(8,128)S(1)} %get-tuple-element.46.proj, f32[8,256]{1,0:T(8,128)S(1)} %get-tuple-element.47.mid, f32[528,256]{1,0:T(8,128)S(1)} %collective-permute-done.10.qy_m, ...), custom_call_target="tpu_custom_call" | custom-call | tf_op jit(solution)/shard_map/pallas_call | solution.py:229
  (36 shorter events, 0.5 us)
Async XLA Ops:
  0.6 8.3 %collective-permute-start = (bf16[8,64,256]{2,1,0:T(8,128)(2,1)}, bf16[8,64,256]{2,1,0:T(8,128)(2,1)S(1)}, u32[]{:S(2)}, u32[]{:S(2)}) collective-permute-start(bf16[8,64,256]{2,1,0:T(8,128)(2,1)} %a.1), channel_id=1, source_target_pairs={{0,1},{1,2},{2,3},{3,0},{4,5},{5,6},{6,7},{7,4},{8,9},{9,10},{10,1... | collective-permute-start | bytes 786440 | tf_op jit(solution)/shard_map/ppermute | solution.py:253
  1.2 10.6 %collective-permute-start.8 = (bf16[8,64,256]{2,1,0:T(8,128)(2,1)}, bf16[8,64,256]{2,1,0:T(8,128)(2,1)S(1)}, u32[]{:S(2)}, u32[]{:S(2)}) collective-permute-start(bf16[8,64,256]{2,1,0:T(8,128)(2,1)} %g.1), channel_id=1, source_target_pairs={{0,3},{1,0},{2,1},{3,2},{4,7},{5,4},{6,5},{7,6},{8,11},{9,8},{10,9... | collective-permute-start | bytes 786440 | tf_op jit(solution)/shard_map/ppermute | solution.py:253
  2.7 30.5 %collective-permute-start.1 = (bf16[8,64,256]{2,1,0:T(8,128)(2,1)}, bf16[8,64,256]{2,1,0:T(8,128)(2,1)S(1)}, u32[]{:S(2)}, u32[]{:S(2)}) collective-permute-start(bf16[8,64,256]{2,1,0:T(8,128)(2,1)} %a.1), channel_id=1, source_target_pairs={{0,3},{1,0},{2,1},{3,2},{4,7},{5,4},{6,5},{7,6},{8,11},{9,8},{10,9... | collective-permute-start | bytes 786440 | tf_op jit(solution)/shard_map/ppermute | solution.py:253
  9.0 24.2 %collective-permute-start.2 = (bf16[8,64,256]{2,1,0:T(8,128)(2,1)S(1)}, bf16[8,64,256]{2,1,0:T(8,128)(2,1)S(1)}, u32[]{:S(2)}, u32[]{:S(2)}) collective-permute-start(bf16[8,64,256]{2,1,0:T(8,128)(2,1)S(1)} %collective-permute-done.a1), channel_id=1, source_target_pairs={{0,1},{1,2},{2,3},{3,0},{4,5},{5,6},{6,7},{7,4},{8,9},{9,10},{10,1... | collective-permute-start | bytes 786440 | tf_op jit(solution)/shard_map/ppermute | solution.py:253
  10.7 24.7 %collective-permute-start.7 = (bf16[8,64,256]{2,1,0:T(8,128)(2,1)}, bf16[8,64,256]{2,1,0:T(8,128)(2,1)S(1)}, u32[]{:S(2)}, u32[]{:S(2)}) collective-permute-start(bf16[8,64,256]{2,1,0:T(8,128)(2,1)} %g.1), channel_id=1, source_target_pairs={{0,1},{1,2},{2,3},{3,0},{4,5},{5,6},{6,7},{7,4},{8,9},{9,10},{10,1... | collective-permute-start | bytes 786440 | tf_op jit(solution)/shard_map/ppermute | solution.py:253
  11.8 23.6 %collective-permute-start.9 = (bf16[8,64,256]{2,1,0:T(8,128)(2,1)S(1)}, bf16[8,64,256]{2,1,0:T(8,128)(2,1)S(1)}, u32[]{:S(2)}, u32[]{:S(2)}) collective-permute-start(bf16[8,64,256]{2,1,0:T(8,128)(2,1)S(1)} %collective-permute-done.8.g2), channel_id=1, source_target_pairs={{0,3},{1,0},{2,1},{3,2},{4,7},{5,4},{6,5},{7,6},{8,11},{9,8},{10,9... | collective-permute-start | bytes 786440 | tf_op jit(solution)/shard_map/ppermute | solution.py:253
  13.5 9.1 %collective-permute-start.3 = (f32[9,4,256]{2,1,0:T(4,128)S(1)}, f32[9,4,256]{2,1,0:T(4,128)S(1)}, u32[]{:S(2)}, u32[]{:S(2)}) collective-permute-start(f32[9,4,256]{2,1,0:T(4,128)S(1)} %pad_maximum_fusion.d0), channel_id=1, source_target_pairs={{0,1},{1,2},{2,3},{3,0},{4,5},{5,6},{6,7},{7,4},{8,9},{9,10},{10,1... | collective-permute-start | bytes 110600 | tf_op jit(solution)/shard_map/ppermute | solution.py:253
  22.6 5.2 %collective-permute-start.4 = (f32[9,4,256]{2,1,0:T(4,128)S(1)}, f32[9,4,256]{2,1,0:T(4,128)S(1)}, u32[]{:S(2)}, u32[]{:S(2)}) collective-permute-start(f32[9,4,256]{2,1,0:T(4,128)S(1)} %pad_maximum_fusion.d0), channel_id=1, source_target_pairs={{0,3},{1,0},{2,1},{3,2},{4,7},{5,4},{6,5},{7,6},{8,11},{9,8},{10,9... | collective-permute-start | bytes 110600 | tf_op jit(solution)/shard_map/ppermute | solution.py:253
  27.7 5.5 %collective-permute-start.5 = (f32[9,4,256]{2,1,0:T(4,128)S(1)}, f32[9,4,256]{2,1,0:T(4,128)S(1)}, u32[]{:S(2)}, u32[]{:S(2)}) collective-permute-start(f32[9,4,256]{2,1,0:T(4,128)S(1)} %pad_maximum_fusion.d0), channel_id=1, source_target_pairs={{0,2},{1,3},{2,0},{3,1},{4,6},{5,7},{6,4},{7,5},{8,10},{9,11},{10,... | collective-permute-start | bytes 110600 | tf_op jit(solution)/shard_map/ppermute | solution.py:253
  28.6 0.9 copy-start.4
  29.5 0.9 copy-start.5
  30.5 0.9 copy-start.6
  37.2 31.7 %copy-start = (bf16[8,256,256]{2,1,0:T(8,128)(2,1)}, bf16[8,256,256]{2,1,0:T(8,128)(2,1)S(1)}, u32[]{:S(2)}) copy-start(bf16[8,256,256]{2,1,0:T(8,128)(2,1)S(1)} %get-tuple-element.44.graw) | copy-start | bytes 3145732
  37.2 2.4 %collective-permute-start.10 = (f32[528,256]{1,0:T(8,128)S(1)}, f32[528,256]{1,0:T(8,128)S(1)}, u32[]{:S(2)}, u32[]{:S(2)}) collective-permute-start(f32[528,256]{1,0:T(8,128)S(1)} %get-tuple-element.34.qy), channel_id=1, source_target_pairs={{0,4},{4,0},{8,12},{12,8},{16,20},{20,16},{24,28},{28,24},{32,36},... | collective-permute-start | bytes 1622024 | tf_op jit(solution)/shard_map/ppermute | solution.py:250
  37.3 2.3 %collective-permute-start.6 = (f32[272,256]{1,0:T(8,128)S(1)}, f32[272,256]{1,0:T(8,128)S(1)}, u32[]{:S(2)}, u32[]{:S(2)}) collective-permute-start(f32[272,256]{1,0:T(8,128)S(1)} %get-tuple-element.30.x.x_b), channel_id=1, source_target_pairs={{0,4},{4,0},{8,12},{12,8},{16,20},{20,16},{24,28},{28,24},{32,36},... | collective-permute-start | bytes 835592 | tf_op jit(solution)/shard_map/ppermute | solution.py:250
  40.7 12.5 %collective-permute-start.11 = (f32[272,256]{1,0:T(8,128)S(1)}, f32[272,256]{1,0:T(8,128)S(1)}, u32[]{:S(2)}, u32[]{:S(2)}) collective-permute-start(f32[272,256]{1,0:T(8,128)S(1)} %get-tuple-element.35.r_0_), channel_id=1, source_target_pairs={{8,0},{16,8},{24,16},{32,24},{40,32},{48,40},{56,48},{64,56},{72,6... | collective-permute-start | bytes 835592 | tf_op jit(solution)/shard_map/ppermute | solution.py:245
  54.1 13.9 %collective-permute-start.12 = (f32[272,256]{1,0:T(8,128)S(1)}, f32[272,256]{1,0:T(8,128)S(1)}, u32[]{:S(2)}, u32[]{:S(2)}) collective-permute-start(f32[272,256]{1,0:T(8,128)S(1)} %get-tuple-element.38.r_0_), channel_id=1, source_target_pairs={{16,0},{24,8},{32,16},{40,24},{48,32},{56,40},{64,48},{72,56},{80,... | collective-permute-start | bytes 835592 | tf_op jit(solution)/shard_map/ppermute | solution.py:245
  56.0 12.0 %collective-permute-start.13 = (f32[272,256]{1,0:T(8,128)S(1)}, f32[272,256]{1,0:T(8,128)S(1)}, u32[]{:S(2)}, u32[]{:S(2)}) collective-permute-start(f32[272,256]{1,0:T(8,128)S(1)} %get-tuple-element.38.r_0_), channel_id=1, source_target_pairs={{0,1},{8,9},{16,17},{24,25},{32,33},{40,41},{48,49},{56,57},{64,65... | collective-permute-start | bytes 835592 | tf_op jit(solution)/shard_map/ppermute | solution.py:245
  56.7 11.3 %collective-permute-start.14 = (f32[272,256]{1,0:T(8,128)S(1)}, f32[272,256]{1,0:T(8,128)S(1)}, u32[]{:S(2)}, u32[]{:S(2)}) collective-permute-start(f32[272,256]{1,0:T(8,128)S(1)} %get-tuple-element.38.r_0_), channel_id=1, source_target_pairs={{2,1},{10,9},{18,17},{26,25},{34,33},{42,41},{50,49},{58,57},{66,6... | collective-permute-start | bytes 835592 | tf_op jit(solution)/shard_map/ppermute | solution.py:245
  68.9 15.7 %collective-permute-start.15 = (f32[272,256]{1,0:T(8,128)S(1)}, f32[272,256]{1,0:T(8,128)S(1)}, u32[]{:S(2)}, u32[]{:S(2)}) collective-permute-start(f32[272,256]{1,0:T(8,128)S(1)} %get-tuple-element.39.r_0_), channel_id=1, source_target_pairs={{32,0},{40,8},{48,16},{56,24},{64,32},{72,40},{80,48},{88,56},{96,... | collective-permute-start | bytes 835592 | tf_op jit(solution)/shard_map/ppermute | solution.py:245
  74.7 9.9 %collective-permute-start.16 = (f32[272,256]{1,0:T(8,128)S(1)}, f32[272,256]{1,0:T(8,128)S(1)}, u32[]{:S(2)}, u32[]{:S(2)}) collective-permute-start(f32[272,256]{1,0:T(8,128)S(1)} %get-tuple-element.39.r_0_), channel_id=1, source_target_pairs={{0,1},{8,9},{16,17},{24,25},{32,33},{40,41},{48,49},{56,57},{64,65... | collective-permute-start | bytes 835592 | tf_op jit(solution)/shard_map/ppermute | solution.py:245
  75.4 9.2 %collective-permute-start.17 = (f32[272,256]{1,0:T(8,128)S(1)}, f32[272,256]{1,0:T(8,128)S(1)}, u32[]{:S(2)}, u32[]{:S(2)}) collective-permute-start(f32[272,256]{1,0:T(8,128)S(1)} %get-tuple-element.39.r_0_), channel_id=1, source_target_pairs={{2,1},{10,9},{18,17},{26,25},{34,33},{42,41},{50,49},{58,57},{66,6... | collective-permute-start | bytes 835592 | tf_op jit(solution)/shard_map/ppermute | solution.py:245
  85.5 8.4 %collective-permute-start.18 = (f32[272,256]{1,0:T(8,128)S(1)}, f32[272,256]{1,0:T(8,128)S(1)}, u32[]{:S(2)}, u32[]{:S(2)}) collective-permute-start(f32[272,256]{1,0:T(8,128)S(1)} %get-tuple-element.40.r_0_), channel_id=1, source_target_pairs={{64,0},{72,8},{80,16},{88,24},{96,32},{104,40},{112,48},{120,56},{... | collective-permute-start | bytes 835592 | tf_op jit(solution)/shard_map/ppermute | solution.py:245
  86.8 7.1 %collective-permute-start.19 = (f32[272,256]{1,0:T(8,128)S(1)}, f32[272,256]{1,0:T(8,128)S(1)}, u32[]{:S(2)}, u32[]{:S(2)}) collective-permute-start(f32[272,256]{1,0:T(8,128)S(1)} %get-tuple-element.40.r_0_), channel_id=1, source_target_pairs={{0,1},{8,9},{16,17},{24,25},{32,33},{40,41},{48,49},{56,57},{64,65... | collective-permute-start | bytes 835592 | tf_op jit(solution)/shard_map/ppermute | solution.py:245
  87.4 6.5 %collective-permute-start.20 = (f32[272,256]{1,0:T(8,128)S(1)}, f32[272,256]{1,0:T(8,128)S(1)}, u32[]{:S(2)}, u32[]{:S(2)}) collective-permute-start(f32[272,256]{1,0:T(8,128)S(1)} %get-tuple-element.40.r_0_), channel_id=1, source_target_pairs={{2,1},{10,9},{18,17},{26,25},{34,33},{42,41},{50,49},{58,57},{66,6... | collective-permute-start | bytes 835592 | tf_op jit(solution)/shard_map/ppermute | solution.py:245
  94.2 17.4 %collective-permute-start.27 = (f32[272,256]{1,0:T(8,128)S(1)}, f32[272,256]{1,0:T(8,128)S(1)}, u32[]{:S(2)}, u32[]{:S(2)}) collective-permute-start(f32[272,256]{1,0:T(8,128)S(1)} %get-tuple-element.41.own), channel_id=1, source_target_pairs={{0,1},{8,9},{16,17},{24,25},{32,33},{40,41},{48,49},{56,57},{64,65... | collective-permute-start | bytes 835592 | tf_op jit(solution)/shard_map/ppermute | solution.py:245
  94.9 20.5 %collective-permute-start.28 = (f32[272,256]{1,0:T(8,128)S(1)}, f32[272,256]{1,0:T(8,128)S(1)}, u32[]{:S(2)}, u32[]{:S(2)}) collective-permute-start(f32[272,256]{1,0:T(8,128)S(1)} %get-tuple-element.41.own), channel_id=1, source_target_pairs={{2,1},{10,9},{18,17},{26,25},{34,33},{42,41},{50,49},{58,57},{66,6... | collective-permute-start | bytes 835592 | tf_op jit(solution)/shard_map/ppermute | solution.py:245
  95.6 19.8 %collective-permute-start.29 = (f32[272,256]{1,0:T(8,128)S(1)}, f32[272,256]{1,0:T(8,128)S(1)}, u32[]{:S(2)}, u32[]{:S(2)}) collective-permute-start(f32[272,256]{1,0:T(8,128)S(1)} %get-tuple-element.41.own), channel_id=1, source_target_pairs={{129,1},{137,9},{145,17},{153,25},{161,33},{169,41},{177,49},{185,... | collective-permute-start | bytes 835592 | tf_op jit(solution)/shard_map/ppermute | solution.py:245
  96.3 7.1 %collective-permute-start.21 = (f32[16,256]{1,0:T(8,128)S(1)}, f32[16,256]{1,0:T(8,128)S(1)}, u32[]{:S(2)}, u32[]{:S(2)}) collective-permute-start(f32[16,256]{1,0:T(8,128)S(1)} %get-tuple-element.42), channel_id=1, source_target_pairs={{3,131},{11,139},{19,147},{27,155},{35,163},{43,171},{51,179},{59,... | collective-permute-start | bytes 49160 | tf_op jit(solution)/shard_map/ppermute | solution.py:245
  103.5 6.7 %collective-permute-start.23 = (f32[16,256]{1,0:T(8,128)S(1)}, f32[16,256]{1,0:T(8,128)S(1)}, u32[]{:S(2)}, u32[]{:S(2)}) collective-permute-start(f32[16,256]{1,0:T(8,128)S(1)} %shard_map.76), channel_id=1, source_target_pairs={{3,9},{11,17},{19,25},{27,33},{35,41},{43,49},{51,57},{59,65},{67,... | collective-permute-start | bytes 49160 | tf_op jit(solution)/shard_map/ppermute | solution.py:245
  108.8 7.6 %collective-permute-start.22 = (f32[16,256]{1,0:T(8,128)S(1)}, f32[16,256]{1,0:T(8,128)S(1)}, u32[]{:S(2)}, u32[]{:S(2)}) collective-permute-start(f32[16,256]{1,0:T(8,128)S(1)} %shard_map.76), channel_id=1, source_target_pairs={{3,8},{11,16},{19,24},{27,32},{35,40},{43,48},{51,56},{59,64},{67,... | collective-permute-start | bytes 49160 | tf_op jit(solution)/shard_map/ppermute | solution.py:245
  110.3 6.2 %collective-permute-start.24 = (f32[16,256]{1,0:T(8,128)S(1)}, f32[16,256]{1,0:T(8,128)S(1)}, u32[]{:S(2)}, u32[]{:S(2)}) collective-permute-start(f32[16,256]{1,0:T(8,128)S(1)} %shard_map.76), channel_id=1, source_target_pairs={{3,10},{11,18},{19,26},{27,34},{35,42},{43,50},{51,58},{59,66},{67... | collective-permute-start | bytes 49160 | tf_op jit(solution)/shard_map/ppermute | solution.py:245
  111.6 0.7 copy-start.2
  112.3 7.7 %collective-permute-start.25 = (f32[16,256]{1,0:T(8,128)S(1)}, f32[16,256]{1,0:T(8,128)S(1)}, u32[]{:S(2)}, u32[]{:S(2)}) collective-permute-start(f32[16,256]{1,0:T(8,128)S(1)} %shard_map.76), channel_id=1, source_target_pairs={{3,11},{11,19},{19,27},{27,35},{35,43},{43,51},{51,59},{59,67},{67... | collective-permute-start | bytes 49160 | tf_op jit(solution)/shard_map/ppermute | solution.py:245
  114.2 1.0 copy-start.3
  115.2 16.2 %copy-start.1 = (bf16[8,256,256]{2,1,0:T(8,128)(2,1)S(1)}, bf16[8,256,256]{2,1,0:T(8,128)(2,1)}, u32[]{:S(2)}) copy-start(bf16[8,256,256]{2,1,0:T(8,128)(2,1)} %copy-done) | copy-start | bytes 3145732
  115.8 5.5 %collective-permute-start.30 = (f32[16,256]{1,0:T(8,128)S(1)}, f32[16,256]{1,0:T(8,128)S(1)}, u32[]{:S(2)}, u32[]{:S(2)}) collective-permute-start(f32[16,256]{1,0:T(8,128)S(1)} %shard_map.79), channel_id=1, source_target_pairs={{1,5},{9,13},{17,21},{25,29},{33,37},{41,45},{49,53},{57,61},{65,6... | collective-permute-start | bytes 49160 | tf_op jit(solution)/shard_map/ppermute | solution.py:245
  120.0 4.6 %collective-permute-start.26 = (f32[16,256]{1,0:T(8,128)S(1)}, f32[16,256]{1,0:T(8,128)S(1)}, u32[]{:S(2)}, u32[]{:S(2)}) collective-permute-start(f32[16,256]{1,0:T(8,128)S(1)} %add_add_fusion), channel_id=1, source_target_pairs={{0,4},{1,5},{2,6},{3,7},{8,12},{9,13},{10,14},{11,15},{16,20},{17,... | collective-permute-start | bytes 49160 | tf_op jit(solution)/shard_map/ppermute | solution.py:245
  121.3 5.2 %collective-permute-start.31 = (f32[16,256]{1,0:T(8,128)S(1)}, f32[16,256]{1,0:T(8,128)S(1)}, u32[]{:S(2)}, u32[]{:S(2)}) collective-permute-start(f32[16,256]{1,0:T(8,128)S(1)} %broadcast_select_fusion), channel_id=1, source_target_pairs={{9,0},{13,4},{17,8},{21,12},{25,16},{29,20},{33,24},{37,28},{41,32... | collective-permute-start | bytes 49160 | tf_op jit(solution)/shard_map/ppermute | solution.py:245
  122.0 4.5 %collective-permute-start.32 = (f32[16,256]{1,0:T(8,128)S(1)}, f32[16,256]{1,0:T(8,128)S(1)}, u32[]{:S(2)}, u32[]{:S(2)}) collective-permute-start(f32[16,256]{1,0:T(8,128)S(1)} %broadcast_select_fusion), channel_id=1, source_target_pairs={{9,2},{13,6},{17,10},{21,14},{25,18},{29,22},{33,26},{37,30},{41,3... | collective-permute-start | bytes 49160 | tf_op jit(solution)/shard_map/ppermute | solution.py:245
  122.7 3.9 %collective-permute-start.33 = (f32[16,256]{1,0:T(8,128)S(1)}, f32[16,256]{1,0:T(8,128)S(1)}, u32[]{:S(2)}, u32[]{:S(2)}) collective-permute-start(f32[16,256]{1,0:T(8,128)S(1)} %broadcast_select_fusion), channel_id=1, source_target_pairs={{9,1},{13,5},{17,9},{21,13},{25,17},{29,21},{33,25},{37,29},{41,33... | collective-permute-start | bytes 49160 | tf_op jit(solution)/shard_map/ppermute | solution.py:245
  123.3 8.0 %collective-permute-start.34 = (f32[16,256]{1,0:T(8,128)S(1)}, f32[16,256]{1,0:T(8,128)S(1)}, u32[]{:S(2)}, u32[]{:S(2)}) collective-permute-start(f32[16,256]{1,0:T(8,128)S(1)} %broadcast_select_fusion), channel_id=1, source_target_pairs={{9,3},{13,7},{17,11},{21,15},{25,19},{29,23},{33,27},{37,31},{41,3... | collective-permute-start | bytes 49160 | tf_op jit(solution)/shard_map/ppermute | solution.py:245

commit v3 on v2

--- a/solution.py
+++ b/solution.py
@@ -181,11 +181,10 @@
     return jnp.where(low, value[:GRP], value[GRP:])
 
 
-def mean_sweep_kernel(araw, drive, dyn, x_b, x_bm, m0, m1, m2, m3, m4, xs, proj, mid, filt):
+def mean_sweep(begin, araw, drive, dyn, x_b, x_bm, xs, proj, mid, filt):
     tm, core, col = place()
     steps = araw.shape[0]
     low = col < 2
-    begin = group((m0[...] + m1[...]) + (m2[...] + m3[...]) + m4[...], low)
 
     @pl.when(core == 0)
     def _():
@@ -204,6 +203,33 @@
         xs[t] = x
         filt[t] = jnp.where(upper, x[per:], x[:per])
     proj[...] = mul(xs[...].reshape(steps * GRP, D), dyn[...]).reshape(steps, GRP, D)
+
+
+def early():
+    _, core, col = place()
+    return jnp.logical_and(col == 1, core == 0)
+
+
+def early_sweep_kernel(araw, drive, dyn, x_b, x_bm, m1, xs, proj, mid, filt):
+    @pl.when(early())
+    def _():
+        begin = group(m1[...], True)
+        mean_sweep(begin, araw, drive, dyn, x_b, x_bm, xs, proj, mid, filt)
+
+
+def mean_sweep_kernel(
+    araw, drive, dyn, x_b, x_bm, m0, m2, m3, m4, m5, xs0, proj0, mid0, filt0, xs, proj, mid, filt
+):
+    @pl.when(early())
+    def _():
+        for out, done in ((xs, xs0), (proj, proj0), (mid, mid0), (filt, filt0)):
+            out[...] = done[...]
+
+    @pl.when(jnp.logical_not(early()))
+    def _():
+        total = (m0[...] + m2[...]) + (m3[...] + m4[...]) + m5[...]
+        begin = group(total, lax.axis_index("col") < 2)
+        mean_sweep(begin, araw, drive, dyn, x_b, x_bm, xs, proj, mid, filt)
 
 
 def smooth_sweep_kernel(graw, xs, proj, mid, qy_m, s0, s1, s2, s3, smooth):
@@ -327,21 +353,27 @@
     xrow = hop(own, [(SUF_X, SUF_Y)])
     qrow = hop(own, [(SUF_Q, SUF_Y)])
     (leaving,) = call(mean_kernel, [vector], own, got_v)
-    means = [hop(leaving, [(PRE_X, (c, 0))], 1) for c in range(4)]
-    begin = means[1]
-    total = (means[0] + means[1]) + (means[2] + means[3])
-    means.append(hop(total, [((c, 0), (c, 1)) for c in range(4)]))
+    begin = hop(leaving, [(PRE_X, SUF_Y)], 1)
+    ahead = hop(leaving, [(PRE_X, PRE_X)], 1)
+    means = {c: hop(ahead, [(PRE_X, (c, 0))]) for c in (0, 2)}
+    means[3] = ahead
+    total = means[0] + (means[2] + means[3])
+    x_pass = hop(total, [((c, 0), (c, 1)) for c in (0, 2, 3)])
+    x_one = hop(begin, [((1, 0), (1, 1))])
+    part = ((steps, GRP, D), f32)
+    result = ((steps, drive.shape[1], D), f32)
+    swept = [part, part, ((GRP, D), f32), result]
+    held = (araw, drive16, dyn, x_b, x_bm)
+    sweep = call(early_sweep_kernel, swept, *held, begin)
     first = lax.rem(lax.axis_index("tm"), 2) == 0
     near, mid = call(near_kernel, [vector, vector], own, xrow, begin)
     (s_one,) = call(top_kernel, [vector], near, mid, qrow, got)
     s_two = jnp.where(first, s_one, hop(s_one, [(SUF_Y, (1, 1))]))
-    s_in = [hop(s_two, across(c), -1) for c in (0, 2, 1, 3)]
-    part = ((steps, GRP, D), f32)
-    result = ((steps, drive.shape[1], D), f32)
+    s_in = [hop(s_two, across(c), -1) for c in (0, 2, 3, 1)]
     xs8, proj8, mid8, filtered = call(
         mean_sweep_kernel,
-        [part, part, ((GRP, D), f32), result],
-        araw, drive16, dyn, x_b, x_bm, *means,
+        swept,
+        *held, means[0], means[2], means[3], x_pass, x_one, *sweep,
     )
     (smoothed,) = call(smooth_sweep_kernel, [result], graw, xs8, proj8, mid8, qy_bm, *s_in)
     return filtered, smoothed

time: 134 us -> 133 us (level)
  the two profiles are of different devices: /device:TPU:30 before, /device:TPU:26 now
where the time goes in v3:
time: 133 us
  starting transfers between devices  58.9 us (44%)
  waiting for transfers between devices  53.8 us (40%)
  Pallas kernels  15.3 us (12%)
  local copies, waits for them, and re-layouts  2.86 us (2%)
    ppermute x25, starting transfers between devices, send(): lax.ppermute(x, ('tm', 'col'), [(a * cols + b, c * cols + d) for (a, b),...  44 us
    ppermute x25, waiting for transfers between devices, send(): lax.ppermute(x, ('tm', 'col'), [(a * cols + b, c * cols + d) for (a, b),...  37.8 us
    pallas_call x14, Pallas kernels, call(): pl.pallas_call(kernel, out_shape=tuple((jax.ShapeDtypeStruct(s, d) for s,...  15.3 us
    ppermute x9, starting transfers between devices, turn(): return lax.ppermute(x, 'col', [(c, (c + by) % 4) for c in range(4)])  14.3 us
    ppermute x9, waiting for transfers between devices, turn(): return lax.ppermute(x, 'col', [(c, (c + by) % 4) for c in range(4)])  14.2 us
    unnamed x10, local copies, waits for them, and re-layouts  2.86 us
  transfers between devices with their start and end apart: 36, of which 15 were waited for; matrix products, arithmetic and copies ran while one was open for 1% of the time, Pallas kernels for 5%

profile of v3, /device:TPU:26, one launch (start us, length us, event | category | flops | bytes accessed | tf_op | source)
XLA Modules:
  0.0 132.6 jit_solution(12060382540911724853)
XLA Ops:
  0.6 1.6 %collective-permute-start = (bf16[8,64,256]{2,1,0:T(8,128)(2,1)}, bf16[8,64,256]{2,1,0:T(8,128)(2,1)S(1)}, u32[]{:S(2)}, u32[]{:S(2)}) collective-permute-start(bf16[8,64,256]{2,1,0:T(8,128)(2,1)} %a.1), channel_id=1, source_target_pairs={{0,1},{1,2},{2,3},{3,0},{4,5},{5,6},{6,7},{7,4},{8,9},{9,10},{10,1... | collective-permute-start | bytes 786440 | tf_op jit(solution)/shard_map/ppermute | solution.py:279
  2.2 0.5 collective-permute-start.8
  2.7 1.7 %collective-permute-start.1 = (bf16[8,64,256]{2,1,0:T(8,128)(2,1)}, bf16[8,64,256]{2,1,0:T(8,128)(2,1)S(1)}, u32[]{:S(2)}, u32[]{:S(2)}) collective-permute-start(bf16[8,64,256]{2,1,0:T(8,128)(2,1)} %a.1), channel_id=1, source_target_pairs={{0,3},{1,0},{2,1},{3,2},{4,7},{5,4},{6,5},{7,6},{8,11},{9,8},{10,9... | collective-permute-start | bytes 786440 | tf_op jit(solution)/shard_map/ppermute | solution.py:279
  4.5 4.5 %collective-permute-done.a1 = bf16[8,64,256]{2,1,0:T(8,128)(2,1)S(1)} collective-permute-done((bf16[8,64,256]{2,1,0:T(8,128)(2,1)}, bf16[8,64,256]{2,1,0:T(8,128)(2,1)S(1)}, u32[]{:S(2)}, u32[]{:S(2)}) %collective-permute-start) | collective-permute-done | bytes 262176 | tf_op jit(solution)/shard_map/ppermute | solution.py:279
  9.0 1.5 %collective-permute-start.2 = (bf16[8,64,256]{2,1,0:T(8,128)(2,1)S(1)}, bf16[8,64,256]{2,1,0:T(8,128)(2,1)S(1)}, u32[]{:S(2)}, u32[]{:S(2)}) collective-permute-start(bf16[8,64,256]{2,1,0:T(8,128)(2,1)S(1)} %collective-permute-done.a1), channel_id=1, source_target_pairs={{0,1},{1,2},{2,3},{3,0},{4,5},{5,6},{6,7},{7,4},{8,9},{9,10},{10,1... | collective-permute-start | bytes 786440 | tf_op jit(solution)/shard_map/ppermute | solution.py:279
  10.5 1.2 collective-permute-start.7
  11.7 0.8 collective-permute-start.9
  12.5 0.8 pad_maximum_fusion.d0
  13.3 1.3 collective-permute-start.3
  14.5 8.0 %collective-permute-done.3.d1 = f32[9,4,256]{2,1,0:T(4,128)S(1)} collective-permute-done((f32[9,4,256]{2,1,0:T(4,128)S(1)}, f32[9,4,256]{2,1,0:T(4,128)S(1)}, u32[]{:S(2)}, u32[]{:S(2)}) %collective-permute-start.3) | collective-permute-done | bytes 36896 | tf_op jit(solution)/shard_map/ppermute | solution.py:279
  22.6 3.0 %collective-permute-start.4 = (f32[9,4,256]{2,1,0:T(4,128)S(1)}, f32[9,4,256]{2,1,0:T(4,128)S(1)}, u32[]{:S(2)}, u32[]{:S(2)}) collective-permute-start(f32[9,4,256]{2,1,0:T(4,128)S(1)} %pad_maximum_fusion.d0), channel_id=1, source_target_pairs={{0,3},{1,0},{2,1},{3,2},{4,7},{5,4},{6,5},{7,6},{8,11},{9,8},{10,9... | collective-permute-start | bytes 110600 | tf_op jit(solution)/shard_map/ppermute | solution.py:279
  25.5 1.6 %collective-permute-done.4.d2 = f32[9,4,256]{2,1,0:T(4,128)S(1)} collective-permute-done((f32[9,4,256]{2,1,0:T(4,128)S(1)}, f32[9,4,256]{2,1,0:T(4,128)S(1)}, u32[]{:S(2)}, u32[]{:S(2)}) %collective-permute-start.4) | collective-permute-done | bytes 36896 | tf_op jit(solution)/shard_map/ppermute | solution.py:279
  27.2 2.7 %collective-permute-start.5 = (f32[9,4,256]{2,1,0:T(4,128)S(1)}, f32[9,4,256]{2,1,0:T(4,128)S(1)}, u32[]{:S(2)}, u32[]{:S(2)}) collective-permute-start(f32[9,4,256]{2,1,0:T(4,128)S(1)} %pad_maximum_fusion.d0), channel_id=1, source_target_pairs={{0,2},{1,3},{2,0},{3,1},{4,6},{5,7},{6,4},{7,5},{8,10},{9,11},{10,... | collective-permute-start | bytes 110600 | tf_op jit(solution)/shard_map/ppermute | solution.py:279
  29.9 0.9 copy-done.2
  30.8 0.9 copy-done.3
  31.8 0.9 copy-done.4
  32.8 2.1 %shard_map.69 = (bf16[8,256,256]{2,1,0:T(8,128)(2,1)S(1)}, f32[9,16,256]{2,1,0:T(8,128)S(1)}, f32[8,272,256]{2,1,0:T(8,128)S(1)}, f32[8,272,256]{2,1,0:T(8,128)S(1)}, f32[272,256]{1,0:T(8,128)S(1)}) custom-call(bf16[8,64,256]{2,1,0:T(8,128)(2,1)S(1)} %get-tuple-element.30.a0, bf16[8,64,256]{2,1,0:T(8,128)(2,1)S(1)} %collective-permute-done.a1, ...), custom_call_target="tpu_custom_call" | custom-call | tf_op jit(solution)/shard_map/pallas_call | solution.py:255
  35.0 1.8 %shard_map.70 = (bf16[8,256,256]{2,1,0:T(8,128)(2,1)S(1)}, f32[528,256]{1,0:T(8,128)S(1)}) custom-call(bf16[8,64,256]{2,1,0:T(8,128)(2,1)S(1)} %get-tuple-element.35.g0, bf16[8,64,256]{2,1,0:T(8,128)(2,1)S(1)} %collective-permute-done.7.g1, bf16[8,64,256]{2,1,0:T(8,128)(2,1)S(1)} %collective-permute-done.8.g2, ...), custom_call_target="tpu_custom_call" | custom-call | tf_op jit(solution)/shard_map/pallas_call | solution.py:255
  36.9 0.5 collective-permute-start.6
  37.4 1.8 %collective-permute-done.6.x_m.x_bm = f32[272,256]{1,0:T(8,128)S(1)} collective-permute-done((f32[272,256]{1,0:T(8,128)S(1)}, f32[272,256]{1,0:T(8,128)S(1)}, u32[]{:S(2)}, u32[]{:S(2)}) %collective-permute-start.6) | collective-permute-done | bytes 278560 | tf_op jit(solution)/shard_map/ppermute | solution.py:276
  39.2 1.1 shard_map.71
  40.3 7.9 %collective-permute-start.11 = (f32[272,256]{1,0:T(8,128)S(1)}, f32[272,256]{1,0:T(8,128)S(1)}, u32[]{:S(2)}, u32[]{:S(2)}) collective-permute-start(f32[272,256]{1,0:T(8,128)S(1)} %get-tuple-element.39.r_0_), channel_id=1, source_target_pairs={{8,0},{16,8},{24,16},{32,24},{40,32},{48,40},{56,48},{64,56},{72,6... | collective-permute-start | bytes 835592 | tf_op jit(solution)/shard_map/ppermute | solution.py:271
  48.2 4.0 %collective-permute-done.11.r_1_ = f32[272,256]{1,0:T(8,128)S(1)} collective-permute-done((f32[272,256]{1,0:T(8,128)S(1)}, f32[272,256]{1,0:T(8,128)S(1)}, u32[]{:S(2)}, u32[]{:S(2)}) %collective-permute-start.11) | collective-permute-done | bytes 278560 | tf_op jit(solution)/shard_map/ppermute | solution.py:271
  52.3 1.2 shard_map.72
  53.5 4.8 %collective-permute-start.12 = (f32[272,256]{1,0:T(8,128)S(1)}, f32[272,256]{1,0:T(8,128)S(1)}, u32[]{:S(2)}, u32[]{:S(2)}) collective-permute-start(f32[272,256]{1,0:T(8,128)S(1)} %get-tuple-element.42.r_0_), channel_id=1, source_target_pairs={{16,0},{24,8},{32,16},{40,24},{48,32},{56,40},{64,48},{72,56},{80,... | collective-permute-start | bytes 835592 | tf_op jit(solution)/shard_map/ppermute | solution.py:271
  58.4 1.3 collective-permute-start.13
  59.7 1.3 collective-permute-start.14
  61.0 4.4 %collective-permute-done.12.r_1_ = f32[272,256]{1,0:T(8,128)S(1)} collective-permute-done((f32[272,256]{1,0:T(8,128)S(1)}, f32[272,256]{1,0:T(8,128)S(1)}, u32[]{:S(2)}, u32[]{:S(2)}) %collective-permute-start.12) | collective-permute-done | bytes 278560 | tf_op jit(solution)/shard_map/ppermute | solution.py:271
  65.3 1.5 %collective-permute-done.13.r_2_ = f32[272,256]{1,0:T(8,128)S(1)} collective-permute-done((f32[272,256]{1,0:T(8,128)S(1)}, f32[272,256]{1,0:T(8,128)S(1)}, u32[]{:S(2)}, u32[]{:S(2)}) %collective-permute-start.13) | collective-permute-done | bytes 278560 | tf_op jit(solution)/shard_map/ppermute | solution.py:271
  66.8 1.3 collective-permute-done.14.r_3_
  68.1 1.2 shard_map.73
  69.4 2.8 %collective-permute-start.15 = (f32[272,256]{1,0:T(8,128)S(1)}, f32[272,256]{1,0:T(8,128)S(1)}, u32[]{:S(2)}, u32[]{:S(2)}) collective-permute-start(f32[272,256]{1,0:T(8,128)S(1)} %get-tuple-element.43.r_0_), channel_id=1, source_target_pairs={{32,0},{40,8},{48,16},{56,24},{64,32},{72,40},{80,48},{88,56},{96,... | collective-permute-start | bytes 835592 | tf_op jit(solution)/shard_map/ppermute | solution.py:271
  72.2 1.3 collective-permute-start.16
  73.5 1.3 collective-permute-start.17
  74.8 9.5 %collective-permute-done.15.r_1_ = f32[272,256]{1,0:T(8,128)S(1)} collective-permute-done((f32[272,256]{1,0:T(8,128)S(1)}, f32[272,256]{1,0:T(8,128)S(1)}, u32[]{:S(2)}, u32[]{:S(2)}) %collective-permute-start.15) | collective-permute-done | bytes 278560 | tf_op jit(solution)/shard_map/ppermute | solution.py:271
  84.3 1.2 shard_map.74
  85.6 2.4 %collective-permute-start.18 = (f32[272,256]{1,0:T(8,128)S(1)}, f32[272,256]{1,0:T(8,128)S(1)}, u32[]{:S(2)}, u32[]{:S(2)}) collective-permute-start(f32[272,256]{1,0:T(8,128)S(1)} %get-tuple-element.44.r_0_), channel_id=1, source_target_pairs={{64,0},{72,8},{80,16},{88,24},{96,32},{104,40},{112,48},{120,56},{... | collective-permute-start | bytes 835592 | tf_op jit(solution)/shard_map/ppermute | solution.py:271
  87.9 1.3 collective-permute-start.19
  89.2 1.3 collective-permute-start.20
  90.5 1.4 %collective-permute-done.18.r_1_ = f32[272,256]{1,0:T(8,128)S(1)} collective-permute-done((f32[272,256]{1,0:T(8,128)S(1)}, f32[272,256]{1,0:T(8,128)S(1)}, u32[]{:S(2)}, u32[]{:S(2)}) %collective-permute-start.18) | collective-permute-done | bytes 278560 | tf_op jit(solution)/shard_map/ppermute | solution.py:271
  92.0 4.4 %collective-permute-done.19.r_2_ = f32[272,256]{1,0:T(8,128)S(1)} collective-permute-done((f32[272,256]{1,0:T(8,128)S(1)}, f32[272,256]{1,0:T(8,128)S(1)}, u32[]{:S(2)}, u32[]{:S(2)}) %collective-permute-start.19) | collective-permute-done | bytes 278560 | tf_op jit(solution)/shard_map/ppermute | solution.py:271
  96.4 1.3 collective-permute-done.20.r_3_
  97.7 0.6 shard_map.75
  98.3 1.3 collective-permute-start.28
  99.6 1.3 collective-permute-start.29
  100.9 2.6 %collective-permute-start.30 = (f32[272,256]{1,0:T(8,128)S(1)}, f32[272,256]{1,0:T(8,128)S(1)}, u32[]{:S(2)}, u32[]{:S(2)}) collective-permute-start(f32[272,256]{1,0:T(8,128)S(1)} %get-tuple-element.45.own), channel_id=1, source_target_pairs={{129,1},{137,9},{145,17},{153,25},{161,33},{169,41},{177,49},{185,... | collective-permute-start | bytes 835592 | tf_op jit(solution)/shard_map/ppermute | solution.py:271
  103.5 0.7 collective-permute-start.21
  104.4 0.7 collective-permute-start.22
  105.1 1.3 collective-permute-start.26
  106.4 0.7 collective-permute-start.23
  107.0 8.2 %collective-permute-done.26.m1.begin = f32[16,256]{1,0:T(8,128)S(1)} collective-permute-done((f32[16,256]{1,0:T(8,128)S(1)}, f32[16,256]{1,0:T(8,128)S(1)}, u32[]{:S(2)}, u32[]{:S(2)}) %collective-permute-start.26) | collective-permute-done | bytes 16416 | tf_op jit(solution)/shard_map/ppermute | solution.py:271
  115.2 0.7 collective-permute-start.24
  115.9 1.3 collective-permute-start.27
  117.2 1.2 shard_map.79
  118.8 1.4 %collective-permute-start.31 = (f32[16,256]{1,0:T(8,128)S(1)}, f32[16,256]{1,0:T(8,128)S(1)}, u32[]{:S(2)}, u32[]{:S(2)}) collective-permute-start(f32[16,256]{1,0:T(8,128)S(1)} %shard_map.80), channel_id=1, source_target_pairs={{1,5},{9,13},{17,21},{25,29},{33,37},{41,45},{49,53},{57,61},{65,6... | collective-permute-start | bytes 49160 | tf_op jit(solution)/shard_map/ppermute | solution.py:271
  120.3 0.7 collective-permute-start.25
  121.0 1.3 collective-permute-start.32
  122.3 1.3 collective-permute-start.33
  123.6 1.3 collective-permute-start.34
  124.9 1.9 %collective-permute-start.35 = (f32[16,256]{1,0:T(8,128)S(1)}, f32[16,256]{1,0:T(8,128)S(1)}, u32[]{:S(2)}, u32[]{:S(2)}) collective-permute-start(f32[16,256]{1,0:T(8,128)S(1)} %broadcast_select_fusion), channel_id=1, source_target_pairs={{9,1},{13,5},{17,9},{21,13},{25,17},{29,21},{33,25},{37,29},{41,33... | collective-permute-start | bytes 49160 | tf_op jit(solution)/shard_map/ppermute | solution.py:271
  126.9 1.4 %shard_map.77 = (f32[8,8,256]{2,1,0:T(8,128)S(1)}, f32[8,8,256]{2,1,0:T(8,128)S(1)}, f32[8,256]{1,0:T(8,128)S(1)}, f32[8,4,256]{2,1,0:T(4,128)S(1)}) custom-call(bf16[8,256,256]{2,1,0:T(8,128)(2,1)S(1)} %get-tuple-element.32.r_4_.araw, f32[9,16,256]{2,1,0:T(8,128)S(1)} %get-tuple-element.33.r_5_.drive, f32[256,256]{1,0:T(8,128)S(1)} %get-tuple-element.31.dyn.r_6_, ...), custom_call_target="tpu_custom_call" | custom-call | tf_op jit(solution)/shard_map/pallas_call | solution.py:255
  128.3 0.7 shard_map.78
  129.0 1.6 %collective-permute-done.35.s3 = f32[16,256]{1,0:T(8,128)S(1)} collective-permute-done((f32[16,256]{1,0:T(8,128)S(1)}, f32[16,256]{1,0:T(8,128)S(1)}, u32[]{:S(2)}, u32[]{:S(2)}) %collective-permute-start.35) | collective-permute-done | bytes 16416 | tf_op jit(solution)/shard_map/ppermute | solution.py:271
  130.6 2.0 %shard_map.81 = f32[8,4,256]{2,1,0:T(4,128)} custom-call(bf16[8,256,256]{2,1,0:T(8,128)(2,1)S(1)} %copy-done.1, f32[8,8,256]{2,1,0:T(8,128)S(1)} %get-tuple-element.53.xs, f32[8,8,256]{2,1,0:T(8,128)S(1)} %get-tuple-element.54.proj, f32[8,256]{1,0:T(8,128)S(1)} %get-tuple-element.55.mid, f32[528,256]{1,0:T(8,128)S(1)} %collective-permute-done.10.qy_m, ...), custom_call_target="tpu_custom_call" | custom-call | tf_op jit(solution)/shard_map/pallas_call | solution.py:255
  (35 shorter events, 0.9 us)
Async XLA Ops:
  0.6 8.3 %collective-permute-start = (bf16[8,64,256]{2,1,0:T(8,128)(2,1)}, bf16[8,64,256]{2,1,0:T(8,128)(2,1)S(1)}, u32[]{:S(2)}, u32[]{:S(2)}) collective-permute-start(bf16[8,64,256]{2,1,0:T(8,128)(2,1)} %a.1), channel_id=1, source_target_pairs={{0,1},{1,2},{2,3},{3,0},{4,5},{5,6},{6,7},{7,4},{8,9},{9,10},{10,1... | collective-permute-start | bytes 786440 | tf_op jit(solution)/shard_map/ppermute | solution.py:279
  2.2 9.5 %collective-permute-start.8 = (bf16[8,64,256]{2,1,0:T(8,128)(2,1)}, bf16[8,64,256]{2,1,0:T(8,128)(2,1)S(1)}, u32[]{:S(2)}, u32[]{:S(2)}) collective-permute-start(bf16[8,64,256]{2,1,0:T(8,128)(2,1)} %g.1), channel_id=1, source_target_pairs={{0,3},{1,0},{2,1},{3,2},{4,7},{5,4},{6,5},{7,6},{8,11},{9,8},{10,9... | collective-permute-start | bytes 786440 | tf_op jit(solution)/shard_map/ppermute | solution.py:279
  2.7 30.0 %collective-permute-start.1 = (bf16[8,64,256]{2,1,0:T(8,128)(2,1)}, bf16[8,64,256]{2,1,0:T(8,128)(2,1)S(1)}, u32[]{:S(2)}, u32[]{:S(2)}) collective-permute-start(bf16[8,64,256]{2,1,0:T(8,128)(2,1)} %a.1), channel_id=1, source_target_pairs={{0,3},{1,0},{2,1},{3,2},{4,7},{5,4},{6,5},{7,6},{8,11},{9,8},{10,9... | collective-permute-start | bytes 786440 | tf_op jit(solution)/shard_map/ppermute | solution.py:279
  9.0 23.8 %collective-permute-start.2 = (bf16[8,64,256]{2,1,0:T(8,128)(2,1)S(1)}, bf16[8,64,256]{2,1,0:T(8,128)(2,1)S(1)}, u32[]{:S(2)}, u32[]{:S(2)}) collective-permute-start(bf16[8,64,256]{2,1,0:T(8,128)(2,1)S(1)} %collective-permute-done.a1), channel_id=1, source_target_pairs={{0,1},{1,2},{2,3},{3,0},{4,5},{5,6},{6,7},{7,4},{8,9},{9,10},{10,1... | collective-permute-start | bytes 786440 | tf_op jit(solution)/shard_map/ppermute | solution.py:279
  10.5 24.5 %collective-permute-start.7 = (bf16[8,64,256]{2,1,0:T(8,128)(2,1)}, bf16[8,64,256]{2,1,0:T(8,128)(2,1)S(1)}, u32[]{:S(2)}, u32[]{:S(2)}) collective-permute-start(bf16[8,64,256]{2,1,0:T(8,128)(2,1)} %g.1), channel_id=1, source_target_pairs={{0,1},{1,2},{2,3},{3,0},{4,5},{5,6},{6,7},{7,4},{8,9},{9,10},{10,1... | collective-permute-start | bytes 786440 | tf_op jit(solution)/shard_map/ppermute | solution.py:279
  11.7 23.3 %collective-permute-start.9 = (bf16[8,64,256]{2,1,0:T(8,128)(2,1)S(1)}, bf16[8,64,256]{2,1,0:T(8,128)(2,1)S(1)}, u32[]{:S(2)}, u32[]{:S(2)}) collective-permute-start(bf16[8,64,256]{2,1,0:T(8,128)(2,1)S(1)} %collective-permute-done.8.g2), channel_id=1, source_target_pairs={{0,3},{1,0},{2,1},{3,2},{4,7},{5,4},{6,5},{7,6},{8,11},{9,8},{10,9... | collective-permute-start | bytes 786440 | tf_op jit(solution)/shard_map/ppermute | solution.py:279
  13.3 9.3 %collective-permute-start.3 = (f32[9,4,256]{2,1,0:T(4,128)S(1)}, f32[9,4,256]{2,1,0:T(4,128)S(1)}, u32[]{:S(2)}, u32[]{:S(2)}) collective-permute-start(f32[9,4,256]{2,1,0:T(4,128)S(1)} %pad_maximum_fusion.d0), channel_id=1, source_target_pairs={{0,1},{1,2},{2,3},{3,0},{4,5},{5,6},{6,7},{7,4},{8,9},{9,10},{10,1... | collective-permute-start | bytes 110600 | tf_op jit(solution)/shard_map/ppermute | solution.py:279
  22.6 4.6 %collective-permute-start.4 = (f32[9,4,256]{2,1,0:T(4,128)S(1)}, f32[9,4,256]{2,1,0:T(4,128)S(1)}, u32[]{:S(2)}, u32[]{:S(2)}) collective-permute-start(f32[9,4,256]{2,1,0:T(4,128)S(1)} %pad_maximum_fusion.d0), channel_id=1, source_target_pairs={{0,3},{1,0},{2,1},{3,2},{4,7},{5,4},{6,5},{7,6},{8,11},{9,8},{10,9... | collective-permute-start | bytes 110600 | tf_op jit(solution)/shard_map/ppermute | solution.py:279
  27.2 5.6 %collective-permute-start.5 = (f32[9,4,256]{2,1,0:T(4,128)S(1)}, f32[9,4,256]{2,1,0:T(4,128)S(1)}, u32[]{:S(2)}, u32[]{:S(2)}) collective-permute-start(f32[9,4,256]{2,1,0:T(4,128)S(1)} %pad_maximum_fusion.d0), channel_id=1, source_target_pairs={{0,2},{1,3},{2,0},{3,1},{4,6},{5,7},{6,4},{7,5},{8,10},{9,11},{10,... | collective-permute-start | bytes 110600 | tf_op jit(solution)/shard_map/ppermute | solution.py:279
  29.9 0.9 copy-start.2
  30.8 0.9 copy-start.3
  31.8 0.9 copy-start.4
  36.8 32.6 %copy-start = (bf16[8,256,256]{2,1,0:T(8,128)(2,1)}, bf16[8,256,256]{2,1,0:T(8,128)(2,1)S(1)}, u32[]{:S(2)}) copy-start(bf16[8,256,256]{2,1,0:T(8,128)(2,1)S(1)} %get-tuple-element.52.graw) | copy-start | bytes 3145732
  36.8 2.4 %collective-permute-start.10 = (f32[528,256]{1,0:T(8,128)S(1)}, f32[528,256]{1,0:T(8,128)S(1)}, u32[]{:S(2)}, u32[]{:S(2)}) collective-permute-start(f32[528,256]{1,0:T(8,128)S(1)} %get-tuple-element.38.qy), channel_id=1, source_target_pairs={{0,4},{4,0},{8,12},{12,8},{16,20},{20,16},{24,28},{28,24},{32,36},... | collective-permute-start | bytes 1622024 | tf_op jit(solution)/shard_map/ppermute | solution.py:276
  36.9 2.3 %collective-permute-start.6 = (f32[272,256]{1,0:T(8,128)S(1)}, f32[272,256]{1,0:T(8,128)S(1)}, u32[]{:S(2)}, u32[]{:S(2)}) collective-permute-start(f32[272,256]{1,0:T(8,128)S(1)} %get-tuple-element.34.x.x_b), channel_id=1, source_target_pairs={{0,4},{4,0},{8,12},{12,8},{16,20},{20,16},{24,28},{28,24},{32,36},... | collective-permute-start | bytes 835592 | tf_op jit(solution)/shard_map/ppermute | solution.py:276
  40.3 12.0 %collective-permute-start.11 = (f32[272,256]{1,0:T(8,128)S(1)}, f32[272,256]{1,0:T(8,128)S(1)}, u32[]{:S(2)}, u32[]{:S(2)}) collective-permute-start(f32[272,256]{1,0:T(8,128)S(1)} %get-tuple-element.39.r_0_), channel_id=1, source_target_pairs={{8,0},{16,8},{24,16},{32,24},{40,32},{48,40},{56,48},{64,56},{72,6... | collective-permute-start | bytes 835592 | tf_op jit(solution)/shard_map/ppermute | solution.py:271
  53.5 11.8 %collective-permute-start.12 = (f32[272,256]{1,0:T(8,128)S(1)}, f32[272,256]{1,0:T(8,128)S(1)}, u32[]{:S(2)}, u32[]{:S(2)}) collective-permute-start(f32[272,256]{1,0:T(8,128)S(1)} %get-tuple-element.42.r_0_), channel_id=1, source_target_pairs={{16,0},{24,8},{32,16},{40,24},{48,32},{56,40},{64,48},{72,56},{80,... | collective-permute-start | bytes 835592 | tf_op jit(solution)/shard_map/ppermute | solution.py:271
  58.4 8.4 %collective-permute-start.13 = (f32[272,256]{1,0:T(8,128)S(1)}, f32[272,256]{1,0:T(8,128)S(1)}, u32[]{:S(2)}, u32[]{:S(2)}) collective-permute-start(f32[272,256]{1,0:T(8,128)S(1)} %get-tuple-element.42.r_0_), channel_id=1, source_target_pairs={{0,1},{8,9},{16,17},{24,25},{32,33},{40,41},{48,49},{56,57},{64,65... | collective-permute-start | bytes 835592 | tf_op jit(solution)/shard_map/ppermute | solution.py:271
  59.7 8.4 %collective-permute-start.14 = (f32[272,256]{1,0:T(8,128)S(1)}, f32[272,256]{1,0:T(8,128)S(1)}, u32[]{:S(2)}, u32[]{:S(2)}) collective-permute-start(f32[272,256]{1,0:T(8,128)S(1)} %get-tuple-element.42.r_0_), channel_id=1, source_target_pairs={{2,1},{10,9},{18,17},{26,25},{34,33},{42,41},{50,49},{58,57},{66,6... | collective-permute-start | bytes 835592 | tf_op jit(solution)/shard_map/ppermute | solution.py:271
  69.4 14.9 %collective-permute-start.15 = (f32[272,256]{1,0:T(8,128)S(1)}, f32[272,256]{1,0:T(8,128)S(1)}, u32[]{:S(2)}, u32[]{:S(2)}) collective-permute-start(f32[272,256]{1,0:T(8,128)S(1)} %get-tuple-element.43.r_0_), channel_id=1, source_target_pairs={{32,0},{40,8},{48,16},{56,24},{64,32},{72,40},{80,48},{88,56},{96,... | collective-permute-start | bytes 835592 | tf_op jit(solution)/shard_map/ppermute | solution.py:271
  72.2 12.1 %collective-permute-start.16 = (f32[272,256]{1,0:T(8,128)S(1)}, f32[272,256]{1,0:T(8,128)S(1)}, u32[]{:S(2)}, u32[]{:S(2)}) collective-permute-start(f32[272,256]{1,0:T(8,128)S(1)} %get-tuple-element.43.r_0_), channel_id=1, source_target_pairs={{0,1},{8,9},{16,17},{24,25},{32,33},{40,41},{48,49},{56,57},{64,65... | collective-permute-start | bytes 835592 | tf_op jit(solution)/shard_map/ppermute | solution.py:271
  73.5 10.9 %collective-permute-start.17 = (f32[272,256]{1,0:T(8,128)S(1)}, f32[272,256]{1,0:T(8,128)S(1)}, u32[]{:S(2)}, u32[]{:S(2)}) collective-permute-start(f32[272,256]{1,0:T(8,128)S(1)} %get-tuple-element.43.r_0_), channel_id=1, source_target_pairs={{2,1},{10,9},{18,17},{26,25},{34,33},{42,41},{50,49},{58,57},{66,6... | collective-permute-start | bytes 835592 | tf_op jit(solution)/shard_map/ppermute | solution.py:271
  85.6 6.4 %collective-permute-start.18 = (f32[272,256]{1,0:T(8,128)S(1)}, f32[272,256]{1,0:T(8,128)S(1)}, u32[]{:S(2)}, u32[]{:S(2)}) collective-permute-start(f32[272,256]{1,0:T(8,128)S(1)} %get-tuple-element.44.r_0_), channel_id=1, source_target_pairs={{64,0},{72,8},{80,16},{88,24},{96,32},{104,40},{112,48},{120,56},{... | collective-permute-start | bytes 835592 | tf_op jit(solution)/shard_map/ppermute | solution.py:271
  87.9 8.4 %collective-permute-start.19 = (f32[272,256]{1,0:T(8,128)S(1)}, f32[272,256]{1,0:T(8,128)S(1)}, u32[]{:S(2)}, u32[]{:S(2)}) collective-permute-start(f32[272,256]{1,0:T(8,128)S(1)} %get-tuple-element.44.r_0_), channel_id=1, source_target_pairs={{0,1},{8,9},{16,17},{24,25},{32,33},{40,41},{48,49},{56,57},{64,65... | collective-permute-start | bytes 835592 | tf_op jit(solution)/shard_map/ppermute | solution.py:271
  89.2 8.4 %collective-permute-start.20 = (f32[272,256]{1,0:T(8,128)S(1)}, f32[272,256]{1,0:T(8,128)S(1)}, u32[]{:S(2)}, u32[]{:S(2)}) collective-permute-start(f32[272,256]{1,0:T(8,128)S(1)} %get-tuple-element.44.r_0_), channel_id=1, source_target_pairs={{2,1},{10,9},{18,17},{26,25},{34,33},{42,41},{50,49},{58,57},{66,6... | collective-permute-start | bytes 835592 | tf_op jit(solution)/shard_map/ppermute | solution.py:271
  98.3 17.6 %collective-permute-start.28 = (f32[272,256]{1,0:T(8,128)S(1)}, f32[272,256]{1,0:T(8,128)}, u32[]{:S(2)}, u32[]{:S(2)}) collective-permute-start(f32[272,256]{1,0:T(8,128)S(1)} %get-tuple-element.45.own), channel_id=1, source_target_pairs={{0,1},{8,9},{16,17},{24,25},{32,33},{40,41},{48,49},{56,57},{64,65... | collective-permute-start | bytes 835592 | tf_op jit(solution)/shard_map/ppermute | solution.py:271
  99.6 18.8 %collective-permute-start.29 = (f32[272,256]{1,0:T(8,128)S(1)}, f32[272,256]{1,0:T(8,128)S(1)}, u32[]{:S(2)}, u32[]{:S(2)}) collective-permute-start(f32[272,256]{1,0:T(8,128)S(1)} %get-tuple-element.45.own), channel_id=1, source_target_pairs={{2,1},{10,9},{18,17},{26,25},{34,33},{42,41},{50,49},{58,57},{66,6... | collective-permute-start | bytes 835592 | tf_op jit(solution)/shard_map/ppermute | solution.py:271
  100.9 17.5 %collective-permute-start.30 = (f32[272,256]{1,0:T(8,128)S(1)}, f32[272,256]{1,0:T(8,128)S(1)}, u32[]{:S(2)}, u32[]{:S(2)}) collective-permute-start(f32[272,256]{1,0:T(8,128)S(1)} %get-tuple-element.45.own), channel_id=1, source_target_pairs={{129,1},{137,9},{145,17},{153,25},{161,33},{169,41},{177,49},{185,... | collective-permute-start | bytes 835592 | tf_op jit(solution)/shard_map/ppermute | solution.py:271
  103.5 0.7 collective-permute-start.21
  104.4 2.0 %collective-permute-start.22 = (f32[16,256]{1,0:T(8,128)S(1)}, f32[16,256]{1,0:T(8,128)S(1)}, u32[]{:S(2)}, u32[]{:S(2)}) collective-permute-start(f32[16,256]{1,0:T(8,128)S(1)} %shard_map.76), channel_id=1, source_target_pairs={{3,11},{11,19},{19,27},{27,35},{35,43},{43,51},{51,59},{59,67},{67... | collective-permute-start | bytes 49160 | tf_op jit(solution)/shard_map/ppermute | solution.py:271
  105.1 10.1 %collective-permute-start.26 = (f32[16,256]{1,0:T(8,128)S(1)}, f32[16,256]{1,0:T(8,128)S(1)}, u32[]{:S(2)}, u32[]{:S(2)}) collective-permute-start(f32[16,256]{1,0:T(8,128)S(1)} %shard_map.76), channel_id=1, source_target_pairs={{3,9},{11,17},{19,25},{27,33},{35,41},{43,49},{51,57},{59,65},{67,... | collective-permute-start | bytes 49160 | tf_op jit(solution)/shard_map/ppermute | solution.py:271
  106.4 13.8 %collective-permute-start.23 = (f32[16,256]{1,0:T(8,128)S(1)}, f32[16,256]{1,0:T(8,128)S(1)}, u32[]{:S(2)}, u32[]{:S(2)}) collective-permute-start(f32[16,256]{1,0:T(8,128)S(1)} %collective-permute-done.22.m3), channel_id=1, source_target_pairs={{3,0},{11,8},{19,16},{27,24},{35,32},{43,40},{51,48},{59,56},{67,6... | collective-permute-start | bytes 49160 | tf_op jit(solution)/shard_map/ppermute | solution.py:271
  115.2 5.0 %collective-permute-start.24 = (f32[16,256]{1,0:T(8,128)S(1)}, f32[16,256]{1,0:T(8,128)S(1)}, u32[]{:S(2)}, u32[]{:S(2)}) collective-permute-start(f32[16,256]{1,0:T(8,128)S(1)} %collective-permute-done.22.m3), channel_id=1, source_target_pairs={{3,2},{11,10},{19,18},{27,26},{35,34},{43,42},{51,50},{59,58},{67,... | collective-permute-start | bytes 49160 | tf_op jit(solution)/shard_map/ppermute | solution.py:271
  115.9 9.0 %collective-permute-start.27 = (f32[16,256]{1,0:T(8,128)S(1)}, f32[16,256]{1,0:T(8,128)S(1)}, u32[]{:S(2)}, u32[]{:S(2)}) collective-permute-start(f32[16,256]{1,0:T(8,128)S(1)} %collective-permute-done.26.m1.begin), channel_id=1, source_target_pairs={{1,5},{9,13},{17,21},{25,29},{33,37},{41,45},{49,53},{57,61},{65,6... | collective-permute-start | bytes 49160 | tf_op jit(solution)/shard_map/ppermute | solution.py:271
  118.8 11.8 %copy-start.1 = (bf16[8,256,256]{2,1,0:T(8,128)(2,1)S(1)}, bf16[8,256,256]{2,1,0:T(8,128)(2,1)}, u32[]{:S(2)}) copy-start(bf16[8,256,256]{2,1,0:T(8,128)(2,1)} %copy-done) | copy-start | bytes 3145732
  118.8 2.3 %collective-permute-start.31 = (f32[16,256]{1,0:T(8,128)S(1)}, f32[16,256]{1,0:T(8,128)S(1)}, u32[]{:S(2)}, u32[]{:S(2)}) collective-permute-start(f32[16,256]{1,0:T(8,128)S(1)} %shard_map.80), channel_id=1, source_target_pairs={{1,5},{9,13},{17,21},{25,29},{33,37},{41,45},{49,53},{57,61},{65,6... | collective-permute-start | bytes 49160 | tf_op jit(solution)/shard_map/ppermute | solution.py:271
  120.3 8.1 %collective-permute-start.25 = (f32[16,256]{1,0:T(8,128)S(1)}, f32[16,256]{1,0:T(8,128)S(1)}, u32[]{:S(2)}, u32[]{:S(2)}) collective-permute-start(f32[16,256]{1,0:T(8,128)S(1)} %add_add_fusion), channel_id=1, source_target_pairs={{0,4},{2,6},{3,7},{8,12},{10,14},{11,15},{16,20},{18,22},{19,23},{... | collective-permute-start | bytes 49160 | tf_op jit(solution)/shard_map/ppermute | solution.py:271
  121.0 7.9 %collective-permute-start.32 = (f32[16,256]{1,0:T(8,128)S(1)}, f32[16,256]{1,0:T(8,128)S(1)}, u32[]{:S(2)}, u32[]{:S(2)}) collective-permute-start(f32[16,256]{1,0:T(8,128)S(1)} %broadcast_select_fusion), channel_id=1, source_target_pairs={{9,0},{13,4},{17,8},{21,12},{25,16},{29,20},{33,24},{37,28},{41,32... | collective-permute-start | bytes 49160 | tf_op jit(solution)/shard_map/ppermute | solution.py:271
  122.3 6.6 %collective-permute-start.33 = (f32[16,256]{1,0:T(8,128)S(1)}, f32[16,256]{1,0:T(8,128)S(1)}, u32[]{:S(2)}, u32[]{:S(2)}) collective-permute-start(f32[16,256]{1,0:T(8,128)S(1)} %broadcast_select_fusion), channel_id=1, source_target_pairs={{9,2},{13,6},{17,10},{21,14},{25,18},{29,22},{33,26},{37,30},{41,3... | collective-permute-start | bytes 49160 | tf_op jit(solution)/shard_map/ppermute | solution.py:271
  123.6 5.4 %collective-permute-start.34 = (f32[16,256]{1,0:T(8,128)S(1)}, f32[16,256]{1,0:T(8,128)S(1)}, u32[]{:S(2)}, u32[]{:S(2)}) collective-permute-start(f32[16,256]{1,0:T(8,128)S(1)} %broadcast_select_fusion), channel_id=1, source_target_pairs={{9,3},{13,7},{17,11},{21,15},{25,19},{29,23},{33,27},{37,31},{41,3... | collective-permute-start | bytes 49160 | tf_op jit(solution)/shard_map/ppermute | solution.py:271
  124.9 5.6 %collective-permute-start.35 = (f32[16,256]{1,0:T(8,128)S(1)}, f32[16,256]{1,0:T(8,128)S(1)}, u32[]{:S(2)}, u32[]{:S(2)}) collective-permute-start(f32[16,256]{1,0:T(8,128)S(1)} %broadcast_select_fusion), channel_id=1, source_target_pairs={{9,1},{13,5},{17,9},{21,13},{25,17},{29,21},{33,25},{37,29},{41,33... | collective-permute-start | bytes 49160 | tf_op jit(solution)/shard_map/ppermute | solution.py:271

commit v4 on v3

--- a/solution.py
+++ b/solution.py
@@ -354,9 +354,9 @@
     qrow = hop(own, [(SUF_Q, SUF_Y)])
     (leaving,) = call(mean_kernel, [vector], own, got_v)
     begin = hop(leaving, [(PRE_X, SUF_Y)], 1)
-    ahead = hop(leaving, [(PRE_X, PRE_X)], 1)
-    means = {c: hop(ahead, [(PRE_X, (c, 0))]) for c in (0, 2)}
-    means[3] = ahead
+    means = {3: hop(leaving, [(PRE_X, PRE_X)], 1)}
+    for c in (0, 2):
+        means[c] = hop(begin, [(SUF_Y, (c, 0))])
     total = means[0] + (means[2] + means[3])
     x_pass = hop(total, [((c, 0), (c, 1)) for c in (0, 2, 3)])
     x_one = hop(begin, [((1, 0), (1, 1))])
@@ -364,16 +364,16 @@
     result = ((steps, drive.shape[1], D), f32)
     swept = [part, part, ((GRP, D), f32), result]
     held = (araw, drive16, dyn, x_b, x_bm)
-    sweep = call(early_sweep_kernel, swept, *held, begin)
+    ahead = call(early_sweep_kernel, swept, *held, begin)
     first = lax.rem(lax.axis_index("tm"), 2) == 0
     near, mid = call(near_kernel, [vector, vector], own, xrow, begin)
     (s_one,) = call(top_kernel, [vector], near, mid, qrow, got)
     s_two = jnp.where(first, s_one, hop(s_one, [(SUF_Y, (1, 1))]))
-    s_in = [hop(s_two, across(c), -1) for c in (0, 2, 3, 1)]
+    s_in = [hop(s_two, across(c), -1) for c in (0, 2, 1, 3)]
     xs8, proj8, mid8, filtered = call(
         mean_sweep_kernel,
         swept,
-        *held, means[0], means[2], means[3], x_pass, x_one, *sweep,
+        *held, means[0], means[2], means[3], x_pass, x_one, *ahead,
     )
     (smoothed,) = call(smooth_sweep_kernel, [result], graw, xs8, proj8, mid8, qy_bm, *s_in)
     return filtered, smoothed

time: 133 us -> 136 us (1.023)
  the two profiles are of different devices: /device:TPU:26 before, /device:TPU:30 now
where the time goes in v4:
time: 136 us; the launch traced here: 135 us
  waiting for transfers between devices  70.9 us (52%)
  starting transfers between devices  45.2 us (33%)
  Pallas kernels  13 us (10%)
  local copies, waits for them, and re-layouts  4.51 us (3%)
    ppermute x25, waiting for transfers between devices, send(): lax.ppermute(x, ('tm', 'col'), [(a * cols + b, c * cols + d) for (a, b),...  50 us
    ppermute x25, starting transfers between devices, send(): lax.ppermute(x, ('tm', 'col'), [(a * cols + b, c * cols + d) for (a, b),...  34.8 us
    ppermute x9, waiting for transfers between devices, turn(): return lax.ppermute(x, 'col', [(c, (c + by) % 4) for c in range(4)])  19 us
    pallas_call x14, Pallas kernels, call(): pl.pallas_call(kernel, out_shape=tuple((jax.ShapeDtypeStruct(s, d) for s,...  13 us
    ppermute x9, starting transfers between devices, turn(): return lax.ppermute(x, 'col', [(c, (c + by) % 4) for c in range(4)])  9.87 us
    unnamed x14, local copies, waits for them, and re-layouts  4.51 us
  transfers between devices with their start and end apart: 36, of which 13 were waited for; matrix products, arithmetic and copies ran while one was open for 1% of the time, Pallas kernels for 4%

profile of v4, /device:TPU:30, one launch (start us, length us, event | category | flops | bytes accessed | tf_op | source)
XLA Modules:
  0.0 135.4 jit_solution(7393955542915838224)
XLA Ops:
  0.6 0.6 collective-permute-start
  1.2 1.5 %collective-permute-start.8 = (bf16[8,64,256]{2,1,0:T(8,128)(2,1)}, bf16[8,64,256]{2,1,0:T(8,128)(2,1)S(1)}, u32[]{:S(2)}, u32[]{:S(2)}) collective-permute-start(bf16[8,64,256]{2,1,0:T(8,128)(2,1)} %g.1), channel_id=1, source_target_pairs={{0,3},{1,0},{2,1},{3,2},{4,7},{5,4},{6,5},{7,6},{8,11},{9,8},{10,9... | collective-permute-start | bytes 786440 | tf_op jit(solution)/shard_map/ppermute | solution.py:279
  2.7 0.8 collective-permute-start.1
  3.6 5.4 %collective-permute-done.a1 = bf16[8,64,256]{2,1,0:T(8,128)(2,1)S(1)} collective-permute-done((bf16[8,64,256]{2,1,0:T(8,128)(2,1)}, bf16[8,64,256]{2,1,0:T(8,128)(2,1)S(1)}, u32[]{:S(2)}, u32[]{:S(2)}) %collective-permute-start) | collective-permute-done | bytes 262176 | tf_op jit(solution)/shard_map/ppermute | solution.py:279
  9.0 1.7 %collective-permute-start.2 = (bf16[8,64,256]{2,1,0:T(8,128)(2,1)S(1)}, bf16[8,64,256]{2,1,0:T(8,128)(2,1)S(1)}, u32[]{:S(2)}, u32[]{:S(2)}) collective-permute-start(bf16[8,64,256]{2,1,0:T(8,128)(2,1)S(1)} %collective-permute-done.a1), channel_id=1, source_target_pairs={{0,1},{1,2},{2,3},{3,0},{4,5},{5,6},{6,7},{7,4},{8,9},{9,10},{10,1... | collective-permute-start | bytes 786440 | tf_op jit(solution)/shard_map/ppermute | solution.py:279
  10.7 0.3 collective-permute-start.7
  10.9 0.8 collective-permute-done.8.g2
  11.8 0.9 collective-permute-start.9
  12.7 0.8 pad_maximum_fusion.d0
  13.5 2.4 %collective-permute-start.3 = (f32[9,4,256]{2,1,0:T(4,128)S(1)}, f32[9,4,256]{2,1,0:T(4,128)S(1)}, u32[]{:S(2)}, u32[]{:S(2)}) collective-permute-start(f32[9,4,256]{2,1,0:T(4,128)S(1)} %pad_maximum_fusion.d0), channel_id=1, source_target_pairs={{0,1},{1,2},{2,3},{3,0},{4,5},{5,6},{6,7},{7,4},{8,9},{9,10},{10,1... | collective-permute-start | bytes 110600 | tf_op jit(solution)/shard_map/ppermute | solution.py:279
  15.9 6.7 %collective-permute-done.3.d1 = f32[9,4,256]{2,1,0:T(4,128)S(1)} collective-permute-done((f32[9,4,256]{2,1,0:T(4,128)S(1)}, f32[9,4,256]{2,1,0:T(4,128)S(1)}, u32[]{:S(2)}, u32[]{:S(2)}) %collective-permute-start.3) | collective-permute-done | bytes 36896 | tf_op jit(solution)/shard_map/ppermute | solution.py:279
  22.6 0.8 collective-permute-start.4
  23.4 4.3 %collective-permute-done.4.d2 = f32[9,4,256]{2,1,0:T(4,128)S(1)} collective-permute-done((f32[9,4,256]{2,1,0:T(4,128)S(1)}, f32[9,4,256]{2,1,0:T(4,128)S(1)}, u32[]{:S(2)}, u32[]{:S(2)}) %collective-permute-start.4) | collective-permute-done | bytes 36896 | tf_op jit(solution)/shard_map/ppermute | solution.py:279
  27.7 0.8 collective-permute-start.5
  28.6 0.9 copy-done.4
  29.5 0.9 copy-done.5
  30.5 0.9 copy-done.6
  31.5 1.7 %collective-permute-done.5.d3 = f32[9,4,256]{2,1,0:T(4,128)S(1)} collective-permute-done((f32[9,4,256]{2,1,0:T(4,128)S(1)}, f32[9,4,256]{2,1,0:T(4,128)S(1)}, u32[]{:S(2)}, u32[]{:S(2)}) %collective-permute-start.5) | collective-permute-done | bytes 36896 | tf_op jit(solution)/shard_map/ppermute | solution.py:279
  33.2 2.1 %shard_map.69 = (bf16[8,256,256]{2,1,0:T(8,128)(2,1)S(1)}, f32[9,16,256]{2,1,0:T(8,128)S(1)}, f32[8,272,256]{2,1,0:T(8,128)S(1)}, f32[8,272,256]{2,1,0:T(8,128)S(1)}, f32[272,256]{1,0:T(8,128)S(1)}) custom-call(bf16[8,64,256]{2,1,0:T(8,128)(2,1)S(1)} %get-tuple-element.30.a0, bf16[8,64,256]{2,1,0:T(8,128)(2,1)S(1)} %collective-permute-done.a1, ...), custom_call_target="tpu_custom_call" | custom-call | tf_op jit(solution)/shard_map/pallas_call | solution.py:255
  35.4 1.8 %shard_map.70 = (bf16[8,256,256]{2,1,0:T(8,128)(2,1)S(1)}, f32[528,256]{1,0:T(8,128)S(1)}) custom-call(bf16[8,64,256]{2,1,0:T(8,128)(2,1)S(1)} %get-tuple-element.35.g0, bf16[8,64,256]{2,1,0:T(8,128)(2,1)S(1)} %collective-permute-done.7.g1, bf16[8,64,256]{2,1,0:T(8,128)(2,1)S(1)} %collective-permute-done.8.g2, ...), custom_call_target="tpu_custom_call" | custom-call | tf_op jit(solution)/shard_map/pallas_call | solution.py:255
  37.3 0.5 collective-permute-start.6
  37.8 1.8 %collective-permute-done.6.x_m.x_bm = f32[272,256]{1,0:T(8,128)S(1)} collective-permute-done((f32[272,256]{1,0:T(8,128)S(1)}, f32[272,256]{1,0:T(8,128)S(1)}, u32[]{:S(2)}, u32[]{:S(2)}) %collective-permute-start.6) | collective-permute-done | bytes 278560 | tf_op jit(solution)/shard_map/ppermute | solution.py:276
  39.6 1.1 shard_map.71
  40.7 3.8 %collective-permute-start.11 = (f32[272,256]{1,0:T(8,128)S(1)}, f32[272,256]{1,0:T(8,128)S(1)}, u32[]{:S(2)}, u32[]{:S(2)}) collective-permute-start(f32[272,256]{1,0:T(8,128)S(1)} %get-tuple-element.39.r_0_), channel_id=1, source_target_pairs={{8,0},{16,8},{24,16},{32,24},{40,32},{48,40},{56,48},{64,56},{72,6... | collective-permute-start | bytes 835592 | tf_op jit(solution)/shard_map/ppermute | solution.py:271
  44.5 8.6 %collective-permute-done.11.r_1_ = f32[272,256]{1,0:T(8,128)S(1)} collective-permute-done((f32[272,256]{1,0:T(8,128)S(1)}, f32[272,256]{1,0:T(8,128)S(1)}, u32[]{:S(2)}, u32[]{:S(2)}) %collective-permute-start.11) | collective-permute-done | bytes 278560 | tf_op jit(solution)/shard_map/ppermute | solution.py:271
  53.2 0.9 shard_map.72
  54.1 1.9 %collective-permute-start.12 = (f32[272,256]{1,0:T(8,128)S(1)}, f32[272,256]{1,0:T(8,128)S(1)}, u32[]{:S(2)}, u32[]{:S(2)}) collective-permute-start(f32[272,256]{1,0:T(8,128)S(1)} %get-tuple-element.42.r_0_), channel_id=1, source_target_pairs={{16,0},{24,8},{32,16},{40,24},{48,32},{56,40},{64,48},{72,56},{80,... | collective-permute-start | bytes 835592 | tf_op jit(solution)/shard_map/ppermute | solution.py:271
  56.0 0.7 collective-permute-start.13
  56.7 0.7 collective-permute-start.14
  57.4 10.6 %collective-permute-done.12.r_1_ = f32[272,256]{1,0:T(8,128)S(1)} collective-permute-done((f32[272,256]{1,0:T(8,128)S(1)}, f32[272,256]{1,0:T(8,128)S(1)}, u32[]{:S(2)}, u32[]{:S(2)}) %collective-permute-start.12) | collective-permute-done | bytes 278560 | tf_op jit(solution)/shard_map/ppermute | solution.py:271
  68.0 0.9 shard_map.73
  68.9 5.8 %collective-permute-start.15 = (f32[272,256]{1,0:T(8,128)S(1)}, f32[272,256]{1,0:T(8,128)S(1)}, u32[]{:S(2)}, u32[]{:S(2)}) collective-permute-start(f32[272,256]{1,0:T(8,128)S(1)} %get-tuple-element.43.r_0_), channel_id=1, source_target_pairs={{32,0},{40,8},{48,16},{56,24},{64,32},{72,40},{80,48},{88,56},{96,... | collective-permute-start | bytes 835592 | tf_op jit(solution)/shard_map/ppermute | solution.py:271
  74.7 0.7 collective-permute-start.16
  75.4 0.7 collective-permute-start.17
  76.1 8.5 %collective-permute-done.15.r_1_ = f32[272,256]{1,0:T(8,128)S(1)} collective-permute-done((f32[272,256]{1,0:T(8,128)S(1)}, f32[272,256]{1,0:T(8,128)S(1)}, u32[]{:S(2)}, u32[]{:S(2)}) %collective-permute-start.15) | collective-permute-done | bytes 278560 | tf_op jit(solution)/shard_map/ppermute | solution.py:271
  84.6 0.9 shard_map.74
  85.5 1.3 collective-permute-start.18
  86.8 0.7 collective-permute-start.19
  87.4 0.7 collective-permute-start.20
  88.1 5.8 %collective-permute-done.18.r_1_ = f32[272,256]{1,0:T(8,128)S(1)} collective-permute-done((f32[272,256]{1,0:T(8,128)S(1)}, f32[272,256]{1,0:T(8,128)S(1)}, u32[]{:S(2)}, u32[]{:S(2)}) %collective-permute-start.18) | collective-permute-done | bytes 278560 | tf_op jit(solution)/shard_map/ppermute | solution.py:271
  93.9 0.3 shard_map.75
  94.2 0.7 collective-permute-start.28
  94.9 0.7 collective-permute-start.29
  95.6 0.7 collective-permute-start.30
  96.3 1.3 collective-permute-start.21
  97.6 5.8 %collective-permute-done.21.got = f32[16,256]{1,0:T(8,128)S(1)} collective-permute-done((f32[16,256]{1,0:T(8,128)S(1)}, f32[16,256]{1,0:T(8,128)S(1)}, u32[]{:S(2)}, u32[]{:S(2)}) %collective-permute-start.21) | collective-permute-done | bytes 16416 | tf_op jit(solution)/shard_map/ppermute | solution.py:271
  103.5 5.3 %collective-permute-start.22 = (f32[16,256]{1,0:T(8,128)S(1)}, f32[16,256]{1,0:T(8,128)S(1)}, u32[]{:S(2)}, u32[]{:S(2)}) collective-permute-start(f32[16,256]{1,0:T(8,128)S(1)} %shard_map.76), channel_id=1, source_target_pairs={{3,9},{11,17},{19,25},{27,33},{35,41},{43,49},{51,57},{59,65},{67,... | collective-permute-start | bytes 49160 | tf_op jit(solution)/shard_map/ppermute | solution.py:271
  108.8 1.9 %collective-permute-start.25 = (f32[16,256]{1,0:T(8,128)S(1)}, f32[16,256]{1,0:T(8,128)S(1)}, u32[]{:S(2)}, u32[]{:S(2)}) collective-permute-start(f32[16,256]{1,0:T(8,128)S(1)} %shard_map.76), channel_id=1, source_target_pairs={{3,11},{11,19},{19,27},{27,35},{35,43},{43,51},{51,59},{59,67},{67... | collective-permute-start | bytes 49160 | tf_op jit(solution)/shard_map/ppermute | solution.py:271
  110.8 0.7 collective-permute-start.23
  111.5 0.7 copy-done.2
  112.2 0.7 collective-permute-start.24
  112.9 0.9 copy-done.3
  114.0 0.7 collective-permute-start.27
  114.7 0.4 shard_map.80
  115.1 0.8 collective-permute-start.31
  115.9 0.7 collective-permute-done.25.m3
  116.6 1.3 collective-permute-start.26
  117.9 0.7 collective-permute-start.32
  118.6 0.7 collective-permute-start.33
  119.3 0.7 collective-permute-start.34
  119.9 1.3 collective-permute-start.35
  121.3 2.1 %shard_map.78 = (f32[8,8,256]{2,1,0:T(8,128)S(1)}, f32[8,8,256]{2,1,0:T(8,128)S(1)}, f32[8,256]{1,0:T(8,128)S(1)}, f32[8,4,256]{2,1,0:T(4,128)}) custom-call(bf16[8,256,256]{2,1,0:T(8,128)(2,1)S(1)} %get-tuple-element.32.r_4_.araw, f32[9,16,256]{2,1,0:T(8,128)S(1)} %get-tuple-element.33.r_5_.drive, f32[256,256]{1,0:T(8,128)S(1)} %get-tuple-element.31.dyn.r_6_, ...), custom_call_target="tpu_custom_call" | custom-call | tf_op jit(solution)/shard_map/pallas_call | solution.py:255
  123.4 10.0 %collective-permute-done.35.s3 = f32[16,256]{1,0:T(8,128)S(1)} collective-permute-done((f32[16,256]{1,0:T(8,128)S(1)}, f32[16,256]{1,0:T(8,128)S(1)}, u32[]{:S(2)}, u32[]{:S(2)}) %collective-permute-start.35) | collective-permute-done | bytes 16416 | tf_op jit(solution)/shard_map/ppermute | solution.py:271
  133.4 2.0 %shard_map.81 = f32[8,4,256]{2,1,0:T(4,128)} custom-call(bf16[8,256,256]{2,1,0:T(8,128)(2,1)S(1)} %copy-done.1, f32[8,8,256]{2,1,0:T(8,128)S(1)} %get-tuple-element.53.xs, f32[8,8,256]{2,1,0:T(8,128)S(1)} %get-tuple-element.54.proj, f32[8,256]{1,0:T(8,128)S(1)} %get-tuple-element.55.mid, f32[528,256]{1,0:T(8,128)S(1)} %collective-permute-done.10.qy_m, ...), custom_call_target="tpu_custom_call" | custom-call | tf_op jit(solution)/shard_map/pallas_call | solution.py:255
  (39 shorter events, 0.6 us)
Async XLA Ops:
  0.6 8.3 %collective-permute-start = (bf16[8,64,256]{2,1,0:T(8,128)(2,1)}, bf16[8,64,256]{2,1,0:T(8,128)(2,1)S(1)}, u32[]{:S(2)}, u32[]{:S(2)}) collective-permute-start(bf16[8,64,256]{2,1,0:T(8,128)(2,1)} %a.1), channel_id=1, source_target_pairs={{0,1},{1,2},{2,3},{3,0},{4,5},{5,6},{6,7},{7,4},{8,9},{9,10},{10,1... | collective-permute-start | bytes 786440 | tf_op jit(solution)/shard_map/ppermute | solution.py:279
  1.2 10.6 %collective-permute-start.8 = (bf16[8,64,256]{2,1,0:T(8,128)(2,1)}, bf16[8,64,256]{2,1,0:T(8,128)(2,1)S(1)}, u32[]{:S(2)}, u32[]{:S(2)}) collective-permute-start(bf16[8,64,256]{2,1,0:T(8,128)(2,1)} %g.1), channel_id=1, source_target_pairs={{0,3},{1,0},{2,1},{3,2},{4,7},{5,4},{6,5},{7,6},{8,11},{9,8},{10,9... | collective-permute-start | bytes 786440 | tf_op jit(solution)/shard_map/ppermute | solution.py:279
  2.7 30.5 %collective-permute-start.1 = (bf16[8,64,256]{2,1,0:T(8,128)(2,1)}, bf16[8,64,256]{2,1,0:T(8,128)(2,1)S(1)}, u32[]{:S(2)}, u32[]{:S(2)}) collective-permute-start(bf16[8,64,256]{2,1,0:T(8,128)(2,1)} %a.1), channel_id=1, source_target_pairs={{0,3},{1,0},{2,1},{3,2},{4,7},{5,4},{6,5},{7,6},{8,11},{9,8},{10,9... | collective-permute-start | bytes 786440 | tf_op jit(solution)/shard_map/ppermute | solution.py:279
  9.0 24.2 %collective-permute-start.2 = (bf16[8,64,256]{2,1,0:T(8,128)(2,1)S(1)}, bf16[8,64,256]{2,1,0:T(8,128)(2,1)S(1)}, u32[]{:S(2)}, u32[]{:S(2)}) collective-permute-start(bf16[8,64,256]{2,1,0:T(8,128)(2,1)S(1)} %collective-permute-done.a1), channel_id=1, source_target_pairs={{0,1},{1,2},{2,3},{3,0},{4,5},{5,6},{6,7},{7,4},{8,9},{9,10},{10,1... | collective-permute-start | bytes 786440 | tf_op jit(solution)/shard_map/ppermute | solution.py:279
  10.7 24.7 %collective-permute-start.7 = (bf16[8,64,256]{2,1,0:T(8,128)(2,1)}, bf16[8,64,256]{2,1,0:T(8,128)(2,1)S(1)}, u32[]{:S(2)}, u32[]{:S(2)}) collective-permute-start(bf16[8,64,256]{2,1,0:T(8,128)(2,1)} %g.1), channel_id=1, source_target_pairs={{0,1},{1,2},{2,3},{3,0},{4,5},{5,6},{6,7},{7,4},{8,9},{9,10},{10,1... | collective-permute-start | bytes 786440 | tf_op jit(solution)/shard_map/ppermute | solution.py:279
  11.8 23.6 %collective-permute-start.9 = (bf16[8,64,256]{2,1,0:T(8,128)(2,1)S(1)}, bf16[8,64,256]{2,1,0:T(8,128)(2,1)S(1)}, u32[]{:S(2)}, u32[]{:S(2)}) collective-permute-start(bf16[8,64,256]{2,1,0:T(8,128)(2,1)S(1)} %collective-permute-done.8.g2), channel_id=1, source_target_pairs={{0,3},{1,0},{2,1},{3,2},{4,7},{5,4},{6,5},{7,6},{8,11},{9,8},{10,9... | collective-permute-start | bytes 786440 | tf_op jit(solution)/shard_map/ppermute | solution.py:279
  13.5 9.1 %collective-permute-start.3 = (f32[9,4,256]{2,1,0:T(4,128)S(1)}, f32[9,4,256]{2,1,0:T(4,128)S(1)}, u32[]{:S(2)}, u32[]{:S(2)}) collective-permute-start(f32[9,4,256]{2,1,0:T(4,128)S(1)} %pad_maximum_fusion.d0), channel_id=1, source_target_pairs={{0,1},{1,2},{2,3},{3,0},{4,5},{5,6},{6,7},{7,4},{8,9},{9,10},{10,1... | collective-permute-start | bytes 110600 | tf_op jit(solution)/shard_map/ppermute | solution.py:279
  22.6 5.2 %collective-permute-start.4 = (f32[9,4,256]{2,1,0:T(4,128)S(1)}, f32[9,4,256]{2,1,0:T(4,128)S(1)}, u32[]{:S(2)}, u32[]{:S(2)}) collective-permute-start(f32[9,4,256]{2,1,0:T(4,128)S(1)} %pad_maximum_fusion.d0), channel_id=1, source_target_pairs={{0,3},{1,0},{2,1},{3,2},{4,7},{5,4},{6,5},{7,6},{8,11},{9,8},{10,9... | collective-permute-start | bytes 110600 | tf_op jit(solution)/shard_map/ppermute | solution.py:279
  27.7 5.5 %collective-permute-start.5 = (f32[9,4,256]{2,1,0:T(4,128)S(1)}, f32[9,4,256]{2,1,0:T(4,128)S(1)}, u32[]{:S(2)}, u32[]{:S(2)}) collective-permute-start(f32[9,4,256]{2,1,0:T(4,128)S(1)} %pad_maximum_fusion.d0), channel_id=1, source_target_pairs={{0,2},{1,3},{2,0},{3,1},{4,6},{5,7},{6,4},{7,5},{8,10},{9,11},{10,... | collective-permute-start | bytes 110600 | tf_op jit(solution)/shard_map/ppermute | solution.py:279
  28.6 0.9 copy-start.4
  29.5 0.9 copy-start.5
  30.5 0.9 copy-start.6
  37.2 31.7 %copy-start = (bf16[8,256,256]{2,1,0:T(8,128)(2,1)}, bf16[8,256,256]{2,1,0:T(8,128)(2,1)S(1)}, u32[]{:S(2)}) copy-start(bf16[8,256,256]{2,1,0:T(8,128)(2,1)S(1)} %get-tuple-element.52.graw) | copy-start | bytes 3145732
  37.2 2.4 %collective-permute-start.10 = (f32[528,256]{1,0:T(8,128)S(1)}, f32[528,256]{1,0:T(8,128)S(1)}, u32[]{:S(2)}, u32[]{:S(2)}) collective-permute-start(f32[528,256]{1,0:T(8,128)S(1)} %get-tuple-element.38.qy), channel_id=1, source_target_pairs={{0,4},{4,0},{8,12},{12,8},{16,20},{20,16},{24,28},{28,24},{32,36},... | collective-permute-start | bytes 1622024 | tf_op jit(solution)/shard_map/ppermute | solution.py:276
  37.3 2.3 %collective-permute-start.6 = (f32[272,256]{1,0:T(8,128)S(1)}, f32[272,256]{1,0:T(8,128)S(1)}, u32[]{:S(2)}, u32[]{:S(2)}) collective-permute-start(f32[272,256]{1,0:T(8,128)S(1)} %get-tuple-element.34.x.x_b), channel_id=1, source_target_pairs={{0,4},{4,0},{8,12},{12,8},{16,20},{20,16},{24,28},{28,24},{32,36},... | collective-permute-start | bytes 835592 | tf_op jit(solution)/shard_map/ppermute | solution.py:276
  40.7 12.5 %collective-permute-start.11 = (f32[272,256]{1,0:T(8,128)S(1)}, f32[272,256]{1,0:T(8,128)S(1)}, u32[]{:S(2)}, u32[]{:S(2)}) collective-permute-start(f32[272,256]{1,0:T(8,128)S(1)} %get-tuple-element.39.r_0_), channel_id=1, source_target_pairs={{8,0},{16,8},{24,16},{32,24},{40,32},{48,40},{56,48},{64,56},{72,6... | collective-permute-start | bytes 835592 | tf_op jit(solution)/shard_map/ppermute | solution.py:271
  54.1 13.9 %collective-permute-start.12 = (f32[272,256]{1,0:T(8,128)S(1)}, f32[272,256]{1,0:T(8,128)S(1)}, u32[]{:S(2)}, u32[]{:S(2)}) collective-permute-start(f32[272,256]{1,0:T(8,128)S(1)} %get-tuple-element.42.r_0_), channel_id=1, source_target_pairs={{16,0},{24,8},{32,16},{40,24},{48,32},{56,40},{64,48},{72,56},{80,... | collective-permute-start | bytes 835592 | tf_op jit(solution)/shard_map/ppermute | solution.py:271
  56.0 12.0 %collective-permute-start.13 = (f32[272,256]{1,0:T(8,128)S(1)}, f32[272,256]{1,0:T(8,128)S(1)}, u32[]{:S(2)}, u32[]{:S(2)}) collective-permute-start(f32[272,256]{1,0:T(8,128)S(1)} %get-tuple-element.42.r_0_), channel_id=1, source_target_pairs={{0,1},{8,9},{16,17},{24,25},{32,33},{40,41},{48,49},{56,57},{64,65... | collective-permute-start | bytes 835592 | tf_op jit(solution)/shard_map/ppermute | solution.py:271
  56.7 11.3 %collective-permute-start.14 = (f32[272,256]{1,0:T(8,128)S(1)}, f32[272,256]{1,0:T(8,128)S(1)}, u32[]{:S(2)}, u32[]{:S(2)}) collective-permute-start(f32[272,256]{1,0:T(8,128)S(1)} %get-tuple-element.42.r_0_), channel_id=1, source_target_pairs={{2,1},{10,9},{18,17},{26,25},{34,33},{42,41},{50,49},{58,57},{66,6... | collective-permute-start | bytes 835592 | tf_op jit(solution)/shard_map/ppermute | solution.py:271
  68.9 15.7 %collective-permute-start.15 = (f32[272,256]{1,0:T(8,128)S(1)}, f32[272,256]{1,0:T(8,128)S(1)}, u32[]{:S(2)}, u32[]{:S(2)}) collective-permute-start(f32[272,256]{1,0:T(8,128)S(1)} %get-tuple-element.43.r_0_), channel_id=1, source_target_pairs={{32,0},{40,8},{48,16},{56,24},{64,32},{72,40},{80,48},{88,56},{96,... | collective-permute-start | bytes 835592 | tf_op jit(solution)/shard_map/ppermute | solution.py:271
  74.7 9.9 %collective-permute-start.16 = (f32[272,256]{1,0:T(8,128)S(1)}, f32[272,256]{1,0:T(8,128)S(1)}, u32[]{:S(2)}, u32[]{:S(2)}) collective-permute-start(f32[272,256]{1,0:T(8,128)S(1)} %get-tuple-element.43.r_0_), channel_id=1, source_target_pairs={{0,1},{8,9},{16,17},{24,25},{32,33},{40,41},{48,49},{56,57},{64,65... | collective-permute-start | bytes 835592 | tf_op jit(solution)/shard_map/ppermute | solution.py:271
  75.4 9.2 %collective-permute-start.17 = (f32[272,256]{1,0:T(8,128)S(1)}, f32[272,256]{1,0:T(8,128)S(1)}, u32[]{:S(2)}, u32[]{:S(2)}) collective-permute-start(f32[272,256]{1,0:T(8,128)S(1)} %get-tuple-element.43.r_0_), channel_id=1, source_target_pairs={{2,1},{10,9},{18,17},{26,25},{34,33},{42,41},{50,49},{58,57},{66,6... | collective-permute-start | bytes 835592 | tf_op jit(solution)/shard_map/ppermute | solution.py:271
  85.5 8.4 %collective-permute-start.18 = (f32[272,256]{1,0:T(8,128)S(1)}, f32[272,256]{1,0:T(8,128)S(1)}, u32[]{:S(2)}, u32[]{:S(2)}) collective-permute-start(f32[272,256]{1,0:T(8,128)S(1)} %get-tuple-element.44.r_0_), channel_id=1, source_target_pairs={{64,0},{72,8},{80,16},{88,24},{96,32},{104,40},{112,48},{120,56},{... | collective-permute-start | bytes 835592 | tf_op jit(solution)/shard_map/ppermute | solution.py:271
  86.8 7.1 %collective-permute-start.19 = (f32[272,256]{1,0:T(8,128)S(1)}, f32[272,256]{1,0:T(8,128)S(1)}, u32[]{:S(2)}, u32[]{:S(2)}) collective-permute-start(f32[272,256]{1,0:T(8,128)S(1)} %get-tuple-element.44.r_0_), channel_id=1, source_target_pairs={{0,1},{8,9},{16,17},{24,25},{32,33},{40,41},{48,49},{56,57},{64,65... | collective-permute-start | bytes 835592 | tf_op jit(solution)/shard_map/ppermute | solution.py:271
  87.4 6.5 %collective-permute-start.20 = (f32[272,256]{1,0:T(8,128)S(1)}, f32[272,256]{1,0:T(8,128)S(1)}, u32[]{:S(2)}, u32[]{:S(2)}) collective-permute-start(f32[272,256]{1,0:T(8,128)S(1)} %get-tuple-element.44.r_0_), channel_id=1, source_target_pairs={{2,1},{10,9},{18,17},{26,25},{34,33},{42,41},{50,49},{58,57},{66,6... | collective-permute-start | bytes 835592 | tf_op jit(solution)/shard_map/ppermute | solution.py:271
  94.2 17.3 %collective-permute-start.28 = (f32[272,256]{1,0:T(8,128)S(1)}, f32[272,256]{1,0:T(8,128)S(1)}, u32[]{:S(2)}, u32[]{:S(2)}) collective-permute-start(f32[272,256]{1,0:T(8,128)S(1)} %get-tuple-element.45.own), channel_id=1, source_target_pairs={{0,1},{8,9},{16,17},{24,25},{32,33},{40,41},{48,49},{56,57},{64,65... | collective-permute-start | bytes 835592 | tf_op jit(solution)/shard_map/ppermute | solution.py:271
  94.9 19.1 %collective-permute-start.29 = (f32[272,256]{1,0:T(8,128)S(1)}, f32[272,256]{1,0:T(8,128)S(1)}, u32[]{:S(2)}, u32[]{:S(2)}) collective-permute-start(f32[272,256]{1,0:T(8,128)S(1)} %get-tuple-element.45.own), channel_id=1, source_target_pairs={{2,1},{10,9},{18,17},{26,25},{34,33},{42,41},{50,49},{58,57},{66,6... | collective-permute-start | bytes 835592 | tf_op jit(solution)/shard_map/ppermute | solution.py:271
  95.6 19.1 %collective-permute-start.30 = (f32[272,256]{1,0:T(8,128)S(1)}, f32[272,256]{1,0:T(8,128)S(1)}, u32[]{:S(2)}, u32[]{:S(2)}) collective-permute-start(f32[272,256]{1,0:T(8,128)S(1)} %get-tuple-element.45.own), channel_id=1, source_target_pairs={{129,1},{137,9},{145,17},{153,25},{161,33},{169,41},{177,49},{185,... | collective-permute-start | bytes 835592 | tf_op jit(solution)/shard_map/ppermute | solution.py:271
  96.3 7.1 %collective-permute-start.21 = (f32[16,256]{1,0:T(8,128)S(1)}, f32[16,256]{1,0:T(8,128)S(1)}, u32[]{:S(2)}, u32[]{:S(2)}) collective-permute-start(f32[16,256]{1,0:T(8,128)S(1)} %get-tuple-element.46), channel_id=1, source_target_pairs={{3,131},{11,139},{19,147},{27,155},{35,163},{43,171},{51,179},{59,... | collective-permute-start | bytes 49160 | tf_op jit(solution)/shard_map/ppermute | solution.py:271
  103.5 7.2 %collective-permute-start.22 = (f32[16,256]{1,0:T(8,128)S(1)}, f32[16,256]{1,0:T(8,128)S(1)}, u32[]{:S(2)}, u32[]{:S(2)}) collective-permute-start(f32[16,256]{1,0:T(8,128)S(1)} %shard_map.76), channel_id=1, source_target_pairs={{3,9},{11,17},{19,25},{27,33},{35,41},{43,49},{51,57},{59,65},{67,... | collective-permute-start | bytes 49160 | tf_op jit(solution)/shard_map/ppermute | solution.py:271
  108.8 7.7 %collective-permute-start.25 = (f32[16,256]{1,0:T(8,128)S(1)}, f32[16,256]{1,0:T(8,128)S(1)}, u32[]{:S(2)}, u32[]{:S(2)}) collective-permute-start(f32[16,256]{1,0:T(8,128)S(1)} %shard_map.76), channel_id=1, source_target_pairs={{3,11},{11,19},{19,27},{27,35},{35,43},{43,51},{51,59},{59,67},{67... | collective-permute-start | bytes 49160 | tf_op jit(solution)/shard_map/ppermute | solution.py:271
  110.8 5.8 %collective-permute-start.23 = (f32[16,256]{1,0:T(8,128)S(1)}, f32[16,256]{1,0:T(8,128)S(1)}, u32[]{:S(2)}, u32[]{:S(2)}) collective-permute-start(f32[16,256]{1,0:T(8,128)S(1)} %collective-permute-done.22.m1.begin), channel_id=1, source_target_pairs={{1,0},{9,8},{17,16},{25,24},{33,32},{41,40},{49,48},{57,56},{65,64... | collective-permute-start | bytes 49160 | tf_op jit(solution)/shard_map/ppermute | solution.py:271
  111.5 0.7 copy-start.2
  112.2 4.4 %collective-permute-start.24 = (f32[16,256]{1,0:T(8,128)S(1)}, f32[16,256]{1,0:T(8,128)S(1)}, u32[]{:S(2)}, u32[]{:S(2)}) collective-permute-start(f32[16,256]{1,0:T(8,128)S(1)} %collective-permute-done.22.m1.begin), channel_id=1, source_target_pairs={{1,2},{9,10},{17,18},{25,26},{33,34},{41,42},{49,50},{57,58},{65,6... | collective-permute-start | bytes 49160 | tf_op jit(solution)/shard_map/ppermute | solution.py:271
  112.8 1.0 copy-start.3
  114.0 5.9 %collective-permute-start.27 = (f32[16,256]{1,0:T(8,128)S(1)}, f32[16,256]{1,0:T(8,128)S(1)}, u32[]{:S(2)}, u32[]{:S(2)}) collective-permute-start(f32[16,256]{1,0:T(8,128)S(1)} %collective-permute-done.22.m1.begin), channel_id=1, source_target_pairs={{1,5},{9,13},{17,21},{25,29},{33,37},{41,45},{49,53},{57,61},{65,6... | collective-permute-start | bytes 49160 | tf_op jit(solution)/shard_map/ppermute | solution.py:271
  115.1 18.3 %copy-start.1 = (bf16[8,256,256]{2,1,0:T(8,128)(2,1)S(1)}, bf16[8,256,256]{2,1,0:T(8,128)(2,1)}, u32[]{:S(2)}) copy-start(bf16[8,256,256]{2,1,0:T(8,128)(2,1)} %copy-done) | copy-start | bytes 3145732
  115.1 2.8 %collective-permute-start.31 = (f32[16,256]{1,0:T(8,128)S(1)}, f32[16,256]{1,0:T(8,128)S(1)}, u32[]{:S(2)}, u32[]{:S(2)}) collective-permute-start(f32[16,256]{1,0:T(8,128)S(1)} %shard_map.80), channel_id=1, source_target_pairs={{1,5},{9,13},{17,21},{25,29},{33,37},{41,45},{49,53},{57,61},{65,6... | collective-permute-start | bytes 49160 | tf_op jit(solution)/shard_map/ppermute | solution.py:271
  116.6 4.7 %collective-permute-start.26 = (f32[16,256]{1,0:T(8,128)S(1)}, f32[16,256]{1,0:T(8,128)S(1)}, u32[]{:S(2)}, u32[]{:S(2)}) collective-permute-start(f32[16,256]{1,0:T(8,128)S(1)} %add_add_fusion), channel_id=1, source_target_pairs={{0,4},{2,6},{3,7},{8,12},{10,14},{11,15},{16,20},{18,22},{19,23},{... | collective-permute-start | bytes 49160 | tf_op jit(solution)/shard_map/ppermute | solution.py:271
  117.9 5.4 %collective-permute-start.32 = (f32[16,256]{1,0:T(8,128)S(1)}, f32[16,256]{1,0:T(8,128)S(1)}, u32[]{:S(2)}, u32[]{:S(2)}) collective-permute-start(f32[16,256]{1,0:T(8,128)S(1)} %broadcast_select_fusion), channel_id=1, source_target_pairs={{9,0},{13,4},{17,8},{21,12},{25,16},{29,20},{33,24},{37,28},{41,32... | collective-permute-start | bytes 49160 | tf_op jit(solution)/shard_map/ppermute | solution.py:271
  118.6 4.8 %collective-permute-start.33 = (f32[16,256]{1,0:T(8,128)S(1)}, f32[16,256]{1,0:T(8,128)S(1)}, u32[]{:S(2)}, u32[]{:S(2)}) collective-permute-start(f32[16,256]{1,0:T(8,128)S(1)} %broadcast_select_fusion), channel_id=1, source_target_pairs={{9,2},{13,6},{17,10},{21,14},{25,18},{29,22},{33,26},{37,30},{41,3... | collective-permute-start | bytes 49160 | tf_op jit(solution)/shard_map/ppermute | solution.py:271
  119.3 4.1 %collective-permute-start.34 = (f32[16,256]{1,0:T(8,128)S(1)}, f32[16,256]{1,0:T(8,128)S(1)}, u32[]{:S(2)}, u32[]{:S(2)}) collective-permute-start(f32[16,256]{1,0:T(8,128)S(1)} %broadcast_select_fusion), channel_id=1, source_target_pairs={{9,1},{13,5},{17,9},{21,13},{25,17},{29,21},{33,25},{37,29},{41,33... | collective-permute-start | bytes 49160 | tf_op jit(solution)/shard_map/ppermute | solution.py:271
  119.9 13.4 %collective-permute-start.35 = (f32[16,256]{1,0:T(8,128)S(1)}, f32[16,256]{1,0:T(8,128)S(1)}, u32[]{:S(2)}, u32[]{:S(2)}) collective-permute-start(f32[16,256]{1,0:T(8,128)S(1)} %broadcast_select_fusion), channel_id=1, source_target_pairs={{9,3},{13,7},{17,11},{21,15},{25,19},{29,23},{33,27},{37,31},{41,3... | collective-permute-start | bytes 49160 | tf_op jit(solution)/shard_map/ppermute | solution.py:271

commit v5 on v4

--- a/solution.py
+++ b/solution.py
@@ -353,10 +353,8 @@
     xrow = hop(own, [(SUF_X, SUF_Y)])
     qrow = hop(own, [(SUF_Q, SUF_Y)])
     (leaving,) = call(mean_kernel, [vector], own, got_v)
-    begin = hop(leaving, [(PRE_X, SUF_Y)], 1)
-    means = {3: hop(leaving, [(PRE_X, PRE_X)], 1)}
-    for c in (0, 2):
-        means[c] = hop(begin, [(SUF_Y, (c, 0))])
+    means = [hop(leaving, [(PRE_X, (c, 0))], 1) for c in range(4)]
+    begin = means[1]
     total = means[0] + (means[2] + means[3])
     x_pass = hop(total, [((c, 0), (c, 1)) for c in (0, 2, 3)])
     x_one = hop(begin, [((1, 0), (1, 1))])

time: 136 us -> 135 us (level)
  waiting for transfers between devices: 70.9 us -> 68.3 us
    ppermute x25, waiting for transfers between devices: 50 us -> 47.5 us  [send(): lax.ppermute(x, ('tm', 'col'), [(a * cols + b, c * cols + d) for (a, b),...]
  transfers between devices with their start and end apart: 36 -> 36, of which waited for: 13 -> 14; matrix products, arithmetic and copies ran while one was open for 1% -> 1% of each run, Pallas kernels for 4% -> 4%
where the time goes in v5:
time: 135 us; the launch traced here: 134 us
  waiting for transfers between devices  68.3 us (51%)
  starting transfers between devices  46.5 us (34%)
  Pallas kernels  13 us (10%)
  local copies, waits for them, and re-layouts  4.51 us (3%)
    ppermute x25, waiting for transfers between devices, send(): lax.ppermute(x, ('tm', 'col'), [(a * cols + b, c * cols + d) for (a, b),...  47.5 us
    ppermute x25, starting transfers between devices, send(): lax.ppermute(x, ('tm', 'col'), [(a * cols + b, c * cols + d) for (a, b),...  36 us
    ppermute x9, waiting for transfers between devices, turn(): return lax.ppermute(x, 'col', [(c, (c + by) % 4) for c in range(4)])  19 us
    pallas_call x14, Pallas kernels, call(): pl.pallas_call(kernel, out_shape=tuple((jax.ShapeDtypeStruct(s, d) for s,...  13 us
    ppermute x9, starting transfers between devices, turn(): return lax.ppermute(x, 'col', [(c, (c + by) % 4) for c in range(4)])  9.87 us
    unnamed x14, local copies, waits for them, and re-layouts  4.51 us
  transfers between devices with their start and end apart: 36, of which 14 were waited for; matrix products, arithmetic and copies ran while one was open for 1% of the time, Pallas kernels for 4%

profile of v5, /device:TPU:30, one launch (start us, length us, event | category | flops | bytes accessed | tf_op | source)
XLA Modules:
  0.0 134.1 jit_solution(3146210761884761701)
XLA Ops:
  0.6 0.6 collective-permute-start
  1.2 1.5 %collective-permute-start.8 = (bf16[8,64,256]{2,1,0:T(8,128)(2,1)}, bf16[8,64,256]{2,1,0:T(8,128)(2,1)S(1)}, u32[]{:S(2)}, u32[]{:S(2)}) collective-permute-start(bf16[8,64,256]{2,1,0:T(8,128)(2,1)} %g.1), channel_id=1, source_target_pairs={{0,3},{1,0},{2,1},{3,2},{4,7},{5,4},{6,5},{7,6},{8,11},{9,8},{10,9... | collective-permute-start | bytes 786440 | tf_op jit(solution)/shard_map/ppermute | solution.py:279
  2.7 0.8 collective-permute-start.1
  3.6 5.4 %collective-permute-done.a1 = bf16[8,64,256]{2,1,0:T(8,128)(2,1)S(1)} collective-permute-done((bf16[8,64,256]{2,1,0:T(8,128)(2,1)}, bf16[8,64,256]{2,1,0:T(8,128)(2,1)S(1)}, u32[]{:S(2)}, u32[]{:S(2)}) %collective-permute-start) | collective-permute-done | bytes 262176 | tf_op jit(solution)/shard_map/ppermute | solution.py:279
  9.0 1.7 %collective-permute-start.2 = (bf16[8,64,256]{2,1,0:T(8,128)(2,1)S(1)}, bf16[8,64,256]{2,1,0:T(8,128)(2,1)S(1)}, u32[]{:S(2)}, u32[]{:S(2)}) collective-permute-start(bf16[8,64,256]{2,1,0:T(8,128)(2,1)S(1)} %collective-permute-done.a1), channel_id=1, source_target_pairs={{0,1},{1,2},{2,3},{3,0},{4,5},{5,6},{6,7},{7,4},{8,9},{9,10},{10,1... | collective-permute-start | bytes 786440 | tf_op jit(solution)/shard_map/ppermute | solution.py:279
  10.7 0.3 collective-permute-start.7
  10.9 0.8 collective-permute-done.8.g2
  11.8 0.9 collective-permute-start.9
  12.7 0.8 pad_maximum_fusion.d0
  13.5 2.4 %collective-permute-start.3 = (f32[9,4,256]{2,1,0:T(4,128)S(1)}, f32[9,4,256]{2,1,0:T(4,128)S(1)}, u32[]{:S(2)}, u32[]{:S(2)}) collective-permute-start(f32[9,4,256]{2,1,0:T(4,128)S(1)} %pad_maximum_fusion.d0), channel_id=1, source_target_pairs={{0,1},{1,2},{2,3},{3,0},{4,5},{5,6},{6,7},{7,4},{8,9},{9,10},{10,1... | collective-permute-start | bytes 110600 | tf_op jit(solution)/shard_map/ppermute | solution.py:279
  15.9 6.7 %collective-permute-done.3.d1 = f32[9,4,256]{2,1,0:T(4,128)S(1)} collective-permute-done((f32[9,4,256]{2,1,0:T(4,128)S(1)}, f32[9,4,256]{2,1,0:T(4,128)S(1)}, u32[]{:S(2)}, u32[]{:S(2)}) %collective-permute-start.3) | collective-permute-done | bytes 36896 | tf_op jit(solution)/shard_map/ppermute | solution.py:279
  22.6 0.8 collective-permute-start.4
  23.4 4.3 %collective-permute-done.4.d2 = f32[9,4,256]{2,1,0:T(4,128)S(1)} collective-permute-done((f32[9,4,256]{2,1,0:T(4,128)S(1)}, f32[9,4,256]{2,1,0:T(4,128)S(1)}, u32[]{:S(2)}, u32[]{:S(2)}) %collective-permute-start.4) | collective-permute-done | bytes 36896 | tf_op jit(solution)/shard_map/ppermute | solution.py:279
  27.7 0.8 collective-permute-start.5
  28.6 0.9 copy-done.4
  29.5 0.9 copy-done.5
  30.5 0.9 copy-done.6
  31.5 1.7 %collective-permute-done.5.d3 = f32[9,4,256]{2,1,0:T(4,128)S(1)} collective-permute-done((f32[9,4,256]{2,1,0:T(4,128)S(1)}, f32[9,4,256]{2,1,0:T(4,128)S(1)}, u32[]{:S(2)}, u32[]{:S(2)}) %collective-permute-start.5) | collective-permute-done | bytes 36896 | tf_op jit(solution)/shard_map/ppermute | solution.py:279
  33.2 2.1 %shard_map.69 = (bf16[8,256,256]{2,1,0:T(8,128)(2,1)S(1)}, f32[9,16,256]{2,1,0:T(8,128)S(1)}, f32[8,272,256]{2,1,0:T(8,128)S(1)}, f32[8,272,256]{2,1,0:T(8,128)S(1)}, f32[272,256]{1,0:T(8,128)S(1)}) custom-call(bf16[8,64,256]{2,1,0:T(8,128)(2,1)S(1)} %get-tuple-element.30.a0, bf16[8,64,256]{2,1,0:T(8,128)(2,1)S(1)} %collective-permute-done.a1, ...), custom_call_target="tpu_custom_call" | custom-call | tf_op jit(solution)/shard_map/pallas_call | solution.py:255
  35.4 1.8 %shard_map.70 = (bf16[8,256,256]{2,1,0:T(8,128)(2,1)S(1)}, f32[528,256]{1,0:T(8,128)S(1)}) custom-call(bf16[8,64,256]{2,1,0:T(8,128)(2,1)S(1)} %get-tuple-element.35.g0, bf16[8,64,256]{2,1,0:T(8,128)(2,1)S(1)} %collective-permute-done.7.g1, bf16[8,64,256]{2,1,0:T(8,128)(2,1)S(1)} %collective-permute-done.8.g2, ...), custom_call_target="tpu_custom_call" | custom-call | tf_op jit(solution)/shard_map/pallas_call | solution.py:255
  37.3 0.5 collective-permute-start.6
  37.8 1.8 %collective-permute-done.6.x_m.x_bm = f32[272,256]{1,0:T(8,128)S(1)} collective-permute-done((f32[272,256]{1,0:T(8,128)S(1)}, f32[272,256]{1,0:T(8,128)S(1)}, u32[]{:S(2)}, u32[]{:S(2)}) %collective-permute-start.6) | collective-permute-done | bytes 278560 | tf_op jit(solution)/shard_map/ppermute | solution.py:276
  39.6 1.1 shard_map.71
  40.7 3.8 %collective-permute-start.11 = (f32[272,256]{1,0:T(8,128)S(1)}, f32[272,256]{1,0:T(8,128)S(1)}, u32[]{:S(2)}, u32[]{:S(2)}) collective-permute-start(f32[272,256]{1,0:T(8,128)S(1)} %get-tuple-element.39.r_0_), channel_id=1, source_target_pairs={{8,0},{16,8},{24,16},{32,24},{40,32},{48,40},{56,48},{64,56},{72,6... | collective-permute-start | bytes 835592 | tf_op jit(solution)/shard_map/ppermute | solution.py:271
  44.5 8.6 %collective-permute-done.11.r_1_ = f32[272,256]{1,0:T(8,128)S(1)} collective-permute-done((f32[272,256]{1,0:T(8,128)S(1)}, f32[272,256]{1,0:T(8,128)S(1)}, u32[]{:S(2)}, u32[]{:S(2)}) %collective-permute-start.11) | collective-permute-done | bytes 278560 | tf_op jit(solution)/shard_map/ppermute | solution.py:271
  53.2 0.9 shard_map.72
  54.1 1.9 %collective-permute-start.12 = (f32[272,256]{1,0:T(8,128)S(1)}, f32[272,256]{1,0:T(8,128)S(1)}, u32[]{:S(2)}, u32[]{:S(2)}) collective-permute-start(f32[272,256]{1,0:T(8,128)S(1)} %get-tuple-element.42.r_0_), channel_id=1, source_target_pairs={{16,0},{24,8},{32,16},{40,24},{48,32},{56,40},{64,48},{72,56},{80,... | collective-permute-start | bytes 835592 | tf_op jit(solution)/shard_map/ppermute | solution.py:271
  56.0 0.7 collective-permute-start.13
  56.7 0.7 collective-permute-start.14
  57.4 10.6 %collective-permute-done.12.r_1_ = f32[272,256]{1,0:T(8,128)S(1)} collective-permute-done((f32[272,256]{1,0:T(8,128)S(1)}, f32[272,256]{1,0:T(8,128)S(1)}, u32[]{:S(2)}, u32[]{:S(2)}) %collective-permute-start.12) | collective-permute-done | bytes 278560 | tf_op jit(solution)/shard_map/ppermute | solution.py:271
  68.0 0.9 shard_map.73
  68.9 5.8 %collective-permute-start.15 = (f32[272,256]{1,0:T(8,128)S(1)}, f32[272,256]{1,0:T(8,128)S(1)}, u32[]{:S(2)}, u32[]{:S(2)}) collective-permute-start(f32[272,256]{1,0:T(8,128)S(1)} %get-tuple-element.43.r_0_), channel_id=1, source_target_pairs={{32,0},{40,8},{48,16},{56,24},{64,32},{72,40},{80,48},{88,56},{96,... | collective-permute-start | bytes 835592 | tf_op jit(solution)/shard_map/ppermute | solution.py:271
  74.7 0.7 collective-permute-start.16
  75.4 0.7 collective-permute-start.17
  76.1 8.5 %collective-permute-done.15.r_1_ = f32[272,256]{1,0:T(8,128)S(1)} collective-permute-done((f32[272,256]{1,0:T(8,128)S(1)}, f32[272,256]{1,0:T(8,128)S(1)}, u32[]{:S(2)}, u32[]{:S(2)}) %collective-permute-start.15) | collective-permute-done | bytes 278560 | tf_op jit(solution)/shard_map/ppermute | solution.py:271
  84.6 0.9 shard_map.74
  85.5 1.3 collective-permute-start.18
  86.8 0.7 collective-permute-start.19
  87.4 0.7 collective-permute-start.20
  88.1 5.8 %collective-permute-done.18.r_1_ = f32[272,256]{1,0:T(8,128)S(1)} collective-permute-done((f32[272,256]{1,0:T(8,128)S(1)}, f32[272,256]{1,0:T(8,128)S(1)}, u32[]{:S(2)}, u32[]{:S(2)}) %collective-permute-start.18) | collective-permute-done | bytes 278560 | tf_op jit(solution)/shard_map/ppermute | solution.py:271
  93.9 0.3 shard_map.75
  94.2 0.7 collective-permute-start.28
  94.9 0.7 collective-permute-start.29
  95.6 0.7 collective-permute-start.30
  96.3 1.3 collective-permute-start.21
  97.6 5.8 %collective-permute-done.21.got = f32[16,256]{1,0:T(8,128)S(1)} collective-permute-done((f32[16,256]{1,0:T(8,128)S(1)}, f32[16,256]{1,0:T(8,128)S(1)}, u32[]{:S(2)}, u32[]{:S(2)}) %collective-permute-start.21) | collective-permute-done | bytes 16416 | tf_op jit(solution)/shard_map/ppermute | solution.py:271
  103.5 5.3 %collective-permute-start.26 = (f32[16,256]{1,0:T(8,128)S(1)}, f32[16,256]{1,0:T(8,128)S(1)}, u32[]{:S(2)}, u32[]{:S(2)}) collective-permute-start(f32[16,256]{1,0:T(8,128)S(1)} %shard_map.76), channel_id=1, source_target_pairs={{3,9},{11,17},{19,25},{27,33},{35,41},{43,49},{51,57},{59,65},{67,... | collective-permute-start | bytes 49160 | tf_op jit(solution)/shard_map/ppermute | solution.py:271
  108.8 1.3 collective-permute-start.22
  110.3 1.3 collective-permute-start.23
  111.6 0.7 copy-done.2
  112.3 1.9 %collective-permute-start.24 = (f32[16,256]{1,0:T(8,128)S(1)}, f32[16,256]{1,0:T(8,128)S(1)}, u32[]{:S(2)}, u32[]{:S(2)}) collective-permute-start(f32[16,256]{1,0:T(8,128)S(1)} %shard_map.76), channel_id=1, source_target_pairs={{3,11},{11,19},{19,27},{27,35},{35,43},{43,51},{51,59},{59,67},{67... | collective-permute-start | bytes 49160 | tf_op jit(solution)/shard_map/ppermute | solution.py:271
  114.2 0.9 copy-done.3
  115.4 0.4 shard_map.80
  115.8 0.8 collective-permute-start.31
  116.6 3.4 %collective-permute-done.24.m3 = f32[16,256]{1,0:T(8,128)S(1)} collective-permute-done((f32[16,256]{1,0:T(8,128)S(1)}, f32[16,256]{1,0:T(8,128)S(1)}, u32[]{:S(2)}, u32[]{:S(2)}) %collective-permute-start.24) | collective-permute-done | bytes 16416 | tf_op jit(solution)/shard_map/ppermute | solution.py:271
  120.0 1.3 collective-permute-start.25
  121.3 0.7 collective-permute-start.27
  122.0 0.7 collective-permute-start.32
  122.7 0.7 collective-permute-start.33
  123.3 0.7 collective-permute-start.34
  124.0 1.3 collective-permute-start.35
  125.4 2.1 %shard_map.78 = (f32[8,8,256]{2,1,0:T(8,128)S(1)}, f32[8,8,256]{2,1,0:T(8,128)S(1)}, f32[8,256]{1,0:T(8,128)S(1)}, f32[8,4,256]{2,1,0:T(4,128)}) custom-call(bf16[8,256,256]{2,1,0:T(8,128)(2,1)S(1)} %get-tuple-element.32.r_4_.araw, f32[9,16,256]{2,1,0:T(8,128)S(1)} %get-tuple-element.33.r_5_.drive, f32[256,256]{1,0:T(8,128)S(1)} %get-tuple-element.31.dyn.r_6_, ...), custom_call_target="tpu_custom_call" | custom-call | tf_op jit(solution)/shard_map/pallas_call | solution.py:255
  127.4 4.6 %collective-permute-done.35.s3 = f32[16,256]{1,0:T(8,128)S(1)} collective-permute-done((f32[16,256]{1,0:T(8,128)S(1)}, f32[16,256]{1,0:T(8,128)S(1)}, u32[]{:S(2)}, u32[]{:S(2)}) %collective-permute-start.35) | collective-permute-done | bytes 16416 | tf_op jit(solution)/shard_map/ppermute | solution.py:271
  132.1 2.0 %shard_map.81 = f32[8,4,256]{2,1,0:T(4,128)} custom-call(bf16[8,256,256]{2,1,0:T(8,128)(2,1)S(1)} %copy-done.1, f32[8,8,256]{2,1,0:T(8,128)S(1)} %get-tuple-element.53.xs, f32[8,8,256]{2,1,0:T(8,128)S(1)} %get-tuple-element.54.proj, f32[8,256]{1,0:T(8,128)S(1)} %get-tuple-element.55.mid, f32[528,256]{1,0:T(8,128)S(1)} %collective-permute-done.10.qy_m, ...), custom_call_target="tpu_custom_call" | custom-call | tf_op jit(solution)/shard_map/pallas_call | solution.py:255
  (39 shorter events, 0.8 us)
Async XLA Ops:
  0.6 8.3 %collective-permute-start = (bf16[8,64,256]{2,1,0:T(8,128)(2,1)}, bf16[8,64,256]{2,1,0:T(8,128)(2,1)S(1)}, u32[]{:S(2)}, u32[]{:S(2)}) collective-permute-start(bf16[8,64,256]{2,1,0:T(8,128)(2,1)} %a.1), channel_id=1, source_target_pairs={{0,1},{1,2},{2,3},{3,0},{4,5},{5,6},{6,7},{7,4},{8,9},{9,10},{10,1... | collective-permute-start | bytes 786440 | tf_op jit(solution)/shard_map/ppermute | solution.py:279
  1.2 10.6 %collective-permute-start.8 = (bf16[8,64,256]{2,1,0:T(8,128)(2,1)}, bf16[8,64,256]{2,1,0:T(8,128)(2,1)S(1)}, u32[]{:S(2)}, u32[]{:S(2)}) collective-permute-start(bf16[8,64,256]{2,1,0:T(8,128)(2,1)} %g.1), channel_id=1, source_target_pairs={{0,3},{1,0},{2,1},{3,2},{4,7},{5,4},{6,5},{7,6},{8,11},{9,8},{10,9... | collective-permute-start | bytes 786440 | tf_op jit(solution)/shard_map/ppermute | solution.py:279
  2.7 30.5 %collective-permute-start.1 = (bf16[8,64,256]{2,1,0:T(8,128)(2,1)}, bf16[8,64,256]{2,1,0:T(8,128)(2,1)S(1)}, u32[]{:S(2)}, u32[]{:S(2)}) collective-permute-start(bf16[8,64,256]{2,1,0:T(8,128)(2,1)} %a.1), channel_id=1, source_target_pairs={{0,3},{1,0},{2,1},{3,2},{4,7},{5,4},{6,5},{7,6},{8,11},{9,8},{10,9... | collective-permute-start | bytes 786440 | tf_op jit(solution)/shard_map/ppermute | solution.py:279
  9.0 24.2 %collective-permute-start.2 = (bf16[8,64,256]{2,1,0:T(8,128)(2,1)S(1)}, bf16[8,64,256]{2,1,0:T(8,128)(2,1)S(1)}, u32[]{:S(2)}, u32[]{:S(2)}) collective-permute-start(bf16[8,64,256]{2,1,0:T(8,128)(2,1)S(1)} %collective-permute-done.a1), channel_id=1, source_target_pairs={{0,1},{1,2},{2,3},{3,0},{4,5},{5,6},{6,7},{7,4},{8,9},{9,10},{10,1... | collective-permute-start | bytes 786440 | tf_op jit(solution)/shard_map/ppermute | solution.py:279
  10.7 24.7 %collective-permute-start.7 = (bf16[8,64,256]{2,1,0:T(8,128)(2,1)}, bf16[8,64,256]{2,1,0:T(8,128)(2,1)S(1)}, u32[]{:S(2)}, u32[]{:S(2)}) collective-permute-start(bf16[8,64,256]{2,1,0:T(8,128)(2,1)} %g.1), channel_id=1, source_target_pairs={{0,1},{1,2},{2,3},{3,0},{4,5},{5,6},{6,7},{7,4},{8,9},{9,10},{10,1... | collective-permute-start | bytes 786440 | tf_op jit(solution)/shard_map/ppermute | solution.py:279
  11.8 23.6 %collective-permute-start.9 = (bf16[8,64,256]{2,1,0:T(8,128)(2,1)S(1)}, bf16[8,64,256]{2,1,0:T(8,128)(2,1)S(1)}, u32[]{:S(2)}, u32[]{:S(2)}) collective-permute-start(bf16[8,64,256]{2,1,0:T(8,128)(2,1)S(1)} %collective-permute-done.8.g2), channel_id=1, source_target_pairs={{0,3},{1,0},{2,1},{3,2},{4,7},{5,4},{6,5},{7,6},{8,11},{9,8},{10,9... | collective-permute-start | bytes 786440 | tf_op jit(solution)/shard_map/ppermute | solution.py:279
  13.5 9.1 %collective-permute-start.3 = (f32[9,4,256]{2,1,0:T(4,128)S(1)}, f32[9,4,256]{2,1,0:T(4,128)S(1)}, u32[]{:S(2)}, u32[]{:S(2)}) collective-permute-start(f32[9,4,256]{2,1,0:T(4,128)S(1)} %pad_maximum_fusion.d0), channel_id=1, source_target_pairs={{0,1},{1,2},{2,3},{3,0},{4,5},{5,6},{6,7},{7,4},{8,9},{9,10},{10,1... | collective-permute-start | bytes 110600 | tf_op jit(solution)/shard_map/ppermute | solution.py:279
  22.6 5.2 %collective-permute-start.4 = (f32[9,4,256]{2,1,0:T(4,128)S(1)}, f32[9,4,256]{2,1,0:T(4,128)S(1)}, u32[]{:S(2)}, u32[]{:S(2)}) collective-permute-start(f32[9,4,256]{2,1,0:T(4,128)S(1)} %pad_maximum_fusion.d0), channel_id=1, source_target_pairs={{0,3},{1,0},{2,1},{3,2},{4,7},{5,4},{6,5},{7,6},{8,11},{9,8},{10,9... | collective-permute-start | bytes 110600 | tf_op jit(solution)/shard_map/ppermute | solution.py:279
  27.7 5.5 %collective-permute-start.5 = (f32[9,4,256]{2,1,0:T(4,128)S(1)}, f32[9,4,256]{2,1,0:T(4,128)S(1)}, u32[]{:S(2)}, u32[]{:S(2)}) collective-permute-start(f32[9,4,256]{2,1,0:T(4,128)S(1)} %pad_maximum_fusion.d0), channel_id=1, source_target_pairs={{0,2},{1,3},{2,0},{3,1},{4,6},{5,7},{6,4},{7,5},{8,10},{9,11},{10,... | collective-permute-start | bytes 110600 | tf_op jit(solution)/shard_map/ppermute | solution.py:279
  28.6 0.9 copy-start.4
  29.5 0.9 copy-start.5
  30.5 0.9 copy-start.6
  37.2 31.7 %copy-start = (bf16[8,256,256]{2,1,0:T(8,128)(2,1)}, bf16[8,256,256]{2,1,0:T(8,128)(2,1)S(1)}, u32[]{:S(2)}) copy-start(bf16[8,256,256]{2,1,0:T(8,128)(2,1)S(1)} %get-tuple-element.52.graw) | copy-start | bytes 3145732
  37.2 2.4 %collective-permute-start.10 = (f32[528,256]{1,0:T(8,128)S(1)}, f32[528,256]{1,0:T(8,128)S(1)}, u32[]{:S(2)}, u32[]{:S(2)}) collective-permute-start(f32[528,256]{1,0:T(8,128)S(1)} %get-tuple-element.38.qy), channel_id=1, source_target_pairs={{0,4},{4,0},{8,12},{12,8},{16,20},{20,16},{24,28},{28,24},{32,36},... | collective-permute-start | bytes 1622024 | tf_op jit(solution)/shard_map/ppermute | solution.py:276
  37.3 2.3 %collective-permute-start.6 = (f32[272,256]{1,0:T(8,128)S(1)}, f32[272,256]{1,0:T(8,128)S(1)}, u32[]{:S(2)}, u32[]{:S(2)}) collective-permute-start(f32[272,256]{1,0:T(8,128)S(1)} %get-tuple-element.34.x.x_b), channel_id=1, source_target_pairs={{0,4},{4,0},{8,12},{12,8},{16,20},{20,16},{24,28},{28,24},{32,36},... | collective-permute-start | bytes 835592 | tf_op jit(solution)/shard_map/ppermute | solution.py:276
  40.7 12.5 %collective-permute-start.11 = (f32[272,256]{1,0:T(8,128)S(1)}, f32[272,256]{1,0:T(8,128)S(1)}, u32[]{:S(2)}, u32[]{:S(2)}) collective-permute-start(f32[272,256]{1,0:T(8,128)S(1)} %get-tuple-element.39.r_0_), channel_id=1, source_target_pairs={{8,0},{16,8},{24,16},{32,24},{40,32},{48,40},{56,48},{64,56},{72,6... | collective-permute-start | bytes 835592 | tf_op jit(solution)/shard_map/ppermute | solution.py:271
  54.1 13.9 %collective-permute-start.12 = (f32[272,256]{1,0:T(8,128)S(1)}, f32[272,256]{1,0:T(8,128)S(1)}, u32[]{:S(2)}, u32[]{:S(2)}) collective-permute-start(f32[272,256]{1,0:T(8,128)S(1)} %get-tuple-element.42.r_0_), channel_id=1, source_target_pairs={{16,0},{24,8},{32,16},{40,24},{48,32},{56,40},{64,48},{72,56},{80,... | collective-permute-start | bytes 835592 | tf_op jit(solution)/shard_map/ppermute | solution.py:271
  56.0 12.0 %collective-permute-start.13 = (f32[272,256]{1,0:T(8,128)S(1)}, f32[272,256]{1,0:T(8,128)S(1)}, u32[]{:S(2)}, u32[]{:S(2)}) collective-permute-start(f32[272,256]{1,0:T(8,128)S(1)} %get-tuple-element.42.r_0_), channel_id=1, source_target_pairs={{0,1},{8,9},{16,17},{24,25},{32,33},{40,41},{48,49},{56,57},{64,65... | collective-permute-start | bytes 835592 | tf_op jit(solution)/shard_map/ppermute | solution.py:271
  56.7 11.3 %collective-permute-start.14 = (f32[272,256]{1,0:T(8,128)S(1)}, f32[272,256]{1,0:T(8,128)S(1)}, u32[]{:S(2)}, u32[]{:S(2)}) collective-permute-start(f32[272,256]{1,0:T(8,128)S(1)} %get-tuple-element.42.r_0_), channel_id=1, source_target_pairs={{2,1},{10,9},{18,17},{26,25},{34,33},{42,41},{50,49},{58,57},{66,6... | collective-permute-start | bytes 835592 | tf_op jit(solution)/shard_map/ppermute | solution.py:271
  68.9 15.7 %collective-permute-start.15 = (f32[272,256]{1,0:T(8,128)S(1)}, f32[272,256]{1,0:T(8,128)S(1)}, u32[]{:S(2)}, u32[]{:S(2)}) collective-permute-start(f32[272,256]{1,0:T(8,128)S(1)} %get-tuple-element.43.r_0_), channel_id=1, source_target_pairs={{32,0},{40,8},{48,16},{56,24},{64,32},{72,40},{80,48},{88,56},{96,... | collective-permute-start | bytes 835592 | tf_op jit(solution)/shard_map/ppermute | solution.py:271
  74.7 9.9 %collective-permute-start.16 = (f32[272,256]{1,0:T(8,128)S(1)}, f32[272,256]{1,0:T(8,128)S(1)}, u32[]{:S(2)}, u32[]{:S(2)}) collective-permute-start(f32[272,256]{1,0:T(8,128)S(1)} %get-tuple-element.43.r_0_), channel_id=1, source_target_pairs={{0,1},{8,9},{16,17},{24,25},{32,33},{40,41},{48,49},{56,57},{64,65... | collective-permute-start | bytes 835592 | tf_op jit(solution)/shard_map/ppermute | solution.py:271
  75.4 9.2 %collective-permute-start.17 = (f32[272,256]{1,0:T(8,128)S(1)}, f32[272,256]{1,0:T(8,128)S(1)}, u32[]{:S(2)}, u32[]{:S(2)}) collective-permute-start(f32[272,256]{1,0:T(8,128)S(1)} %get-tuple-element.43.r_0_), channel_id=1, source_target_pairs={{2,1},{10,9},{18,17},{26,25},{34,33},{42,41},{50,49},{58,57},{66,6... | collective-permute-start | bytes 835592 | tf_op jit(solution)/shard_map/ppermute | solution.py:271
  85.5 8.4 %collective-permute-start.18 = (f32[272,256]{1,0:T(8,128)S(1)}, f32[272,256]{1,0:T(8,128)S(1)}, u32[]{:S(2)}, u32[]{:S(2)}) collective-permute-start(f32[272,256]{1,0:T(8,128)S(1)} %get-tuple-element.44.r_0_), channel_id=1, source_target_pairs={{64,0},{72,8},{80,16},{88,24},{96,32},{104,40},{112,48},{120,56},{... | collective-permute-start | bytes 835592 | tf_op jit(solution)/shard_map/ppermute | solution.py:271
  86.8 7.1 %collective-permute-start.19 = (f32[272,256]{1,0:T(8,128)S(1)}, f32[272,256]{1,0:T(8,128)S(1)}, u32[]{:S(2)}, u32[]{:S(2)}) collective-permute-start(f32[272,256]{1,0:T(8,128)S(1)} %get-tuple-element.44.r_0_), channel_id=1, source_target_pairs={{0,1},{8,9},{16,17},{24,25},{32,33},{40,41},{48,49},{56,57},{64,65... | collective-permute-start | bytes 835592 | tf_op jit(solution)/shard_map/ppermute | solution.py:271
  87.4 6.5 %collective-permute-start.20 = (f32[272,256]{1,0:T(8,128)S(1)}, f32[272,256]{1,0:T(8,128)S(1)}, u32[]{:S(2)}, u32[]{:S(2)}) collective-permute-start(f32[272,256]{1,0:T(8,128)S(1)} %get-tuple-element.44.r_0_), channel_id=1, source_target_pairs={{2,1},{10,9},{18,17},{26,25},{34,33},{42,41},{50,49},{58,57},{66,6... | collective-permute-start | bytes 835592 | tf_op jit(solution)/shard_map/ppermute | solution.py:271
  94.2 17.4 %collective-permute-start.28 = (f32[272,256]{1,0:T(8,128)S(1)}, f32[272,256]{1,0:T(8,128)S(1)}, u32[]{:S(2)}, u32[]{:S(2)}) collective-permute-start(f32[272,256]{1,0:T(8,128)S(1)} %get-tuple-element.45.own), channel_id=1, source_target_pairs={{0,1},{8,9},{16,17},{24,25},{32,33},{40,41},{48,49},{56,57},{64,65... | collective-permute-start | bytes 835592 | tf_op jit(solution)/shard_map/ppermute | solution.py:271
  94.9 20.5 %collective-permute-start.29 = (f32[272,256]{1,0:T(8,128)S(1)}, f32[272,256]{1,0:T(8,128)S(1)}, u32[]{:S(2)}, u32[]{:S(2)}) collective-permute-start(f32[272,256]{1,0:T(8,128)S(1)} %get-tuple-element.45.own), channel_id=1, source_target_pairs={{2,1},{10,9},{18,17},{26,25},{34,33},{42,41},{50,49},{58,57},{66,6... | collective-permute-start | bytes 835592 | tf_op jit(solution)/shard_map/ppermute | solution.py:271
  95.6 19.8 %collective-permute-start.30 = (f32[272,256]{1,0:T(8,128)S(1)}, f32[272,256]{1,0:T(8,128)S(1)}, u32[]{:S(2)}, u32[]{:S(2)}) collective-permute-start(f32[272,256]{1,0:T(8,128)S(1)} %get-tuple-element.45.own), channel_id=1, source_target_pairs={{129,1},{137,9},{145,17},{153,25},{161,33},{169,41},{177,49},{185,... | collective-permute-start | bytes 835592 | tf_op jit(solution)/shard_map/ppermute | solution.py:271
  96.3 7.1 %collective-permute-start.21 = (f32[16,256]{1,0:T(8,128)S(1)}, f32[16,256]{1,0:T(8,128)S(1)}, u32[]{:S(2)}, u32[]{:S(2)}) collective-permute-start(f32[16,256]{1,0:T(8,128)S(1)} %get-tuple-element.46), channel_id=1, source_target_pairs={{3,131},{11,139},{19,147},{27,155},{35,163},{43,171},{51,179},{59,... | collective-permute-start | bytes 49160 | tf_op jit(solution)/shard_map/ppermute | solution.py:271
  103.5 6.7 %collective-permute-start.26 = (f32[16,256]{1,0:T(8,128)S(1)}, f32[16,256]{1,0:T(8,128)S(1)}, u32[]{:S(2)}, u32[]{:S(2)}) collective-permute-start(f32[16,256]{1,0:T(8,128)S(1)} %shard_map.76), channel_id=1, source_target_pairs={{3,9},{11,17},{19,25},{27,33},{35,41},{43,49},{51,57},{59,65},{67,... | collective-permute-start | bytes 49160 | tf_op jit(solution)/shard_map/ppermute | solution.py:271
  108.8 7.8 %collective-permute-start.22 = (f32[16,256]{1,0:T(8,128)S(1)}, f32[16,256]{1,0:T(8,128)S(1)}, u32[]{:S(2)}, u32[]{:S(2)}) collective-permute-start(f32[16,256]{1,0:T(8,128)S(1)} %shard_map.76), channel_id=1, source_target_pairs={{3,8},{11,16},{19,24},{27,32},{35,40},{43,48},{51,56},{59,64},{67,... | collective-permute-start | bytes 49160 | tf_op jit(solution)/shard_map/ppermute | solution.py:271
  110.3 6.4 %collective-permute-start.23 = (f32[16,256]{1,0:T(8,128)S(1)}, f32[16,256]{1,0:T(8,128)S(1)}, u32[]{:S(2)}, u32[]{:S(2)}) collective-permute-start(f32[16,256]{1,0:T(8,128)S(1)} %shard_map.76), channel_id=1, source_target_pairs={{3,10},{11,18},{19,26},{27,34},{35,42},{43,50},{51,58},{59,66},{67... | collective-permute-start | bytes 49160 | tf_op jit(solution)/shard_map/ppermute | solution.py:271
  111.6 0.7 copy-start.2
  112.3 7.7 %collective-permute-start.24 = (f32[16,256]{1,0:T(8,128)S(1)}, f32[16,256]{1,0:T(8,128)S(1)}, u32[]{:S(2)}, u32[]{:S(2)}) collective-permute-start(f32[16,256]{1,0:T(8,128)S(1)} %shard_map.76), channel_id=1, source_target_pairs={{3,11},{11,19},{19,27},{27,35},{35,43},{43,51},{51,59},{59,67},{67... | collective-permute-start | bytes 49160 | tf_op jit(solution)/shard_map/ppermute | solution.py:271
  114.2 1.0 copy-start.3
  115.8 16.3 %copy-start.1 = (bf16[8,256,256]{2,1,0:T(8,128)(2,1)S(1)}, bf16[8,256,256]{2,1,0:T(8,128)(2,1)}, u32[]{:S(2)}) copy-start(bf16[8,256,256]{2,1,0:T(8,128)(2,1)} %copy-done) | copy-start | bytes 3145732
  115.8 6.2 %collective-permute-start.31 = (f32[16,256]{1,0:T(8,128)S(1)}, f32[16,256]{1,0:T(8,128)S(1)}, u32[]{:S(2)}, u32[]{:S(2)}) collective-permute-start(f32[16,256]{1,0:T(8,128)S(1)} %shard_map.80), channel_id=1, source_target_pairs={{1,5},{9,13},{17,21},{25,29},{33,37},{41,45},{49,53},{57,61},{65,6... | collective-permute-start | bytes 49160 | tf_op jit(solution)/shard_map/ppermute | solution.py:271
  120.0 4.0 %collective-permute-start.25 = (f32[16,256]{1,0:T(8,128)S(1)}, f32[16,256]{1,0:T(8,128)S(1)}, u32[]{:S(2)}, u32[]{:S(2)}) collective-permute-start(f32[16,256]{1,0:T(8,128)S(1)} %add_add_fusion), channel_id=1, source_target_pairs={{0,4},{2,6},{3,7},{8,12},{10,14},{11,15},{16,20},{18,22},{19,23},{... | collective-permute-start | bytes 49160 | tf_op jit(solution)/shard_map/ppermute | solution.py:271
  121.3 4.0 %collective-permute-start.27 = (f32[16,256]{1,0:T(8,128)S(1)}, f32[16,256]{1,0:T(8,128)S(1)}, u32[]{:S(2)}, u32[]{:S(2)}) collective-permute-start(f32[16,256]{1,0:T(8,128)S(1)} %collective-permute-done.26.m1.begin), channel_id=1, source_target_pairs={{1,5},{9,13},{17,21},{25,29},{33,37},{41,45},{49,53},{57,61},{65,6... | collective-permute-start | bytes 49160 | tf_op jit(solution)/shard_map/ppermute | solution.py:271
  122.0 5.4 %collective-permute-start.32 = (f32[16,256]{1,0:T(8,128)S(1)}, f32[16,256]{1,0:T(8,128)S(1)}, u32[]{:S(2)}, u32[]{:S(2)}) collective-permute-start(f32[16,256]{1,0:T(8,128)S(1)} %broadcast_select_fusion), channel_id=1, source_target_pairs={{9,0},{13,4},{17,8},{21,12},{25,16},{29,20},{33,24},{37,28},{41,32... | collective-permute-start | bytes 49160 | tf_op jit(solution)/shard_map/ppermute | solution.py:271
  122.7 4.8 %collective-permute-start.33 = (f32[16,256]{1,0:T(8,128)S(1)}, f32[16,256]{1,0:T(8,128)S(1)}, u32[]{:S(2)}, u32[]{:S(2)}) collective-permute-start(f32[16,256]{1,0:T(8,128)S(1)} %broadcast_select_fusion), channel_id=1, source_target_pairs={{9,2},{13,6},{17,10},{21,14},{25,18},{29,22},{33,26},{37,30},{41,3... | collective-permute-start | bytes 49160 | tf_op jit(solution)/shard_map/ppermute | solution.py:271
  123.3 4.1 %collective-permute-start.34 = (f32[16,256]{1,0:T(8,128)S(1)}, f32[16,256]{1,0:T(8,128)S(1)}, u32[]{:S(2)}, u32[]{:S(2)}) collective-permute-start(f32[16,256]{1,0:T(8,128)S(1)} %broadcast_select_fusion), channel_id=1, source_target_pairs={{9,1},{13,5},{17,9},{21,13},{25,17},{29,21},{33,25},{37,29},{41,33... | collective-permute-start | bytes 49160 | tf_op jit(solution)/shard_map/ppermute | solution.py:271
  124.0 8.0 %collective-permute-start.35 = (f32[16,256]{1,0:T(8,128)S(1)}, f32[16,256]{1,0:T(8,128)S(1)}, u32[]{:S(2)}, u32[]{:S(2)}) collective-permute-start(f32[16,256]{1,0:T(8,128)S(1)} %broadcast_select_fusion), channel_id=1, source_target_pairs={{9,3},{13,7},{17,11},{21,15},{25,19},{29,23},{33,27},{37,31},{41,3... | collective-permute-start | bytes 49160 | tf_op jit(solution)/shard_map/ppermute | solution.py:271
